TPU v7x, 1024 devices: a whole 8x8x8 slice. The times are simulated.
1024 devices in a mesh: fsdp: 32 (over y_lo, z, core), head: 32 (over y_hi, x).
Axes of the slice: x: 8, y: 8 (y_hi: 4, y_lo: 2; y = y_hi * 2 + y_lo), z: 8, core: 2. Of those that a mesh axis runs over, the one named last changes fastest.
Arguments:
- tokens: bfloat16 [8192, 4096], P('fsdp'), may hold values from -6 to 6
- zx_weight: bfloat16 [4096, 128, 128], P('fsdp', 'head'), may hold values from -0.09375 to 0.09375
- dt_weight: bfloat16 [4096, 128], P('fsdp', 'head'), may hold values from -0.09375 to 0.09375
- bc_weight: bfloat16 [4096, 1024], P('fsdp'), may hold values from -0.09375 to 0.09375
- conv_x: float32 [4, 8192], P(None, 'head'), may hold values from -2 to 2
- conv_bc: float32 [4, 1024], replicated, may hold values from -2 to 2
- a_log: float32 [128], P('head'), may hold values from -5 to 0.5
- dt_bias: float32 [128], P('head'), may hold values from -4 to 0
- d_skip: float32 [128], P('head'), may hold values from 0.5 to 2
- norm_gain: float32 [8192], P('head'), may hold values from 0.1 to 1.9
- out_weight: bfloat16 [8192, 4096], P('head'), may hold values from -0.125 to 0.125
Outputs:
- mixed: bfloat16 [8192, 4096], P('fsdp', 'head')
All inputs are finite; a program needn't handle non-finite values.
Results may differ from a plain program's by a relative error of at most 0.015.
Values may be sent and summed in bfloat16 or wider, within the bound.
No kernel may reach another device: no remote copies, remote signals or barrier semaphores. Data moves between devices by JAX's collectives and lax.ppermute only.
A program may use at most 32 MiB of HBM per device.

v0:
```python
import jax
import jax.numpy as jnp
from jax import lax
from jax.sharding import PartitionSpec as P

G = 4
LEN = 256


def settle(values):
    return lax.optimization_barrier(values.astype(jnp.bfloat16))


def causal(values, kernel, seq_len):
    columns = values.shape[1]
    seqs = values.reshape(-1, seq_len, columns).astype(jnp.float32)
    taps = kernel.shape[0]
    padded = jnp.pad(seqs, ((0, 0), (taps - 1, 0), (0, 0)))
    total = jnp.zeros(seqs.shape, jnp.float32)
    for tap in range(taps):
        total = total + kernel[tap] * padded[:, tap : tap + seq_len]
    return settle(jax.nn.silu(total).reshape(-1, columns))


def on_device(
    tokens,
    zx_weight,
    dt_weight,
    bc_weight,
    conv_x,
    conv_bc,
    a_log,
    dt_bias,
    d_skip,
    norm_gain,
    out_weight,
):
    tok_rows = tokens.shape[0]
    heads_here = zx_weight.shape[1]
    head_size = zx_weight.shape[2] // 2
    n_head = lax.axis_size("head")
    head_pos = lax.axis_index("head")
    per_group = n_head // G
    group_id = head_pos // per_group
    group_cols = bc_weight.shape[1] // G
    state = group_cols // 2
    bc_part = lax.dynamic_slice_in_dim(bc_weight, group_id * group_cols, group_cols, 1)
    flat_zx = zx_weight.reshape(zx_weight.shape[0], heads_here * 2 * head_size)
    zx_acc = jnp.dot(
        tokens,
        lax.all_gather(flat_zx, "fsdp", axis=0, tiled=True),
        preferred_element_type=jnp.float32,
    )
    dt_acc = jnp.dot(
        tokens,
        lax.all_gather(dt_weight, "fsdp", axis=0, tiled=True),
        preferred_element_type=jnp.float32,
    )
    bc_acc = jnp.dot(
        tokens,
        lax.all_gather(bc_part, "fsdp", axis=0, tiled=True),
        preferred_element_type=jnp.float32,
    )
    zx = settle(zx_acc).reshape(tok_rows, heads_here, 2, head_size)
    dt_raw = settle(dt_acc)
    bc_raw = settle(bc_acc)
    channels = heads_here * head_size
    gate = zx[:, :, 0, :].astype(jnp.float32).reshape(tok_rows, channels)
    xin = zx[:, :, 1, :].reshape(tok_rows, channels)
    xconv = causal(xin, conv_x, LEN)
    conv_group = lax.dynamic_slice_in_dim(conv_bc, group_id * group_cols, group_cols, 1)
    bconv = causal(bc_raw, conv_group, LEN)
    count = tok_rows // LEN
    steps = jax.nn.softplus(dt_raw.astype(jnp.float32) + dt_bias).reshape(count, LEN, heads_here)
    cum = jnp.cumsum(-steps * jnp.exp(a_log), axis=1)
    seg = cum[:, :, None, :] - cum[:, None, :, :]
    lower = jnp.arange(LEN)[:, None] >= jnp.arange(LEN)[None, :]
    decay = jnp.exp(jnp.where(lower[None, :, :, None], seg, -1e30))
    bseq = bconv[:, :state].reshape(count, LEN, state)
    cseq = bconv[:, state:].reshape(count, LEN, state)
    inner = jnp.einsum("btn,bsn->bts", cseq, bseq, preferred_element_type=jnp.float32)
    weights = inner[..., None] * decay * steps[:, None, :, :]
    xval = xconv.astype(jnp.float32).reshape(count, LEN, heads_here, head_size)
    ys = jnp.einsum("btsh,bshp->bthp", weights, xval, precision=lax.Precision.HIGHEST)
    ys = ys + d_skip[None, None, :, None] * xval
    gated = ys.reshape(tok_rows, channels) * jax.nn.silu(gate)
    local_sq = jnp.sum(gated * gated, axis=1)
    picks = jnp.arange(G)[None, :] == group_id
    totals = lax.psum(jnp.where(picks, local_sq[:, None], 0.0), "head")
    mine = jnp.sum(jnp.where(picks, totals, 0.0), axis=1)
    meansq = mine / (per_group * channels)
    normed = (gated / jnp.sqrt(meansq + 1e-05)[:, None] * norm_gain).astype(jnp.bfloat16)
    partial_out = jnp.dot(normed, out_weight, preferred_element_type=jnp.float32)
    return lax.psum_scatter(
        partial_out.astype(jnp.bfloat16), "head", scatter_dimension=1, tiled=True
    )


def solution(mesh):
    in_specs = (
        P("fsdp", None),
        P("fsdp", "head", None),
        P("fsdp", "head"),
        P("fsdp", None),
        P(None, "head"),
        P(),
        P("head"),
        P("head"),
        P("head"),
        P("head"),
        P("head", None),
    )
    out_specs = P("fsdp", "head")
    return jax.shard_map(
        on_device, mesh=mesh, in_specs=in_specs, out_specs=out_specs, check_vma=False
    )
```

profile of v0, /device:TPU:4, one launch (start us, length us, event | category | flops | bytes accessed | tf_op | source)
XLA Modules:
  0.0 496.9 jit_solution(5254783685193526557)
XLA Ops:
  6.6 1.6 constant_dynamic-slice_fusion.1
  8.3 1.6 copy.29
  9.9 0.7 exp.36
  10.6 47.2 %all_gather.11 = bf16[4096,4]{0,1:T(4,128)(2,1)S(1)} all-gather(bf16[128,4]{0,1:T(4,128)(2,1)} %param.13), channel_id=1, replica_groups=mesh['fsdp'=32,'head'=32] {'fsdp'}, dimensions={0}, use_global_device_ids=true | all-gather | bytes 33792 | tf_op jit(solution)/shard_map/all_gather | solution.py:56
  57.8 2.3 convolution_convert_fusion.3
  60.0 0.1 multiply_bitcast_fusion
  60.1 1.2 reduce-window.6
  61.5 0.1 copy.21
  61.8 0.9 constant_dynamic-slice_fusion
  62.8 29.5 %all-gather.5.cloned.1.call-done = bf16[4096,256]{1,0:T(8,128)(2,1)} async-done(((bf16[128,256]{1,0:T(8,128)(2,1)}), bf16[4096,256]{1,0:T(8,128)(2,1)}) %all-gather.5.cloned.1.call-update) | async-done | bytes 2097168 | tf_op jit(solution)/shard_map/all_gather | solution.py:61
  92.3 3.0 fusion.1
  95.3 0.4 fusion.37
  95.7 0.2 fusion.39
  95.9 71.5 %all-gather.3.cloned.1.call-done = bf16[4096,512]{1,0:T(8,128)(2,1)} async-done(((bf16[128,512]{1,0:T(8,128)(2,1)}), bf16[4096,512]{1,0:T(8,128)(2,1)}) %all-gather.3.cloned.1.call-update) | async-done | bytes 4194320 | tf_op jit(solution)/shard_map/all_gather | solution.py:51
  167.4 4.1 convolution_convert_fusion.1
  171.5 0.1 copy.20
  171.7 0.4 fusion.38
  172.1 1.0 fusion.36
  173.2 77.3 %psum.7 = f32[256,4]{0,1:T(4,128)S(1)} all-reduce(f32[256,4]{0,1:T(4,128)S(1)} %broadcast_select_fusion), channel_id=1, replica_groups=mesh['fsdp'=32,'head'=32] {'head'}, use_global_device_ids=true, to_apply=%region_3.4 | all-reduce | flops 1024 | bytes 8192 | tf_op jit(solution)/shard_map/psum | solution.py:89
  250.6 0.1 multiply_convert_fusion
  250.7 2.0 convolution_convert_fusion
  252.7 4.1 copy.24
  256.9 232.0 %reduce-scatter.4.cloned.1.call-done = bf16[128,256]{1,0:T(8,128)(2,1)} async-done(((bf16[4096,256]{1,0:T(8,128)(2,1)}), bf16[128,256]{1,0:T(8,128)(2,1)}) %reduce-scatter.4.cloned.1.call-update) | async-done | bytes 65552
  488.8 1.6 copy.25
  (34 shorter events, 0.8 us)
Async XLA Ops:
  6.5 244.2 %copy-start = (bf16[256,4096]{1,0:T(8,128)(2,1)S(1)}, bf16[256,4096]{1,0:T(8,128)(2,1)}, u32[]{:S(2)}) copy-start(bf16[256,4096]{1,0:T(8,128)(2,1)} %param.21) | copy-start | bytes 6291460
  6.5 53.5 %copy-start.3 = (f32[4]{0:T(128)S(1)}, f32[4]{0:T(128)}, u32[]{:S(2)}) copy-start(f32[4]{0:T(128)} %param.18) | copy-start | bytes 52
  6.5 56.2 %copy-start.1 = (f32[4,256]{1,0:T(4,128)S(1)}, f32[4,256]{1,0:T(4,128)}, u32[]{:S(2)}) copy-start(f32[4,256]{1,0:T(4,128)} %param.15) | copy-start | bytes 12292
  6.5 85.7 %all-gather.5.cloned.1.call-start = ((), (), s32[]{:S(2)}) async-start(), calls=%async_computation.2 | async-start | bytes 2162688 | tf_op jit(solution)/shard_map/all_gather | solution.py:61
  8.2 159.2 %all-gather.3.cloned.1.call-start = ((), (), s32[]{:S(2)}) async-start(), calls=%async_computation.1 | async-start | bytes 4325376 | tf_op jit(solution)/shard_map/all_gather | solution.py:51
  9.9 479.0 %reduce-scatter.4.cloned.1.call-start = ((), (), s32[]{:S(2)}) async-start(), calls=%async_computation.3 | async-start | bytes 2162688
  95.9 76.2 %copy-start.4 = (f32[4]{0:T(128)S(1)}, f32[4]{0:T(128)}, u32[]{:S(2)}) copy-start(f32[4]{0:T(128)} %param.19) | copy-start | bytes 52
  171.6 78.9 %copy-start.2 = (f32[256]{0:T(256)S(1)}, f32[256]{0:T(256)}, u32[]{:S(2)}) copy-start(f32[256]{0:T(256)} %param.20) | copy-start | bytes 3076
Sparse Core Ops, SparseCore 0:
  10.1 82.1 all-gather.4
  95.0 72.3 all-gather.2
  257.0 231.7 reduce-scatter.3
where the time goes:
time: 497 us
  waiting for transfers between devices  333 us (67%)
  blocking collectives  124 us (25%)
  between operations  13.3 us (3%)
  matrix products  12.5 us (3%)
  local copies, waits for them, and re-layouts  11 us (2%)
    unnamed x4, waiting for transfers between devices  232 us
    psum x1, blocking collectives, on_device(): totals = lax.psum(jnp.where(picks, local_sq[:, None], 0.0), 'head')  77.3 us
    all_gather x1, waiting for transfers between devices, on_device(): lax.all_gather(flat_zx, 'fsdp', axis=0, tiled=True)  71.5 us
    all_gather x1, blocking collectives, on_device(): lax.all_gather(dt_weight, 'fsdp', axis=0, tiled=True)  47.2 us
    all_gather x1, waiting for transfers between devices, on_device(): lax.all_gather(bc_part, 'fsdp', axis=0, tiled=True)  29.5 us
  transfers between devices with their start and end apart: 3, of which 3 were waited for; matrix products, arithmetic and copies ran while one was open for 2% of the time, Pallas kernels for 0%

commit v1 on v0

v1 whole, which is shorter than its diff:
```python
import jax
import jax.numpy as jnp
from jax import lax
from jax.sharding import Mesh, PartitionSpec as P

LEN = 256
FSDP = ("yl", "z", "core")
HEAD = ("yh", "x")
SIZES = (2, 8, 2, 4, 8)


def settle(values):
    return lax.optimization_barrier(values.astype(jnp.bfloat16))


def causal(values, kernel, seq_len):
    columns = values.shape[1]
    seqs = values.reshape(-1, seq_len, columns).astype(jnp.float32)
    taps = kernel.shape[0]
    padded = jnp.pad(seqs, ((0, 0), (taps - 1, 0), (0, 0)))
    total = jnp.zeros(seqs.shape, jnp.float32)
    for tap in range(taps):
        total = total + kernel[tap] * padded[:, tap : tap + seq_len]
    return settle(jax.nn.silu(total).reshape(-1, columns))


def on_device(
    tokens,
    zx_weight,
    dt_weight,
    bc_weight,
    conv_x,
    conv_bc,
    a_log,
    dt_bias,
    d_skip,
    norm_gain,
    out_weight,
):
    f32, bf16 = jnp.float32, jnp.bfloat16
    tok_rows = tokens.shape[0]
    rows, heads_here, two_p = zx_weight.shape
    head_size = two_p // 2
    channels = heads_here * head_size
    n_yh, n_x = lax.axis_size("yh"), lax.axis_size("x")
    group_id = lax.axis_index("yh")
    group_cols = bc_weight.shape[1] // n_yh
    state = group_cols // 2
    bc_part = lax.dynamic_slice_in_dim(bc_weight, group_id * group_cols, group_cols, 1)
    zx_cols = heads_here * two_p
    pad = -(zx_cols + group_cols + heads_here) % 128
    mine = jnp.concatenate(
        [
            zx_weight.reshape(rows, zx_cols),
            bc_part,
            dt_weight,
            jnp.zeros((rows, pad), bf16),
        ],
        axis=1,
    )
    whole = lax.all_gather(mine, FSDP, axis=0, tiled=True)

    width = out_weight.shape[1] // (n_yh * n_x)
    scaled = (out_weight.astype(f32) * norm_gain[:, None]).astype(bf16)
    pieces = scaled.reshape(channels, n_yh, n_x, width).transpose(2, 0, 1, 3)
    pieces = pieces.reshape(n_x, channels, n_yh * width)
    group_weight = lax.all_to_all(pieces, "x", 0, 0).reshape(n_x * channels, n_yh * width)

    whole, group_weight = lax.optimization_barrier((whole, group_weight))
    acc = jnp.dot(tokens, whole, preferred_element_type=f32)
    acc = settle(acc)
    zx = acc[:, :zx_cols].reshape(tok_rows, heads_here, 2, head_size)
    bc_raw = acc[:, zx_cols : zx_cols + group_cols]
    dt_raw = acc[:, zx_cols + group_cols : zx_cols + group_cols + heads_here]
    gate = zx[:, :, 0, :].astype(f32).reshape(tok_rows, channels)
    xin = zx[:, :, 1, :].reshape(tok_rows, channels)
    xconv = causal(xin, conv_x, LEN)
    conv_group = lax.dynamic_slice_in_dim(conv_bc, group_id * group_cols, group_cols, 1)
    bconv = causal(bc_raw, conv_group, LEN)
    count = tok_rows // LEN
    steps = jax.nn.softplus(dt_raw.astype(f32) + dt_bias).reshape(count, LEN, heads_here)
    cum = jnp.cumsum(-steps * jnp.exp(a_log), axis=1)
    seg = cum[:, :, None, :] - cum[:, None, :, :]
    lower = jnp.arange(LEN)[:, None] >= jnp.arange(LEN)[None, :]
    decay = jnp.exp(jnp.where(lower[None, :, :, None], seg, -1e30))
    bseq = bconv[:, :state].reshape(count, LEN, state)
    cseq = bconv[:, state:].reshape(count, LEN, state)
    inner = jnp.einsum("btn,bsn->bts", cseq, bseq, preferred_element_type=f32)
    weights = inner[..., None] * decay * steps[:, None, :, :]
    xval = xconv.astype(f32).reshape(count, LEN, heads_here, head_size)
    ys = jnp.einsum("btsh,bshp->bthp", weights, xval, precision=lax.Precision.HIGHEST)
    ys = ys + d_skip[None, None, :, None] * xval
    gated = (ys.reshape(tok_rows, channels) * jax.nn.silu(gate)).astype(bf16)

    spread = jnp.broadcast_to(gated[None], (n_x, tok_rows, channels))
    group = lax.all_to_all(spread, "x", 0, 0)
    squares = jnp.sum(jnp.square(group.astype(f32)), axis=(0, 2))
    scale = lax.rsqrt(squares / (n_x * channels) + 1e-05)
    parts = jnp.einsum(
        "xtc,xcyw->ytw",
        group,
        group_weight.reshape(n_x, channels, n_yh, width),
        preferred_element_type=f32,
    )
    parts = (parts * scale[None, :, None]).astype(bf16)
    got = lax.all_to_all(parts, "yh", 0, 0)
    return jnp.sum(got.astype(f32), axis=0).astype(bf16)


def solution(mesh):
    fine = Mesh(mesh.devices.reshape(SIZES), FSDP + HEAD)
    in_specs = (
        P(FSDP, None),
        P(FSDP, HEAD, None),
        P(FSDP, HEAD),
        P(FSDP, None),
        P(None, HEAD),
        P(),
        P(HEAD),
        P(HEAD),
        P(HEAD),
        P(HEAD),
        P(HEAD, None),
    )
    return jax.shard_map(
        on_device, mesh=fine, in_specs=in_specs, out_specs=P(FSDP, HEAD), check_vma=False
    )
```

time: 497 us -> 173 us (0.35)
  the two profiles are of different devices: /device:TPU:4 before, /device:TPU:16 now
where the time goes in v1:
time: 173 us; the launch traced here: 172 us
  waiting for transfers between devices  94.1 us (54%)
  local copies, waits for them, and re-layouts  19.7 us (11%)
  blocking collectives  16.8 us (10%)
  starting transfers between devices  13.6 us (8%)
  between operations  13.6 us (8%)
  matrix products  8.71 us (5%)
  other arithmetic  5.42 us (3%)
    all_to_all x1, waiting for transfers between devices, on_device(): lax.all_to_all(pieces, 'x', 0, 0).reshape(n_x * channels, n_yh * width)  50.3 us
    all_to_all x1, waiting for transfers between devices, on_device(): group = lax.all_to_all(spread, 'x', 0, 0)  25.2 us
    all_gather x1, waiting for transfers between devices, on_device(): whole = lax.all_gather(mine, FSDP, axis=0, tiled=True)  18.6 us
    all_to_all x1, blocking collectives, on_device(): got = lax.all_to_all(parts, 'yh', 0, 0)  16.8 us
    all_to_all x1, starting transfers between devices, on_device(): lax.all_to_all(pieces, 'x', 0, 0).reshape(n_x * channels, n_yh * width)  6.89 us
    all_to_all x1, starting transfers between devices, on_device(): group = lax.all_to_all(spread, 'x', 0, 0)  6.67 us
    unnamed x15, local copies, waits for them, and re-layouts  6.05 us
    dot_general x1, matrix products, on_device(): acc = jnp.dot(tokens, whole, preferred_element_type=f32)  5.2 us
  transfers between devices with their start and end apart: 3, of which 3 were waited for; matrix products, arithmetic and copies ran while one was open for 10% of the time, Pallas kernels for 0%

profile of v1, /device:TPU:16, one launch (start us, length us, event | category | flops | bytes accessed | tf_op | source)
XLA Modules:
  0.0 171.8 jit_solution(9687656460526708246)
XLA Ops:
  6.5 1.1 copy.60
  7.6 0.8 copy.33
  8.4 0.8 constant_dynamic-slice_fusion.1
  9.4 0.7 maximum_maximum_fusion
  10.1 4.1 %copy.34 = bf16[256,4096]{0,1:T(8,128)(2,1)} copy(bf16[256,4096]{1,0:T(8,128)(2,1)} %param.21) | data formatting | bytes 4194304 | tf_op args[10]
  14.3 2.0 %multiply_convert_fusion = bf16[256,4096]{0,1:T(8,128)(2,1)S(1)} fusion(bf16[256,4096]{0,1:T(8,128)(2,1)} %copy.34, f32[256]{0:T(256)S(1)} %copy-done.2), kind=kLoop, calls=%fused_computation | loop fusion | flops 3145728 | bytes 4195328 | tf_op jit(solution)/shard_map/convert_element_type | solution.py:64
  16.3 1.5 copy.35
  17.8 6.9 %all-to-all-start = ((bf16[8,256,512]{1,2,0:T(8,128)(2,1)}), bf16[8,256,512]{1,2,0:T(8,128)(2,1)}, u32[]{:S(2)}, u32[]{:S(2)}) async-start(bf16[8,256,512]{1,2,0:T(8,128)(2,1)} %bitcast.84), calls=%async_computation | async-start | bytes 4194304 | tf_op jit(solution)/shard_map/all_to_all | solution.py:67
  24.7 0.9 constant_dynamic-slice_fusion
  25.7 50.3 %all-to-all-done = bf16[8,256,512]{1,2,0:T(8,128)(2,1)} async-done(((bf16[8,256,512]{1,2,0:T(8,128)(2,1)}), bf16[8,256,512]{1,2,0:T(8,128)(2,1)}, u32[]{:S(2)}, u32[]{:S(2)}) %all-to-all-start) | async-done | bytes 2097184 | tf_op jit(solution)/shard_map/all_to_all | solution.py:67
  76.0 4.0 %copy.36 = bf16[8,256,512]{2,1,0:T(8,128)(2,1)} copy(bf16[8,256,512]{1,2,0:T(8,128)(2,1)} %all-to-all-done) | data formatting | bytes 4194304 | tf_op jit(solution)/shard_map/all_to_all | solution.py:67
  80.0 18.6 %all-gather.2.cloned.1.call-done = bf16[4096,896]{1,0:T(8,128)(2,1)} async-done(((bf16[128,896]{1,0:T(8,128)(2,1)}), bf16[4096,896]{1,0:T(8,128)(2,1)}) %all-gather.2.cloned.1.call-update) | async-done | bytes 7340048 | tf_op jit(solution)/shard_map/all_gather | solution.py:61
  98.6 5.2 %fusion.8 = bf16[256,896]{0,1:T(8,128)(2,1)S(1)} fusion(bf16[4096,896]{1,0:T(8,128)(2,1)} %all-gather.2.cloned.1.call-done, bf16[256,4096]{1,0:T(8,128)(2,1)S(1)} %copy-done), kind=kOutput, calls=%fused_computation.7 | convolution fusion | flops 1879277568 | bytes 9895936 | tf_op jit(solution)/shard_map/dot_general | solution.py:70
  103.9 1.2 reduce-window.6
  105.3 0.4 fusion.46
  106.3 0.4 fusion.47
  106.7 1.0 fusion.12
  107.9 1.1 broadcast_in_dim.19
  109.0 6.7 %all-to-all-start.1 = ((bf16[8,256,256]{2,1,0:T(8,128)(2,1)}), bf16[8,256,256]{2,1,0:T(8,128)(2,1)S(1)}, u32[]{:S(2)}, u32[]{:S(2)}) async-start(bf16[8,256,256]{2,1,0:T(8,128)(2,1)} %broadcast_in_dim.19), calls=%async_computation.1 | async-start | bytes 2097152 | tf_op jit(solution)/shard_map/all_to_all | solution.py:96
  115.6 3.9 %reshape.254 = bf16[8,256,4,128]{3,2,1,0:T(4,128)(2,1)} reshape(bf16[2048,512]{1,0:T(8,128)(2,1)} %bitcast.83) | data formatting | bytes 4194304 | tf_op jit(solution)/shard_map/reshape | solution.py:102
  119.6 25.2 %all-to-all-done.1 = bf16[8,256,256]{2,1,0:T(8,128)(2,1)S(1)} async-done(((bf16[8,256,256]{2,1,0:T(8,128)(2,1)}), bf16[8,256,256]{2,1,0:T(8,128)(2,1)S(1)}, u32[]{:S(2)}, u32[]{:S(2)}) %all-to-all-start.1) | async-done | bytes 1048608 | tf_op jit(solution)/shard_map/all_to_all | solution.py:96
  145.1 2.4 %fusion.13 = bf16[4,256,128]{1,2,0:T(8,128)(2,1)S(1)} fusion(bf16[8,256,4,128]{3,2,1,0:T(4,128)(2,1)} %reshape.254, bf16[8,256,256]{2,1,0:T(8,128)(2,1)S(1)} %all-to-all-done.1, f32[256]{0:T(256)S(1)} %add_rsqrt_fusion), kind=kOutput, calls=%fused_computation.11 | convolution fusion | flops 537133056 | bytes 3408896 | tf_op jit(solution)/shard_map/xtc,xcyw->ytw/dot_general | solution.py:99
  147.4 16.8 %all_to_all.15 = bf16[4,256,128]{1,2,0:T(8,128)(2,1)S(1)} all-to-all(bf16[4,256,128]{1,2,0:T(8,128)(2,1)S(1)} %fusion.13), channel_id=1, replica_groups=mesh['yl'=2,'z'=8,'core'=2,'yh'=4,'x'=8] {'yh'}, dimensions={0} | all-to-all | bytes 524288 | tf_op jit(solution)/shard_map/all_to_all | solution.py:106
  164.3 0.7 copy.43
  (40 shorter events, 1.5 us)
Async XLA Ops:
  6.5 92.0 %copy-start = (bf16[256,4096]{1,0:T(8,128)(2,1)S(1)}, bf16[256,4096]{1,0:T(8,128)(2,1)}, u32[]{:S(2)}) copy-start(bf16[256,4096]{1,0:T(8,128)(2,1)} %param.11) | copy-start | bytes 6291460
  6.5 92.0 %all-gather.2.cloned.1.call-start = ((), (), s32[]{:S(2)}) async-start(), calls=%async_computation.3 | async-start | bytes 7569408 | tf_op jit(solution)/shard_map/all_gather | solution.py:61
  10.1 4.2 %copy-start.2 = (f32[256]{0:T(256)S(1)}, f32[256]{0:T(256)}, u32[]{:S(2)}) copy-start(f32[256]{0:T(256)} %param.20) | copy-start | bytes 3076
  17.8 6.9 %copy-start.4 = (f32[4]{0:T(128)S(1)}, f32[4]{0:T(128)}, u32[]{:S(2)}) copy-start(f32[4]{0:T(128)} %param.17) | copy-start | bytes 52
  17.8 7.9 %copy-start.1 = (f32[4,256]{1,0:T(4,128)S(1)}, f32[4,256]{1,0:T(4,128)}, u32[]{:S(2)}) copy-start(f32[4,256]{1,0:T(4,128)} %param.15) | copy-start | bytes 12292
  17.8 58.2 %all-to-all-start = ((bf16[8,256,512]{1,2,0:T(8,128)(2,1)}), bf16[8,256,512]{1,2,0:T(8,128)(2,1)}, u32[]{:S(2)}, u32[]{:S(2)}) async-start(bf16[8,256,512]{1,2,0:T(8,128)(2,1)} %bitcast.84), calls=%async_computation | async-start | bytes 4194304 | tf_op jit(solution)/shard_map/all_to_all | solution.py:67
  98.6 5.2 %copy-start.3 = (f32[4]{0:T(128)S(1)}, f32[4]{0:T(128)}, u32[]{:S(2)}) copy-start(f32[4]{0:T(128)} %param.18) | copy-start | bytes 52
  103.8 3.0 %copy-start.5 = (f32[4]{0:T(128)S(1)}, f32[4]{0:T(128)}, u32[]{:S(2)}) copy-start(f32[4]{0:T(128)} %param.19) | copy-start | bytes 52
  109.0 35.8 %all-to-all-start.1 = ((bf16[8,256,256]{2,1,0:T(8,128)(2,1)}), bf16[8,256,256]{2,1,0:T(8,128)(2,1)S(1)}, u32[]{:S(2)}, u32[]{:S(2)}) async-start(bf16[8,256,256]{2,1,0:T(8,128)(2,1)} %broadcast_in_dim.19), calls=%async_computation.1 | async-start | bytes 2097152 | tf_op jit(solution)/shard_map/all_to_all | solution.py:96
Sparse Core Ops, SparseCore 0:
  10.2 88.2 all-gather.1

commit v2 on v1

--- a/solution.py
+++ b/solution.py
@@ -1,12 +1,40 @@
 import jax
 import jax.numpy as jnp
 from jax import lax
+from jax.experimental import pallas as pl
 from jax.sharding import Mesh, PartitionSpec as P
 
 LEN = 256
 FSDP = ("yl", "z", "core")
 HEAD = ("yh", "x")
 SIZES = (2, 8, 2, 4, 8)
+SWAP = [(0, 1), (1, 0)]
+
+
+def repack(weight, gain, n_yh, n_x):
+    rows, columns = weight.shape
+    width = columns // (n_yh * n_x)
+
+    def kernel(gain_ref, *refs):
+        out_ref = refs[-1]
+        for i, ref in enumerate(refs[:-1]):
+            value = ref[...].astype(jnp.float32) * gain_ref[...]
+            out_ref[0, :, i * width : (i + 1) * width] = value.astype(jnp.bfloat16)
+
+    def spec(i):
+        return pl.BlockSpec((rows, width), lambda x: (0, i * n_x + x))
+
+    return pl.pallas_call(
+        kernel,
+        grid=(n_x,),
+        in_specs=[pl.BlockSpec((rows, 1), lambda x: (0, 0))] + [spec(i) for i in range(n_yh)],
+        out_specs=pl.BlockSpec((1, rows, n_yh * width), lambda x: (x, 0, 0)),
+        out_shape=jax.ShapeDtypeStruct((n_x, rows, n_yh * width), jnp.bfloat16),
+        cost_estimate=pl.CostEstimate(
+            flops=rows * columns, bytes_accessed=4 * rows * columns, transcendentals=0
+        ),
+        name="repack",
+    )(gain[:, None], *[weight] * n_yh)
 
 
 def settle(values):
@@ -24,7 +52,7 @@
     return settle(jax.nn.silu(total).reshape(-1, columns))
 
 
-def on_device(
+def layer(
     tokens,
     zx_weight,
     dt_weight,
@@ -58,17 +86,53 @@
         ],
         axis=1,
     )
-    whole = lax.all_gather(mine, FSDP, axis=0, tiled=True)
+    k_half, z_pos, c_pos = lax.axis_index("yl"), lax.axis_index("z"), lax.axis_index("core")
+    n_z = lax.axis_size("z")
+    k_rows = tokens.shape[1] // 2
+    kept = lax.dynamic_slice_in_dim(tokens, k_half * k_rows, k_rows, 1)
+    given = lax.dynamic_slice_in_dim(tokens, (1 - k_half) * k_rows, k_rows, 1)
+    given = lax.ppermute(given, "yl", SWAP)
+
+    up = [(i, (i + 1) % n_z) for i in range(n_z)]
+    down = [(i, (i - 1) % n_z) for i in range(n_z)]
+    own = jnp.zeros((n_z,) + mine.shape, bf16)
+
+    def place(total, block, offset, row=0):
+        return lax.dynamic_update_slice(total, block[None], ((z_pos + offset) % n_z, row, 0))
+
+    own = place(own, mine, 0)
+    above = below = mine
+    for i in range(1, n_z // 2):
+        below = lax.ppermute(below, "z", up)
+        above = lax.ppermute(above, "z", down)
+        own = place(place(own, below, -i), above, i)
+    below = lax.ppermute(below[: rows // 2], "z", up)
+    above = lax.ppermute(above[rows // 2 :], "z", down)
+    own = place(place(own, below, n_z // 2), above, n_z // 2, rows // 2)
+    theirs = lax.ppermute(own, "core", SWAP)
 
     width = out_weight.shape[1] // (n_yh * n_x)
-    scaled = (out_weight.astype(f32) * norm_gain[:, None]).astype(bf16)
-    pieces = scaled.reshape(channels, n_yh, n_x, width).transpose(2, 0, 1, 3)
-    pieces = pieces.reshape(n_x, channels, n_yh * width)
-    group_weight = lax.all_to_all(pieces, "x", 0, 0).reshape(n_x * channels, n_yh * width)
+    pieces = repack(out_weight, norm_gain, n_yh, n_x)
+    group_weight = lax.all_to_all(pieces, "x", 0, 0)
+    group_weight = group_weight.reshape(n_x * channels, n_yh * width)
 
-    whole, group_weight = lax.optimization_barrier((whole, group_weight))
-    acc = jnp.dot(tokens, whole, preferred_element_type=f32)
-    acc = settle(acc)
+    def by_core(values):
+        split = values.reshape(tok_rows, n_z, 2, rows)
+        first = split[:, :, 0].reshape(tok_rows, n_z * rows)
+        second = split[:, :, 1].reshape(tok_rows, n_z * rows)
+        return jnp.where(c_pos == 0, first, second), jnp.where(c_pos == 0, second, first)
+
+    def product(pair):
+        return sum(
+            jnp.dot(left, right.reshape(n_z * rows, -1), preferred_element_type=f32)
+            for left, right in zip(pair, (own, theirs))
+        )
+
+    kept, given = by_core(kept), by_core(given)
+    away = lax.ppermute(product(given).astype(bf16), "yl", SWAP)
+    acc = product(kept)
+    acc = acc + away.astype(f32)
+    acc, group_weight = lax.optimization_barrier((acc, group_weight))
     zx = acc[:, :zx_cols].reshape(tok_rows, heads_here, 2, head_size)
     bc_raw = acc[:, zx_cols : zx_cols + group_cols]
     dt_raw = acc[:, zx_cols + group_cols : zx_cols + group_cols + heads_here]
@@ -123,5 +187,5 @@
         P(HEAD, None),
     )
     return jax.shard_map(
-        on_device, mesh=fine, in_specs=in_specs, out_specs=P(FSDP, HEAD), check_vma=False
+        layer, mesh=fine, in_specs=in_specs, out_specs=P(FSDP, HEAD), check_vma=False
     )

time: 173 us -> 179 us (1.035)
  starting transfers between devices: 13.6 us -> 60.5 us
  waiting for transfers between devices: 94.1 us -> 63 us
  between operations: 13.6 us -> 0.44 us
  Pallas kernels: 0 us -> 6.43 us
  local copies, waits for them, and re-layouts: 19.7 us -> 16 us
    all_to_all x2, waiting for transfers between devices: 75.5 us -> 23.7 us  [the longest x1 23.7 us: layer(): group = lax.all_to_all(spread, 'x', 0, 0)]
    ppermute x0 -> x11, starting transfers between devices: none -> 46.8 us  [the longest x3 24.3 us: layer(): above = lax.ppermute(above, 'z', down)]
    ppermute x0 -> x11, waiting for transfers between devices: none -> 39.4 us  [the longest x1 24 us: layer(): given = lax.ppermute(given, 'yl', SWAP)]
    all_gather x1 -> x0, waiting for transfers between devices: 18.6 us -> none  [on_device(): whole = lax.all_gather(mine, FSDP, axis=0, tiled=True)]
    pallas_call x0 -> x1, Pallas kernels: none -> 6.43 us  [repack(): pl.pallas_call(kernel, grid=(n_x,), in_specs=[pl.BlockSpec((rows, 1), lam...]
    all_to_all x1 -> x0, local copies, waits for them, and re-layouts: 3.96 us -> none  [on_device(): lax.all_to_all(pieces, 'x', 0, 0).reshape(n_x * channels, n_yh * width)]
    convert_element_type x4 -> x1, other arithmetic: 2.14 us -> 0.08 us  [layer(): gated = (ys.reshape(tok_rows, channels) * jax.nn.silu(gate)).astype(bf16)]
    dynamic_slice x1 -> x2, local copies, waits for them, and re-layouts: 0.85 us -> 2.75 us  [the longest x1 2.74 us: layer(): given = lax.dynamic_slice_in_dim(tokens, (1 - k_half) * k_rows, k_rows, 1)]
  transfers between devices with their start and end apart: 3 -> 13, of which waited for: 3 -> 7; matrix products, arithmetic and copies ran while one was open for 10% -> 11% of each run, Pallas kernels for 0% -> 4%
where the time goes in v2:
time: 179 us; the launch traced here: 178 us
  waiting for transfers between devices  63 us (35%)
  starting transfers between devices  60.5 us (34%)
  blocking collectives  17.5 us (10%)
  local copies, waits for them, and re-layouts  16 us (9%)
  matrix products  9.88 us (6%)
  Pallas kernels  6.43 us (4%)
  other arithmetic  4.05 us (2%)
    ppermute x3, starting transfers between devices, layer(): above = lax.ppermute(above, 'z', down)  24.3 us
    ppermute x1, waiting for transfers between devices, layer(): given = lax.ppermute(given, 'yl', SWAP)  24 us
    all_to_all x1, waiting for transfers between devices, layer(): group = lax.all_to_all(spread, 'x', 0, 0)  23.7 us
    all_to_all x1, blocking collectives, layer(): got = lax.all_to_all(parts, 'yh', 0, 0)  17.5 us
    ppermute x3, starting transfers between devices, layer(): below = lax.ppermute(below, 'z', up)  9.02 us
    ppermute x1, waiting for transfers between devices, layer(): away = lax.ppermute(product(given).astype(bf16), 'yl', SWAP)  8.39 us
    all_to_all x1, starting transfers between devices, layer(): group = lax.all_to_all(spread, 'x', 0, 0)  6.91 us
    all_to_all x1, starting transfers between devices, layer(): group_weight = lax.all_to_all(pieces, 'x', 0, 0)  6.76 us
  transfers between devices with their start and end apart: 13, of which 7 were waited for; matrix products, arithmetic and copies ran while one was open for 11% of the time, Pallas kernels for 4%

profile of v2, /device:TPU:16, one launch (start us, length us, event | category | flops | bytes accessed | tf_op | source)
XLA Modules:
  0.0 177.8 jit_solution(9054815211974508559)
XLA Ops:
  2.2 5.2 %collective-permute-start = (bf16[128,896]{1,0:T(8,128)(2,1)S(1)}, bf16[128,896]{1,0:T(8,128)(2,1)S(1)}, u32[]{:S(2)}, u32[]{:S(2)}) collective-permute-start(bf16[128,896]{1,0:T(8,128)(2,1)S(1)} %get-tuple-element.12), channel_id=1, source_target_pairs={{0,64},{64,128},{128,192},{192,256},{256,320},{320,384},{384,448},... | collective-permute-start | bytes 688136 | tf_op jit(solution)/shard_map/ppermute | solution.py:106
  7.4 14.0 %collective-permute-start.1 = (bf16[128,896]{1,0:T(8,128)(2,1)S(1)}, bf16[128,896]{1,0:T(8,128)(2,1)S(1)}, u32[]{:S(2)}, u32[]{:S(2)}) collective-permute-start(bf16[128,896]{1,0:T(8,128)(2,1)S(1)} %get-tuple-element.12), channel_id=1, source_target_pairs={{0,448},{64,0},{128,64},{192,128},{256,192},{320,256},{384,320},{4... | collective-permute-start | bytes 688136 | tf_op jit(solution)/shard_map/ppermute | solution.py:107
  22.3 6.4 %repack.1 = bf16[8,256,512]{2,1,0:T(8,128)(2,1)} custom-call(f32[256,1]{1,0:T(8,128)} %copy.77.gain_ref, bf16[256,4096]{1,0:T(8,128)(2,1)} %refs_3_.1, bf16[256,4096]{1,0:T(8,128)(2,1)} %refs_3_.1, bf16[256,4096]{1,0:T(8,128)(2,1)} %refs_3_.1, bf16[256,4096]{1,0:T(8,128)(2,1)} %refs_3_.1), custom_call_target="tpu_custom_call" | custom-call | flops 1048576 | bytes 4194304 | tf_op jit(solution)/shard_map/repack/pallas_call | solution.py:27
  28.7 6.8 %all-to-all-start = ((bf16[8,256,512]{2,1,0:T(8,128)(2,1)}), bf16[8,256,512]{2,1,0:T(8,128)(2,1)}, u32[]{:S(2)}, u32[]{:S(2)}) async-start(bf16[8,256,512]{2,1,0:T(8,128)(2,1)} %repack.1), calls=%async_computation | async-start | bytes 4194304 | tf_op jit(solution)/shard_map/all_to_all | solution.py:116
  35.5 1.9 %collective-permute-start.2 = (bf16[128,896]{1,0:T(8,128)(2,1)S(1)}, bf16[128,896]{1,0:T(8,128)(2,1)S(1)}, u32[]{:S(2)}, u32[]{:S(2)}) collective-permute-start(bf16[128,896]{1,0:T(8,128)(2,1)S(1)} %collective-permute-done), channel_id=1, source_target_pairs={{0,64},{64,128},{128,192},{192,256},{256,320},{320,384},{384,448},... | collective-permute-start | bytes 688136 | tf_op jit(solution)/shard_map/ppermute | solution.py:106
  37.4 5.1 %collective-permute-start.3 = (bf16[128,896]{1,0:T(8,128)(2,1)S(1)}, bf16[128,896]{1,0:T(8,128)(2,1)S(1)}, u32[]{:S(2)}, u32[]{:S(2)}) collective-permute-start(bf16[128,896]{1,0:T(8,128)(2,1)S(1)} %collective-permute-done.1), channel_id=1, source_target_pairs={{0,448},{64,0},{128,64},{192,128},{256,192},{320,256},{384,320},{4... | collective-permute-start | bytes 688136 | tf_op jit(solution)/shard_map/ppermute | solution.py:107
  42.6 2.7 %collective-permute-done.2 = bf16[128,896]{1,0:T(8,128)(2,1)S(1)} collective-permute-done((bf16[128,896]{1,0:T(8,128)(2,1)S(1)}, bf16[128,896]{1,0:T(8,128)(2,1)S(1)}, u32[]{:S(2)}, u32[]{:S(2)}) %collective-permute-start.2) | collective-permute-done | bytes 229408 | tf_op jit(solution)/shard_map/ppermute | solution.py:106
  47.3 5.1 %collective-permute-start.5 = (bf16[128,896]{1,0:T(8,128)(2,1)S(1)}, bf16[128,896]{1,0:T(8,128)(2,1)S(1)}, u32[]{:S(2)}, u32[]{:S(2)}) collective-permute-start(bf16[128,896]{1,0:T(8,128)(2,1)S(1)} %collective-permute-done.3), channel_id=1, source_target_pairs={{0,448},{64,0},{128,64},{192,128},{256,192},{320,256},{384,320},{4... | collective-permute-start | bytes 688136 | tf_op jit(solution)/shard_map/ppermute | solution.py:107
  52.5 2.0 %collective-permute-done.4 = bf16[128,896]{1,0:T(8,128)(2,1)S(1)} collective-permute-done((bf16[128,896]{1,0:T(8,128)(2,1)S(1)}, bf16[128,896]{1,0:T(8,128)(2,1)S(1)}, u32[]{:S(2)}, u32[]{:S(2)}) %collective-permute-start.4) | collective-permute-done | bytes 229408 | tf_op jit(solution)/shard_map/ppermute | solution.py:106
  54.5 1.9 %collective-permute-start.6 = (bf16[64,896]{1,0:T(8,128)(2,1)S(1)}, bf16[64,896]{1,0:T(8,128)(2,1)S(1)}, u32[]{:S(2)}, u32[]{:S(2)}) collective-permute-start(bf16[64,896]{1,0:T(8,128)(2,1)S(1)} %slice.120), channel_id=1, source_target_pairs={{0,64},{64,128},{128,192},{192,256},{256,320},{320,384},{384,448},... | collective-permute-start | bytes 344072 | tf_op jit(solution)/shard_map/ppermute | solution.py:109
  56.4 5.1 %collective-permute-start.7 = (bf16[64,896]{1,0:T(8,128)(2,1)S(1)}, bf16[64,896]{1,0:T(8,128)(2,1)S(1)}, u32[]{:S(2)}, u32[]{:S(2)}) collective-permute-start(bf16[64,896]{1,0:T(8,128)(2,1)S(1)} %slice.121), channel_id=1, source_target_pairs={{0,448},{64,0},{128,64},{192,128},{256,192},{320,256},{384,320},{4... | collective-permute-start | bytes 344072 | tf_op jit(solution)/shard_map/ppermute | solution.py:110
  63.9 1.9 %collective-permute-start.8 = (bf16[8,128,896]{2,1,0:T(8,128)(2,1)S(1)}, bf16[8,128,896]{2,1,0:T(8,128)(2,1)}, u32[]{:S(2)}, u32[]{:S(2)}) collective-permute-start(bf16[8,128,896]{2,1,0:T(8,128)(2,1)S(1)} %bitcast_dynamic-update-slice_fusion.7), channel_id=1, source_target_pairs={{0,32},{32,0},{1,33},{33,1},{2,34},{34,2},{3,35},{35,3},{4,36},{36... | collective-permute-start | bytes 5505032 | tf_op jit(solution)/shard_map/ppermute | solution.py:112
  65.9 2.7 %constant_dynamic-slice_fusion.1 = (bf16[256,2048]{1,0:T(8,128)(2,1)S(1)}, bf16[256,2048]{1,0:T(8,128)(2,1)}) fusion(bf16[256,4096]{1,0:T(8,128)(2,1)} %param.11, s32[]{:T(128)S(6)} %select_n.138, s32[]{:T(128)S(6)} %select_n.116), kind=kLoop, calls=%fused_computation.79 | loop fusion | bytes 4194312 | tf_op jit(solution)/shard_map/dynamic_slice | solution.py:93
  69.9 2.2 %collective-permute-start.9 = (bf16[256,2048]{0,1:T(8,128)(2,1)}, bf16[256,2048]{0,1:T(8,128)(2,1)}, u32[]{:S(2)}, u32[]{:S(2)}) collective-permute-start(bf16[256,2048]{0,1:T(8,128)(2,1)} %copy.92), channel_id=1, source_target_pairs={{0,512},{512,0},{1,513},{513,1},{2,514},{514,2},{3,515},{515,3},{4... | collective-permute-start | bytes 3145736 | tf_op jit(solution)/shard_map/ppermute | solution.py:94
  73.7 24.0 %collective-permute-done.9 = bf16[256,2048]{0,1:T(8,128)(2,1)} collective-permute-done((bf16[256,2048]{0,1:T(8,128)(2,1)}, bf16[256,2048]{0,1:T(8,128)(2,1)}, u32[]{:S(2)}, u32[]{:S(2)}) %collective-permute-start.9) | collective-permute-done | bytes 1048608 | tf_op jit(solution)/shard_map/ppermute | solution.py:94
  99.1 2.3 %fusion.55 = f32[256,896]{0,1:T(8,128)S(1)} fusion(bf16[256,1024]{0,1:T(8,128)(2,1)S(1)} %bitcast.122, bf16[1024,896]{1,0:T(8,128)(2,1)} %bitcast.13), kind=kOutput, calls=%fused_computation.88 | convolution fusion | flops 469762048 | bytes 3276800 | tf_op jit(solution)/shard_map/dot_general | solution.py:127
  102.3 2.2 %collective-permute-start.10 = (bf16[256,896]{0,1:T(8,128)(2,1)S(1)}, bf16[256,896]{0,1:T(8,128)(2,1)S(1)}, u32[]{:S(2)}, u32[]{:S(2)}) collective-permute-start(bf16[256,896]{0,1:T(8,128)(2,1)S(1)} %fusion.3), channel_id=1, source_target_pairs={{0,512},{512,0},{1,513},{513,1},{2,514},{514,2},{3,515},{515,3},{4... | collective-permute-start | bytes 1376264 | tf_op jit(solution)/shard_map/ppermute | solution.py:132
  105.5 2.3 %fusion.54 = f32[256,896]{0,1:T(8,128)S(1)} fusion(bf16[256,1024]{0,1:T(8,128)(2,1)S(1)} %bitcast.120, bf16[1024,896]{1,0:T(8,128)(2,1)} %bitcast.13), kind=kOutput, calls=%fused_computation.87 | convolution fusion | flops 469762048 | bytes 3276800 | tf_op jit(solution)/shard_map/dot_general | solution.py:127
  107.8 8.4 %collective-permute-done.10 = bf16[256,896]{0,1:T(8,128)(2,1)S(1)} collective-permute-done((bf16[256,896]{0,1:T(8,128)(2,1)S(1)}, bf16[256,896]{0,1:T(8,128)(2,1)S(1)}, u32[]{:S(2)}, u32[]{:S(2)}) %collective-permute-start.10) | collective-permute-done | bytes 458784 | tf_op jit(solution)/shard_map/ppermute | solution.py:132
  122.3 6.9 %all-to-all-start.1 = ((bf16[8,256,256]{2,1,0:T(8,128)(2,1)}), bf16[8,256,256]{2,1,0:T(8,128)(2,1)S(1)}, u32[]{:S(2)}, u32[]{:S(2)}) async-start(bf16[8,256,256]{2,1,0:T(8,128)(2,1)} %broadcast_in_dim.78), calls=%async_computation.1 | async-start | bytes 2097152 | tf_op jit(solution)/shard_map/all_to_all | solution.py:160
  129.2 4.0 %reshape.255 = bf16[8,256,4,128]{3,2,1,0:T(4,128)(2,1)} reshape(bf16[2048,512]{1,0:T(8,128)(2,1)} %bitcast.18) | data formatting | bytes 4194304 | tf_op jit(solution)/shard_map/reshape | solution.py:166
  133.2 23.7 %all-to-all-done.1 = bf16[8,256,256]{2,1,0:T(8,128)(2,1)S(1)} async-done(((bf16[8,256,256]{2,1,0:T(8,128)(2,1)}), bf16[8,256,256]{2,1,0:T(8,128)(2,1)S(1)}, u32[]{:S(2)}, u32[]{:S(2)}) %all-to-all-start.1) | async-done | bytes 1048608 | tf_op jit(solution)/shard_map/all_to_all | solution.py:160
  157.2 2.4 %fusion.14 = bf16[4,256,128]{1,2,0:T(8,128)(2,1)S(1)} fusion(bf16[8,256,4,128]{3,2,1,0:T(4,128)(2,1)} %reshape.255, bf16[8,256,256]{2,1,0:T(8,128)(2,1)S(1)} %all-to-all-done.1, f32[256]{0:T(256)S(1)} %add_rsqrt_fusion), kind=kOutput, calls=%fused_computation.12 | convolution fusion | flops 537133056 | bytes 3408896 | tf_op jit(solution)/shard_map/xtc,xcyw->ytw/dot_general | solution.py:163
  159.5 17.5 %all_to_all.15 = bf16[4,256,128]{1,2,0:T(8,128)(2,1)S(1)} all-to-all(bf16[4,256,128]{1,2,0:T(8,128)(2,1)S(1)} %fusion.14), channel_id=1, replica_groups=mesh['yl'=2,'z'=8,'core'=2,'yh'=4,'x'=8] {'yh'}, dimensions={0} | all-to-all | bytes 524288 | tf_op jit(solution)/shard_map/all_to_all | solution.py:170
  (74 shorter events, 20.4 us)
Async XLA Ops:
  0.0 1.9 %copy-start = (bf16[128,1024]{1,0:T(8,128)(2,1)S(1)}, bf16[128,1024]{1,0:T(8,128)(2,1)}, u32[]{:S(2)}) copy-start(bf16[128,1024]{1,0:T(8,128)(2,1)} %param.14) | copy-start | bytes 786436
  0.0 21.4 %copy-start.2 = (f32[256]{0:T(256)S(1)}, f32[256]{0:T(256)}, u32[]{:S(2)}) copy-start(f32[256]{0:T(256)} %param.20) | copy-start | bytes 3076
  2.2 33.3 %collective-permute-start = (bf16[128,896]{1,0:T(8,128)(2,1)S(1)}, bf16[128,896]{1,0:T(8,128)(2,1)S(1)}, u32[]{:S(2)}, u32[]{:S(2)}) collective-permute-start(bf16[128,896]{1,0:T(8,128)(2,1)S(1)} %get-tuple-element.12), channel_id=1, source_target_pairs={{0,64},{64,128},{128,192},{192,256},{256,320},{320,384},{384,448},... | collective-permute-start | bytes 688136 | tf_op jit(solution)/shard_map/ppermute | solution.py:106
  7.4 30.0 %collective-permute-start.1 = (bf16[128,896]{1,0:T(8,128)(2,1)S(1)}, bf16[128,896]{1,0:T(8,128)(2,1)S(1)}, u32[]{:S(2)}, u32[]{:S(2)}) collective-permute-start(bf16[128,896]{1,0:T(8,128)(2,1)S(1)} %get-tuple-element.12), channel_id=1, source_target_pairs={{0,448},{64,0},{128,64},{192,128},{256,192},{320,256},{384,320},{4... | collective-permute-start | bytes 688136 | tf_op jit(solution)/shard_map/ppermute | solution.py:107
  28.7 88.4 %all-to-all-start = ((bf16[8,256,512]{2,1,0:T(8,128)(2,1)}), bf16[8,256,512]{2,1,0:T(8,128)(2,1)}, u32[]{:S(2)}, u32[]{:S(2)}) async-start(bf16[8,256,512]{2,1,0:T(8,128)(2,1)} %repack.1), calls=%async_computation | async-start | bytes 4194304 | tf_op jit(solution)/shard_map/all_to_all | solution.py:116
  35.5 9.9 %collective-permute-start.2 = (bf16[128,896]{1,0:T(8,128)(2,1)S(1)}, bf16[128,896]{1,0:T(8,128)(2,1)S(1)}, u32[]{:S(2)}, u32[]{:S(2)}) collective-permute-start(bf16[128,896]{1,0:T(8,128)(2,1)S(1)} %collective-permute-done), channel_id=1, source_target_pairs={{0,64},{64,128},{128,192},{192,256},{256,320},{320,384},{384,448},... | collective-permute-start | bytes 688136 | tf_op jit(solution)/shard_map/ppermute | solution.py:106
  37.4 9.9 %collective-permute-start.3 = (bf16[128,896]{1,0:T(8,128)(2,1)S(1)}, bf16[128,896]{1,0:T(8,128)(2,1)S(1)}, u32[]{:S(2)}, u32[]{:S(2)}) collective-permute-start(bf16[128,896]{1,0:T(8,128)(2,1)S(1)} %collective-permute-done.1), channel_id=1, source_target_pairs={{0,448},{64,0},{128,64},{192,128},{256,192},{320,256},{384,320},{4... | collective-permute-start | bytes 688136 | tf_op jit(solution)/shard_map/ppermute | solution.py:107
  45.3 9.1 %collective-permute-start.4 = (bf16[128,896]{1,0:T(8,128)(2,1)S(1)}, bf16[128,896]{1,0:T(8,128)(2,1)S(1)}, u32[]{:S(2)}, u32[]{:S(2)}) collective-permute-start(bf16[128,896]{1,0:T(8,128)(2,1)S(1)} %collective-permute-done.2), channel_id=1, source_target_pairs={{0,64},{64,128},{128,192},{192,256},{256,320},{320,384},{384,448},... | collective-permute-start | bytes 688136 | tf_op jit(solution)/shard_map/ppermute | solution.py:106
  47.3 9.1 %collective-permute-start.5 = (bf16[128,896]{1,0:T(8,128)(2,1)S(1)}, bf16[128,896]{1,0:T(8,128)(2,1)S(1)}, u32[]{:S(2)}, u32[]{:S(2)}) collective-permute-start(bf16[128,896]{1,0:T(8,128)(2,1)S(1)} %collective-permute-done.3), channel_id=1, source_target_pairs={{0,448},{64,0},{128,64},{192,128},{256,192},{320,256},{384,320},{4... | collective-permute-start | bytes 688136 | tf_op jit(solution)/shard_map/ppermute | solution.py:107
  54.5 7.9 %collective-permute-start.6 = (bf16[64,896]{1,0:T(8,128)(2,1)S(1)}, bf16[64,896]{1,0:T(8,128)(2,1)S(1)}, u32[]{:S(2)}, u32[]{:S(2)}) collective-permute-start(bf16[64,896]{1,0:T(8,128)(2,1)S(1)} %slice.120), channel_id=1, source_target_pairs={{0,64},{64,128},{128,192},{192,256},{256,320},{320,384},{384,448},... | collective-permute-start | bytes 344072 | tf_op jit(solution)/shard_map/ppermute | solution.py:109
  56.4 7.5 %collective-permute-start.7 = (bf16[64,896]{1,0:T(8,128)(2,1)S(1)}, bf16[64,896]{1,0:T(8,128)(2,1)S(1)}, u32[]{:S(2)}, u32[]{:S(2)}) collective-permute-start(bf16[64,896]{1,0:T(8,128)(2,1)S(1)} %slice.121), channel_id=1, source_target_pairs={{0,448},{64,0},{128,64},{192,128},{256,192},{320,256},{384,320},{4... | collective-permute-start | bytes 344072 | tf_op jit(solution)/shard_map/ppermute | solution.py:110
  63.9 35.1 %collective-permute-start.8 = (bf16[8,128,896]{2,1,0:T(8,128)(2,1)S(1)}, bf16[8,128,896]{2,1,0:T(8,128)(2,1)}, u32[]{:S(2)}, u32[]{:S(2)}) collective-permute-start(bf16[8,128,896]{2,1,0:T(8,128)(2,1)S(1)} %bitcast_dynamic-update-slice_fusion.7), channel_id=1, source_target_pairs={{0,32},{32,0},{1,33},{33,1},{2,34},{34,2},{3,35},{35,3},{4,36},{36... | collective-permute-start | bytes 5505032 | tf_op jit(solution)/shard_map/ppermute | solution.py:112
  68.6 5.1 %copy-start.1 = (f32[4,256]{1,0:T(4,128)S(1)}, f32[4,256]{1,0:T(4,128)}, u32[]{:S(2)}) copy-start(f32[4,256]{1,0:T(4,128)} %param.15) | copy-start | bytes 12292
  69.9 27.8 %collective-permute-start.9 = (bf16[256,2048]{0,1:T(8,128)(2,1)}, bf16[256,2048]{0,1:T(8,128)(2,1)}, u32[]{:S(2)}, u32[]{:S(2)}) collective-permute-start(bf16[256,2048]{0,1:T(8,128)(2,1)} %copy.92), channel_id=1, source_target_pairs={{0,512},{512,0},{1,513},{513,1},{2,514},{514,2},{3,515},{515,3},{4... | collective-permute-start | bytes 3145736 | tf_op jit(solution)/shard_map/ppermute | solution.py:94
  101.4 4.0 %copy-start.4 = (f32[4]{0:T(128)S(1)}, f32[4]{0:T(128)}, u32[]{:S(2)}) copy-start(f32[4]{0:T(128)} %param.17) | copy-start | bytes 52
  102.3 14.0 %collective-permute-start.10 = (bf16[256,896]{0,1:T(8,128)(2,1)S(1)}, bf16[256,896]{0,1:T(8,128)(2,1)S(1)}, u32[]{:S(2)}, u32[]{:S(2)}) collective-permute-start(bf16[256,896]{0,1:T(8,128)(2,1)S(1)} %fusion.3), channel_id=1, source_target_pairs={{0,512},{512,0},{1,513},{513,1},{2,514},{514,2},{3,515},{515,3},{4... | collective-permute-start | bytes 1376264 | tf_op jit(solution)/shard_map/ppermute | solution.py:132
  116.2 0.9 copy-start.3
  117.2 2.9 %copy-start.5 = (f32[4]{0:T(128)S(1)}, f32[4]{0:T(128)}, u32[]{:S(2)}) copy-start(f32[4]{0:T(128)} %param.19) | copy-start | bytes 52
  122.3 34.6 %all-to-all-start.1 = ((bf16[8,256,256]{2,1,0:T(8,128)(2,1)}), bf16[8,256,256]{2,1,0:T(8,128)(2,1)S(1)}, u32[]{:S(2)}, u32[]{:S(2)}) async-start(bf16[8,256,256]{2,1,0:T(8,128)(2,1)} %broadcast_in_dim.78), calls=%async_computation.1 | async-start | bytes 2097152 | tf_op jit(solution)/shard_map/all_to_all | solution.py:160

commit v3 on v2

--- a/solution.py
+++ b/solution.py
@@ -86,51 +86,22 @@
         ],
         axis=1,
     )
-    k_half, z_pos, c_pos = lax.axis_index("yl"), lax.axis_index("z"), lax.axis_index("core")
-    n_z = lax.axis_size("z")
+    k_half = lax.axis_index("yl")
     k_rows = tokens.shape[1] // 2
     kept = lax.dynamic_slice_in_dim(tokens, k_half * k_rows, k_rows, 1)
     given = lax.dynamic_slice_in_dim(tokens, (1 - k_half) * k_rows, k_rows, 1)
     given = lax.ppermute(given, "yl", SWAP)
 
-    up = [(i, (i + 1) % n_z) for i in range(n_z)]
-    down = [(i, (i - 1) % n_z) for i in range(n_z)]
-    own = jnp.zeros((n_z,) + mine.shape, bf16)
-
-    def place(total, block, offset, row=0):
-        return lax.dynamic_update_slice(total, block[None], ((z_pos + offset) % n_z, row, 0))
-
-    own = place(own, mine, 0)
-    above = below = mine
-    for i in range(1, n_z // 2):
-        below = lax.ppermute(below, "z", up)
-        above = lax.ppermute(above, "z", down)
-        own = place(place(own, below, -i), above, i)
-    below = lax.ppermute(below[: rows // 2], "z", up)
-    above = lax.ppermute(above[rows // 2 :], "z", down)
-    own = place(place(own, below, n_z // 2), above, n_z // 2, rows // 2)
-    theirs = lax.ppermute(own, "core", SWAP)
+    whole = lax.all_gather(mine, ("z", "core"), axis=0, tiled=True)
 
     width = out_weight.shape[1] // (n_yh * n_x)
     pieces = repack(out_weight, norm_gain, n_yh, n_x)
     group_weight = lax.all_to_all(pieces, "x", 0, 0)
     group_weight = group_weight.reshape(n_x * channels, n_yh * width)
 
-    def by_core(values):
-        split = values.reshape(tok_rows, n_z, 2, rows)
-        first = split[:, :, 0].reshape(tok_rows, n_z * rows)
-        second = split[:, :, 1].reshape(tok_rows, n_z * rows)
-        return jnp.where(c_pos == 0, first, second), jnp.where(c_pos == 0, second, first)
-
-    def product(pair):
-        return sum(
-            jnp.dot(left, right.reshape(n_z * rows, -1), preferred_element_type=f32)
-            for left, right in zip(pair, (own, theirs))
-        )
-
-    kept, given = by_core(kept), by_core(given)
-    away = lax.ppermute(product(given).astype(bf16), "yl", SWAP)
-    acc = product(kept)
+    away = jnp.dot(given, whole, preferred_element_type=f32)
+    away = lax.ppermute(away.astype(bf16), "yl", SWAP)
+    acc = jnp.dot(kept, whole, preferred_element_type=f32)
     acc = acc + away.astype(f32)
     acc, group_weight = lax.optimization_barrier((acc, group_weight))
     zx = acc[:, :zx_cols].reshape(tok_rows, heads_here, 2, head_size)

time: 179 us -> 161 us (0.90)
  the two profiles are of different devices: /device:TPU:16 before, /device:TPU:1 now
where the time goes in v3:
time: 161 us; the launch traced here: 160 us
  waiting for transfers between devices  74 us (46%)
  starting transfers between devices  20.3 us (13%)
  blocking collectives  15.5 us (10%)
  local copies, waits for them, and re-layouts  13.6 us (8%)
  between operations  13.6 us (8%)
  matrix products  9.98 us (6%)
  other arithmetic  6.5 us (4%)
  Pallas kernels  6.42 us (4%)
    all_gather x1, waiting for transfers between devices, layer(): whole = lax.all_gather(mine, ('z', 'core'), axis=0, tiled=True)  29.7 us
    all_to_all x1, waiting for transfers between devices, layer(): group = lax.all_to_all(spread, 'x', 0, 0)  25.2 us
    all_to_all x1, blocking collectives, layer(): got = lax.all_to_all(parts, 'yh', 0, 0)  15.5 us
    ppermute x1, waiting for transfers between devices, layer(): given = lax.ppermute(given, 'yl', SWAP)  11.7 us
    ppermute x1, waiting for transfers between devices, layer(): away = lax.ppermute(away.astype(bf16), 'yl', SWAP)  7.4 us
    all_to_all x1, starting transfers between devices, layer(): group_weight = lax.all_to_all(pieces, 'x', 0, 0)  7.3 us
    all_to_all x1, starting transfers between devices, layer(): group = lax.all_to_all(spread, 'x', 0, 0)  6.5 us
    pallas_call x1, Pallas kernels, repack(): pl.pallas_call(kernel, grid=(n_x,), in_specs=[pl.BlockSpec((rows, 1), lam...  6.42 us
  transfers between devices with their start and end apart: 5, of which 4 were waited for; matrix products, arithmetic and copies ran while one was open for 9% of the time, Pallas kernels for 4%

profile of v3, /device:TPU:1, one launch (start us, length us, event | category | flops | bytes accessed | tf_op | source)
XLA Modules:
  0.0 159.8 jit_solution(13838968713605120189)
XLA Ops:
  6.5 1.1 copy.79
  7.6 0.8 copy.52
  8.4 0.8 constant_dynamic-slice_fusion.2
  10.1 1.5 copy.55.gain_ref
  11.6 6.4 %repack.1 = bf16[8,256,512]{2,1,0:T(8,128)(2,1)} custom-call(f32[256,1]{1,0:T(8,128)} %copy.55.gain_ref, bf16[256,4096]{1,0:T(8,128)(2,1)} %refs_3_.1, bf16[256,4096]{1,0:T(8,128)(2,1)} %refs_3_.1, bf16[256,4096]{1,0:T(8,128)(2,1)} %refs_3_.1, bf16[256,4096]{1,0:T(8,128)(2,1)} %refs_3_.1), custom_call_target="tpu_custom_call" | custom-call | flops 1048576 | bytes 4194304 | tf_op jit(solution)/shard_map/repack/pallas_call | solution.py:27
  18.0 7.3 %all-to-all-start = ((bf16[8,256,512]{2,1,0:T(8,128)(2,1)}), bf16[8,256,512]{2,1,0:T(8,128)(2,1)}, u32[]{:S(2)}, u32[]{:S(2)}) async-start(bf16[8,256,512]{2,1,0:T(8,128)(2,1)} %repack.1), calls=%async_computation | async-start | bytes 4194304 | tf_op jit(solution)/shard_map/all_to_all | solution.py:99
  25.5 3.3 %collective-permute-start = (bf16[256,2048]{1,0:T(8,128)(2,1)S(1)}, bf16[256,2048]{1,0:T(8,128)(2,1)}, u32[]{:S(2)}, u32[]{:S(2)}) collective-permute-start(bf16[256,2048]{1,0:T(8,128)(2,1)S(1)} %constant_dynamic-slice_fusion.1), channel_id=1, source_target_pairs={{0,512},{512,0},{1,513},{513,1},{2,514},{514,2},{3,515},{515,3},{4... | collective-permute-start | bytes 3145736 | tf_op jit(solution)/shard_map/ppermute | solution.py:93
  30.1 11.7 %collective-permute-done = bf16[256,2048]{1,0:T(8,128)(2,1)} collective-permute-done((bf16[256,2048]{1,0:T(8,128)(2,1)S(1)}, bf16[256,2048]{1,0:T(8,128)(2,1)}, u32[]{:S(2)}, u32[]{:S(2)}) %collective-permute-start) | collective-permute-done | bytes 1048608 | tf_op jit(solution)/shard_map/ppermute | solution.py:93
  41.8 29.7 %all-gather.2.cloned.1.call-done = bf16[2048,896]{1,0:T(8,128)(2,1)} async-done(((bf16[128,896]{1,0:T(8,128)(2,1)}), bf16[2048,896]{1,0:T(8,128)(2,1)}) %all-gather.2.cloned.1.call-update) | async-done | bytes 3670032 | tf_op jit(solution)/shard_map/all_gather | solution.py:95
  71.4 4.0 %convolution_convert_fusion = bf16[256,896]{0,1:T(8,128)(2,1)S(1)} fusion(bf16[256,2048]{1,0:T(8,128)(2,1)} %collective-permute-done, bf16[2048,896]{1,0:T(8,128)(2,1)} %all-gather.2.cloned.1.call-done), kind=kOutput, calls=%fused_computation.3 | convolution fusion | flops 939753472 | bytes 5177344 | tf_op jit(solution)/shard_map/dot_general | solution.py:102
  75.5 3.1 %collective-permute-start.1 = (bf16[256,896]{0,1:T(8,128)(2,1)S(1)}, bf16[256,896]{0,1:T(8,128)(2,1)S(1)}, u32[]{:S(2)}, u32[]{:S(2)}) collective-permute-start(bf16[256,896]{0,1:T(8,128)(2,1)S(1)} %convolution_convert_fusion), channel_id=1, source_target_pairs={{0,512},{512,0},{1,513},{513,1},{2,514},{514,2},{3,515},{515,3},{4... | collective-permute-start | bytes 1376264 | tf_op jit(solution)/shard_map/ppermute | solution.py:103
  78.6 1.5 constant_dynamic-slice_fusion
  80.2 1.6 fusion.21
  81.8 7.4 %collective-permute-done.1 = bf16[256,896]{0,1:T(8,128)(2,1)S(1)} collective-permute-done((bf16[256,896]{0,1:T(8,128)(2,1)S(1)}, bf16[256,896]{0,1:T(8,128)(2,1)S(1)}, u32[]{:S(2)}, u32[]{:S(2)}) %collective-permute-start.1) | collective-permute-done | bytes 458784 | tf_op jit(solution)/shard_map/ppermute | solution.py:103
  90.7 1.2 reduce-window.6
  92.0 1.5 fusion.47
  94.2 1.1 fusion.46
  95.3 1.8 %fusion.11 = f32[1,256,4,64]{1,3,2,0:T(8,128)S(1)} fusion(bf16[256,4,64]{0,2,1:T(8,128)(2,1)S(1)} %bitcast.88, f32[256,4]{0,1:T(4,128)} %get-tuple-element.10, f32[256,4]{0,1:T(4,128)S(1)} %add_bitcast_fusion, f32[256,256]{1,0:T(8,128)S(1)} %fusion.48, pred[256,256]{1,0:T(8,128)(4,1)} %iota_compare_fusion, bf16[1,256,4,64]{1,3,2,0:T(8,128)(2,1)S(1)} %bitcast.89, ...), kind=kOutput, calls=%fused_computation.8 | convolution fusion | flops 202571776 | bytes 860176 | tf_op jit(solution)/shard_map/btsh,bshp->bthp/dot_general | solution.py:126
  97.3 1.1 broadcast_in_dim.22
  98.4 6.5 %all-to-all-start.1 = ((bf16[8,256,256]{2,1,0:T(8,128)(2,1)}), bf16[8,256,256]{2,1,0:T(8,128)(2,1)S(1)}, u32[]{:S(2)}, u32[]{:S(2)}) async-start(bf16[8,256,256]{2,1,0:T(8,128)(2,1)} %broadcast_in_dim.22), calls=%async_computation.1 | async-start | bytes 2097152 | tf_op jit(solution)/shard_map/all_to_all | solution.py:131
  104.9 4.0 %reshape.233 = bf16[8,256,4,128]{3,2,1,0:T(4,128)(2,1)} reshape(bf16[2048,512]{1,0:T(8,128)(2,1)} %bitcast.1) | data formatting | bytes 4194304 | tf_op jit(solution)/shard_map/reshape | solution.py:137
  108.8 25.2 %all-to-all-done.1 = bf16[8,256,256]{2,1,0:T(8,128)(2,1)S(1)} async-done(((bf16[8,256,256]{2,1,0:T(8,128)(2,1)}), bf16[8,256,256]{2,1,0:T(8,128)(2,1)S(1)}, u32[]{:S(2)}, u32[]{:S(2)}) %all-to-all-start.1) | async-done | bytes 1048608 | tf_op jit(solution)/shard_map/all_to_all | solution.py:131
  134.4 2.4 %fusion.12 = bf16[4,256,128]{1,2,0:T(8,128)(2,1)S(1)} fusion(bf16[8,256,4,128]{3,2,1,0:T(4,128)(2,1)} %reshape.233, bf16[8,256,256]{2,1,0:T(8,128)(2,1)S(1)} %all-to-all-done.1, f32[256]{0:T(256)S(1)} %add_rsqrt_fusion), kind=kOutput, calls=%fused_computation.9 | convolution fusion | flops 537133056 | bytes 3408896 | tf_op jit(solution)/shard_map/xtc,xcyw->ytw/dot_general | solution.py:134
  136.7 15.5 %all_to_all.15 = bf16[4,256,128]{1,2,0:T(8,128)(2,1)S(1)} all-to-all(bf16[4,256,128]{1,2,0:T(8,128)(2,1)S(1)} %fusion.12), channel_id=1, replica_groups=mesh['yl'=2,'z'=8,'core'=2,'yh'=4,'x'=8] {'yh'}, dimensions={0} | all-to-all | bytes 524288 | tf_op jit(solution)/shard_map/all_to_all | solution.py:141
  (42 shorter events, 5.7 us)
Async XLA Ops:
  6.5 18.8 %copy-start = (bf16[256,4096]{1,0:T(8,128)(2,1)S(1)}, bf16[256,4096]{1,0:T(8,128)(2,1)}, u32[]{:S(2)}) copy-start(bf16[256,4096]{1,0:T(8,128)(2,1)} %param.11) | copy-start | bytes 6291460
  6.5 64.9 %all-gather.2.cloned.1.call-start = ((), (), s32[]{:S(2)}) async-start(), calls=%async_computation.3 | async-start | bytes 3899392 | tf_op jit(solution)/shard_map/all_gather | solution.py:95
  18.0 71.2 %all-to-all-start = ((bf16[8,256,512]{2,1,0:T(8,128)(2,1)}), bf16[8,256,512]{2,1,0:T(8,128)(2,1)}, u32[]{:S(2)}, u32[]{:S(2)}) async-start(bf16[8,256,512]{2,1,0:T(8,128)(2,1)} %repack.1), calls=%async_computation | async-start | bytes 4194304 | tf_op jit(solution)/shard_map/all_to_all | solution.py:99
  25.3 3.4 %copy-start.4 = (f32[4]{0:T(128)S(1)}, f32[4]{0:T(128)}, u32[]{:S(2)}) copy-start(f32[4]{0:T(128)} %param.17) | copy-start | bytes 52
  25.4 4.1 %copy-start.1 = (f32[4,256]{1,0:T(4,128)S(1)}, f32[4,256]{1,0:T(4,128)}, u32[]{:S(2)}) copy-start(f32[4,256]{1,0:T(4,128)} %param.15) | copy-start | bytes 12292
  25.5 16.3 %collective-permute-start = (bf16[256,2048]{1,0:T(8,128)(2,1)S(1)}, bf16[256,2048]{1,0:T(8,128)(2,1)}, u32[]{:S(2)}, u32[]{:S(2)}) collective-permute-start(bf16[256,2048]{1,0:T(8,128)(2,1)S(1)} %constant_dynamic-slice_fusion.1), channel_id=1, source_target_pairs={{0,512},{512,0},{1,513},{513,1},{2,514},{514,2},{3,515},{515,3},{4... | collective-permute-start | bytes 3145736 | tf_op jit(solution)/shard_map/ppermute | solution.py:93
  71.4 8.7 %copy-start.3 = (bf16[2048,896]{1,0:T(8,128)(2,1)S(1)}, bf16[2048,896]{1,0:T(8,128)(2,1)}, u32[]{:S(2)}) copy-start(bf16[2048,896]{1,0:T(8,128)(2,1)} %all-gather.2.cloned.1.call-done) | copy-start | bytes 11010052
  75.5 13.7 %collective-permute-start.1 = (bf16[256,896]{0,1:T(8,128)(2,1)S(1)}, bf16[256,896]{0,1:T(8,128)(2,1)S(1)}, u32[]{:S(2)}, u32[]{:S(2)}) collective-permute-start(bf16[256,896]{0,1:T(8,128)(2,1)S(1)} %convolution_convert_fusion), channel_id=1, source_target_pairs={{0,512},{512,0},{1,513},{513,1},{2,514},{514,2},{3,515},{515,3},{4... | collective-permute-start | bytes 1376264 | tf_op jit(solution)/shard_map/ppermute | solution.py:103
  81.8 8.2 %copy-start.2 = (f32[4]{0:T(128)S(1)}, f32[4]{0:T(128)}, u32[]{:S(2)}) copy-start(f32[4]{0:T(128)} %param.18) | copy-start | bytes 52
  98.4 35.7 %all-to-all-start.1 = ((bf16[8,256,256]{2,1,0:T(8,128)(2,1)}), bf16[8,256,256]{2,1,0:T(8,128)(2,1)S(1)}, u32[]{:S(2)}, u32[]{:S(2)}) async-start(bf16[8,256,256]{2,1,0:T(8,128)(2,1)} %broadcast_in_dim.22), calls=%async_computation.1 | async-start | bytes 2097152 | tf_op jit(solution)/shard_map/all_to_all | solution.py:131
Sparse Core Ops, SparseCore 0:
  10.3 61.1 all-gather.1

commit v4 on v3

v4 whole, which is shorter than its diff:
```python
import jax
import jax.numpy as jnp
from jax import lax
from jax.experimental import pallas as pl
from jax.experimental.pallas import tpu as pltpu
from jax.sharding import Mesh, PartitionSpec as P

FSDP = ("yl", "z", "core")
HEAD = ("yh", "x")
SIZES = (2, 8, 2, 4, 8)
SWAP = [(0, 1), (1, 0)]


def repack(weight, gain, n_yh, n_x):
    rows, columns = weight.shape
    width = columns // (n_yh * n_x)

    step = rows // 8

    def kernel(gain_ref, weight_ref, out_ref):
        gains = gain_ref[...]
        for x in range(n_x):
            for y in range(n_yh):
                start = (y * n_x + x) * width
                value = weight_ref[:, start : start + width].astype(jnp.float32) * gains
                out_ref[x, :, y * width : (y + 1) * width] = value.astype(jnp.bfloat16)

    return pl.pallas_call(
        kernel,
        grid=(rows // step,),
        in_specs=[
            pl.BlockSpec((step, 1), lambda i: (i, 0)),
            pl.BlockSpec((step, columns), lambda i: (i, 0)),
        ],
        out_specs=pl.BlockSpec((n_x, step, n_yh * width), lambda i: (0, i, 0)),
        out_shape=jax.ShapeDtypeStruct((n_x, rows, n_yh * width), jnp.bfloat16),
        cost_estimate=pl.CostEstimate(
            flops=rows * columns, bytes_accessed=4 * rows * columns, transcendentals=0
        ),
        name="repack",
    )(gain[:, None], weight)


def silu(values):
    return values * jax.nn.sigmoid(values)


def causal(values, taps_ref, columns):
    rows = lax.broadcasted_iota(jnp.int32, values.shape, 0)
    n_taps = taps_ref.shape[0]
    total = taps_ref[n_taps - 1 : n_taps, columns] * values
    for back in range(1, n_taps):
        moved = jnp.where(rows >= back, pltpu.roll(values, back, 0), 0.0)
        total = total + taps_ref[n_taps - 1 - back : n_taps - back, columns] * moved
    return silu(total).astype(jnp.bfloat16)


def mixing_kernel(own_ref, away_ref, taps_ref, rate_ref, bias_ref, out_ref):
    f32 = jnp.float32
    heads, length, _ = out_ref.shape
    state = taps_ref.shape[1] // 2
    both = own_ref[...] + away_ref[...].astype(f32)
    keys = causal(both[:, :state], taps_ref, slice(0, state))
    queries = causal(both[:, state : 2 * state], taps_ref, slice(state, 2 * state))
    inner = lax.dot_general(queries, keys, (((1,), (1,)), ((), ())), preferred_element_type=f32)
    steps = jax.nn.softplus(both[:, 2 * state :] + bias_ref[...])
    rates = -steps * jnp.exp(rate_ref[...])
    shape = (length, length)
    lower = lax.broadcasted_iota(jnp.int32, shape, 0) >= lax.broadcasted_iota(jnp.int32, shape, 1)
    cum = jnp.dot(
        jnp.where(lower, 1.0, 0.0),
        rates,
        precision=lax.Precision.HIGHEST,
        preferred_element_type=f32,
    )
    cum_t, steps_t = cum.T, steps.T
    for h in range(heads):
        seg = cum[:, h : h + 1] - cum_t[h : h + 1, :]
        decay = jnp.exp(jnp.where(lower, seg, -1e30))
        out_ref[h] = (inner * decay * steps_t[h : h + 1, :]).astype(jnp.bfloat16)


def gated_kernel(own_ref, away_ref, taps_ref, skip_ref, mix_ref, out_ref):
    f32 = jnp.float32
    heads = mix_ref.shape[0]
    length = own_ref.shape[0]
    wide = own_ref.shape[1] // heads
    half = wide // 2
    first = lax.broadcasted_iota(jnp.int32, (length, wide), 1) < half
    kept = None
    for h in range(heads):
        columns = slice(h * wide, (h + 1) * wide)
        both = own_ref[:, columns] + away_ref[:, columns].astype(f32)
        conv = causal(both, taps_ref, columns)
        out = jnp.dot(mix_ref[h], conv, preferred_element_type=f32)
        out = out + skip_ref[:, columns] * conv.astype(f32)
        out = out * pltpu.roll(silu(both), half, 1)
        if h % 2 == 0:
            kept = pltpu.roll(out, half, 1)
        else:
            pair = jnp.where(first, kept, out).astype(jnp.bfloat16)
            for copy in range(out_ref.shape[0]):
                out_ref[copy, :, (h // 2) * wide : (h // 2 + 1) * wide] = pair


def on_chip(kernel, out_shape, flops, *args):
    moved = sum(a.size * a.dtype.itemsize for a in args) + 2 * out_shape.size
    return pl.pallas_call(
        kernel,
        out_shape=out_shape,
        cost_estimate=pl.CostEstimate(flops=flops, bytes_accessed=moved, transcendentals=0),
    )(*args)


def layer(
    tokens,
    zx_weight,
    dt_weight,
    bc_weight,
    conv_x,
    conv_bc,
    a_log,
    dt_bias,
    d_skip,
    norm_gain,
    out_weight,
):
    f32, bf16 = jnp.float32, jnp.bfloat16
    tok_rows = tokens.shape[0]
    rows, heads_here, two_p = zx_weight.shape
    head_size = two_p // 2
    channels = heads_here * head_size
    n_yh, n_x = lax.axis_size("yh"), lax.axis_size("x")
    group_id = lax.axis_index("yh")
    group_cols = bc_weight.shape[1] // n_yh
    bc_part = lax.dynamic_slice_in_dim(bc_weight, group_id * group_cols, group_cols, 1)
    zx_cols = heads_here * two_p
    pad = -(zx_cols + group_cols + heads_here) % 128
    mine = jnp.concatenate(
        [
            zx_weight.reshape(rows, zx_cols),
            bc_part,
            dt_weight,
            jnp.zeros((rows, pad), bf16),
        ],
        axis=1,
    )
    k_half = lax.axis_index("yl")
    k_rows = tokens.shape[1] // 2
    kept = lax.dynamic_slice_in_dim(tokens, k_half * k_rows, k_rows, 1)
    given = lax.dynamic_slice_in_dim(tokens, (1 - k_half) * k_rows, k_rows, 1)
    given = lax.ppermute(given, "yl", SWAP)

    whole = lax.all_gather(mine, ("z", "core"), axis=0, tiled=True)

    width = out_weight.shape[1] // (n_yh * n_x)
    pieces = repack(out_weight, norm_gain, n_yh, n_x)
    group_weight = lax.all_to_all(pieces, "x", 0, 0)
    group_weight = group_weight.reshape(n_x * channels, n_yh * width)

    def padded(values):
        return jnp.pad(values, (0, 128 - heads_here))[None]

    conv_group = lax.dynamic_slice_in_dim(conv_bc, group_id * group_cols, group_cols, 1)
    taps = conv_x.shape[0]
    x_taps = conv_x.reshape(taps, heads_here, head_size)
    x_taps = jnp.concatenate([jnp.zeros_like(x_taps), x_taps], axis=2).reshape(taps, zx_cols)
    skips = jnp.repeat(d_skip, two_p)[None]
    rate, bias = padded(a_log), padded(dt_bias)

    def product(left, columns):
        return jnp.dot(left, whole[:, columns], preferred_element_type=f32)

    small, large = slice(zx_cols, None), slice(0, zx_cols)
    small_away = lax.ppermute(product(given, small).astype(bf16), "yl", SWAP)
    large_away = lax.ppermute(product(given, large).astype(bf16), "yl", SWAP)
    small_own, large_own = product(kept, small), product(kept, large)
    mix = on_chip(
        mixing_kernel,
        jax.ShapeDtypeStruct((heads_here, tok_rows, tok_rows), bf16),
        10 * heads_here * tok_rows * tok_rows,
        small_own,
        small_away,
        conv_group,
        rate,
        bias,
    )
    mix, group_weight = lax.optimization_barrier((mix, group_weight))
    spread = on_chip(
        gated_kernel,
        jax.ShapeDtypeStruct((n_x, tok_rows, channels), bf16),
        4 * tok_rows * tok_rows * channels,
        large_own,
        large_away,
        x_taps,
        skips,
        mix,
    )
    group = lax.all_to_all(spread, "x", 0, 0)
    squares = jnp.sum(jnp.square(group.astype(f32)), axis=(0, 2))
    scale = lax.rsqrt(squares / (n_x * channels) + 1e-05)
    parts = jnp.einsum(
        "xtc,xcyw->ytw",
        group,
        group_weight.reshape(n_x, channels, n_yh, width),
        preferred_element_type=f32,
    )
    parts = (parts * scale[None, :, None]).astype(bf16)
    got = lax.all_to_all(parts, "yh", 0, 0)
    return jnp.sum(got.astype(f32), axis=0).astype(bf16)


def solution(mesh):
    fine = Mesh(mesh.devices.reshape(SIZES), FSDP + HEAD)
    in_specs = (
        P(FSDP, None),
        P(FSDP, HEAD, None),
        P(FSDP, HEAD),
        P(FSDP, None),
        P(None, HEAD),
        P(),
        P(HEAD),
        P(HEAD),
        P(HEAD),
        P(HEAD),
        P(HEAD, None),
    )
    return jax.shard_map(
        layer, mesh=fine, in_specs=in_specs, out_specs=P(FSDP, HEAD), check_vma=False
    )
```

time: 161 us -> 154 us (0.957)
  the two profiles are of different devices: /device:TPU:1 before, /device:TPU:16 now
where the time goes in v4:
time: 154 us; the launch traced here: 153 us
  waiting for transfers between devices  54.8 us (36%)
  starting transfers between devices  31.8 us (21%)
  blocking collectives  17.1 us (11%)
  between operations  13.5 us (9%)
  local copies, waits for them, and re-layouts  13.1 us (9%)
  Pallas kernels  11.9 us (8%)
  matrix products  9.9 us (6%)
    all_to_all x1, waiting for transfers between devices, layer(): group = lax.all_to_all(spread, 'x', 0, 0)  24.5 us
    all_gather x1, waiting for transfers between devices, layer(): whole = lax.all_gather(mine, ('z', 'core'), axis=0, tiled=True)  18.8 us
    all_to_all x1, blocking collectives, layer(): got = lax.all_to_all(parts, 'yh', 0, 0)  17.1 us
    ppermute x1, starting transfers between devices, layer(): given = lax.ppermute(given, 'yl', SWAP)  12.5 us
    ppermute x1, waiting for transfers between devices, layer(): given = lax.ppermute(given, 'yl', SWAP)  11.5 us
    dot_general x4, matrix products, product(): return jnp.dot(left, whole[:, columns], preferred_element_type=f32)  7.55 us
    all_to_all x1, starting transfers between devices, layer(): group_weight = lax.all_to_all(pieces, 'x', 0, 0)  6.76 us
    all_to_all x1, starting transfers between devices, layer(): group = lax.all_to_all(spread, 'x', 0, 0)  6.7 us
  transfers between devices with their start and end apart: 6, of which 4 were waited for; matrix products, arithmetic and copies ran while one was open for 10% of the time, Pallas kernels for 6%

profile of v4, /device:TPU:16, one launch (start us, length us, event | category | flops | bytes accessed | tf_op | source)
XLA Modules:
  0.0 153.3 jit_solution(4881890978299570149)
XLA Ops:
  6.5 1.0 copy.17
  7.5 0.9 copy.39
  8.5 0.8 constant_dynamic-slice_fusion.2
  9.4 0.7 maximum_maximum_fusion
  10.1 1.5 copy.18.gain_ref
  11.6 6.1 %repack.1 = bf16[8,256,512]{2,1,0:T(8,128)(2,1)} custom-call(f32[256,1]{1,0:T(8,128)} %copy.18.gain_ref, bf16[256,4096]{1,0:T(8,128)(2,1)} %weight_ref.1), custom_call_target="tpu_custom_call" | custom-call | flops 1048576 | bytes 4194304 | tf_op jit(solution)/shard_map/repack/pallas_call | solution.py:28
  17.7 6.8 %all-to-all-start = ((bf16[8,256,512]{2,1,0:T(8,128)(2,1)}), bf16[8,256,512]{2,1,0:T(8,128)(2,1)}, u32[]{:S(2)}, u32[]{:S(2)}) async-start(bf16[8,256,512]{2,1,0:T(8,128)(2,1)} %repack.1), calls=%async_computation | async-start | bytes 4194304 | tf_op jit(solution)/shard_map/all_to_all | solution.py:158
  24.6 12.5 %collective-permute-start = (bf16[256,2048]{1,0:T(8,128)(2,1)S(1)}, bf16[256,2048]{1,0:T(8,128)(2,1)}, u32[]{:S(2)}, u32[]{:S(2)}) collective-permute-start(bf16[256,2048]{1,0:T(8,128)(2,1)S(1)} %constant_dynamic-slice_fusion.1), channel_id=1, source_target_pairs={{0,512},{512,0},{1,513},{513,1},{2,514},{514,2},{3,515},{515,3},{4... | collective-permute-start | bytes 3145736 | tf_op jit(solution)/shard_map/ppermute | solution.py:152
  38.5 1.3 constant_dynamic-slice_fusion.taps_ref
  39.8 11.5 %collective-permute-done = bf16[256,2048]{1,0:T(8,128)(2,1)} collective-permute-done((bf16[256,2048]{1,0:T(8,128)(2,1)S(1)}, bf16[256,2048]{1,0:T(8,128)(2,1)}, u32[]{:S(2)}, u32[]{:S(2)}) %collective-permute-start) | collective-permute-done | bytes 1048608 | tf_op jit(solution)/shard_map/ppermute | solution.py:152
  51.3 18.8 %all-gather.2.cloned.1.call-done = bf16[2048,896]{1,0:T(8,128)(2,1)} async-done(((bf16[128,896]{1,0:T(8,128)(2,1)}), bf16[2048,896]{1,0:T(8,128)(2,1)}) %all-gather.2.cloned.1.call-update) | async-done | bytes 3670032 | tf_op jit(solution)/shard_map/all_gather | solution.py:154
  70.0 2.6 %fusion.22 = bf16[256,384]{1,0:T(8,128)(2,1)S(1)} fusion(bf16[256,2048]{1,0:T(8,128)(2,1)} %collective-permute-done, bf16[2048,896]{1,0:T(8,128)(2,1)} %all-gather.2.cloned.1.call-done), kind=kOutput, calls=%fused_computation.15 | convolution fusion | flops 402751488 | bytes 2818048 | tf_op jit(solution)/shard_map/dot_general | solution.py:172
  72.6 2.5 %collective-permute-start.1 = (bf16[256,384]{1,0:T(8,128)(2,1)S(1)}, bf16[256,384]{1,0:T(8,128)(2,1)S(1)}, u32[]{:S(2)}, u32[]{:S(2)}) collective-permute-start(bf16[256,384]{1,0:T(8,128)(2,1)S(1)} %fusion.22), channel_id=1, source_target_pairs={{0,512},{512,0},{1,513},{513,1},{2,514},{514,2},{3,515},{515,3},{4... | collective-permute-start | bytes 589832 | tf_op jit(solution)/shard_map/ppermute | solution.py:175
  75.1 2.0 %fusion.19 = bf16[256,512]{1,0:T(8,128)(2,1)S(1)} fusion(bf16[256,2048]{1,0:T(8,128)(2,1)} %collective-permute-done, bf16[2048,896]{1,0:T(8,128)(2,1)S(1)} %copy-done.7), kind=kOutput, calls=%fused_computation.14 | convolution fusion | flops 537001984 | bytes 3407872 | tf_op jit(solution)/shard_map/dot_general | solution.py:172
  77.1 3.4 %collective-permute-start.2 = (bf16[256,512]{1,0:T(8,128)(2,1)S(1)}, bf16[256,512]{1,0:T(8,128)(2,1)S(1)}, u32[]{:S(2)}, u32[]{:S(2)}) collective-permute-start(bf16[256,512]{1,0:T(8,128)(2,1)S(1)} %fusion.19), channel_id=1, source_target_pairs={{0,512},{512,0},{1,513},{513,1},{2,514},{514,2},{3,515},{515,3},{4... | collective-permute-start | bytes 786440 | tf_op jit(solution)/shard_map/ppermute | solution.py:176
  80.4 1.6 %fusion.4.own_ref = f32[256,512]{1,0:T(8,128)} fusion(bf16[2048,896]{1,0:T(8,128)(2,1)S(1)} %copy-done.7, bf16[256,4096]{1,0:T(8,128)(2,1)S(1)} %copy-done, s32[]{:T(128)S(6)} %select_n.10), kind=kOutput, calls=%fused_computation.5 | convolution fusion | flops 536870912 | bytes 3670020 | tf_op jit(solution)/shard_map/dot_general | solution.py:172
  82.0 1.5 fusion.8.own_ref
  84.1 2.9 %shard_map.109.mix_ref = bf16[4,256,256]{2,1,0:T(8,128)(2,1)} custom-call(f32[256,384]{1,0:T(8,128)} %fusion.8.own_ref, bf16[256,384]{1,0:T(8,128)(2,1)} %copy-done.2, f32[4,256]{1,0:T(4,128)} %constant_dynamic-slice_fusion.taps_ref, f32[1,128]{1,0:T(1,128)} %get-tuple-element.10.rate_ref, f32[1,128]{1,0:T(1,128)} %get-tuple-element.9.bias_ref), custom_call_target="tpu_custom_call" | custom-call | flops 2621440 | bytes 1119232 | tf_op jit(solution)/shard_map/pallas_call | solution.py:108
  87.9 2.9 %shard_map.110 = bf16[8,256,256]{2,1,0:T(8,128)(2,1)} custom-call(f32[256,512]{1,0:T(8,128)} %fusion.4.own_ref, bf16[256,512]{1,0:T(8,128)(2,1)} %copy-done.1, f32[4,512]{1,0:T(4,128)} %bitcast.34, f32[1,512]{1,0:T(1,128)} %bitcast.35, bf16[4,256,256]{2,1,0:T(8,128)(2,1)} %shard_map.109.mix_ref), custom_call_target="tpu_custom_call" | custom-call | flops 67108864 | bytes 2369536 | tf_op jit(solution)/shard_map/pallas_call | solution.py:108
  90.8 6.7 %all-to-all-start.1 = ((bf16[8,256,256]{2,1,0:T(8,128)(2,1)}), bf16[8,256,256]{2,1,0:T(8,128)(2,1)S(1)}, u32[]{:S(2)}, u32[]{:S(2)}) async-start(bf16[8,256,256]{2,1,0:T(8,128)(2,1)} %shard_map.110), calls=%async_computation.1 | async-start | bytes 2097152 | tf_op jit(solution)/shard_map/all_to_all | solution.py:199
  97.5 4.0 %reshape.27 = bf16[8,256,4,128]{3,2,1,0:T(4,128)(2,1)} reshape(bf16[2048,512]{1,0:T(8,128)(2,1)} %bitcast.3) | data formatting | bytes 4194304 | tf_op jit(solution)/shard_map/reshape | solution.py:205
  101.4 24.5 %all-to-all-done.1 = bf16[8,256,256]{2,1,0:T(8,128)(2,1)S(1)} async-done(((bf16[8,256,256]{2,1,0:T(8,128)(2,1)}), bf16[8,256,256]{2,1,0:T(8,128)(2,1)S(1)}, u32[]{:S(2)}, u32[]{:S(2)}) %all-to-all-start.1) | async-done | bytes 1048608 | tf_op jit(solution)/shard_map/all_to_all | solution.py:199
  126.2 2.4 %fusion.25 = bf16[4,256,128]{1,2,0:T(8,128)(2,1)S(1)} fusion(bf16[8,256,4,128]{3,2,1,0:T(4,128)(2,1)} %reshape.27, bf16[8,256,256]{2,1,0:T(8,128)(2,1)S(1)} %all-to-all-done.1, f32[256]{0:T(256)S(1)} %add_rsqrt_fusion), kind=kOutput, calls=%fused_computation.16 | convolution fusion | flops 537133056 | bytes 3408896 | tf_op jit(solution)/shard_map/xtc,xcyw->ytw/dot_general | solution.py:202
  128.6 17.1 %all_to_all.15 = bf16[4,256,128]{1,2,0:T(8,128)(2,1)S(1)} all-to-all(bf16[4,256,128]{1,2,0:T(8,128)(2,1)S(1)} %fusion.25), channel_id=1, replica_groups=mesh['yl'=2,'z'=8,'core'=2,'yh'=4,'x'=8] {'yh'}, dimensions={0} | all-to-all | bytes 524288 | tf_op jit(solution)/shard_map/all_to_all | solution.py:209
  (33 shorter events, 4.1 us)
Async XLA Ops:
  6.5 18.0 %copy-start = (bf16[256,4096]{1,0:T(8,128)(2,1)S(1)}, bf16[256,4096]{1,0:T(8,128)(2,1)}, u32[]{:S(2)}) copy-start(bf16[256,4096]{1,0:T(8,128)(2,1)} %param.11) | copy-start | bytes 6291460
  6.5 63.5 %all-gather.2.cloned.1.call-start = ((), (), s32[]{:S(2)}) async-start(), calls=%async_computation.3 | async-start | bytes 3899392 | tf_op jit(solution)/shard_map/all_gather | solution.py:154
  17.7 69.3 %all-to-all-start = ((bf16[8,256,512]{2,1,0:T(8,128)(2,1)}), bf16[8,256,512]{2,1,0:T(8,128)(2,1)}, u32[]{:S(2)}, u32[]{:S(2)}) async-start(bf16[8,256,512]{2,1,0:T(8,128)(2,1)} %repack.1), calls=%async_computation | async-start | bytes 4194304 | tf_op jit(solution)/shard_map/all_to_all | solution.py:158
  24.5 12.7 %copy-start.3 = (f32[4,256]{1,0:T(4,128)S(1)}, f32[4,256]{1,0:T(4,128)}, u32[]{:S(2)}) copy-start(f32[4,256]{1,0:T(4,128)} %param.15) | copy-start | bytes 12292
  24.5 13.4 %copy-start.5 = (f32[4]{0:T(128)S(1)}, f32[4]{0:T(128)}, u32[]{:S(2)}) copy-start(f32[4]{0:T(128)} %param.18) | copy-start | bytes 52
  24.5 13.4 %copy-start.6 = (f32[4]{0:T(128)S(1)}, f32[4]{0:T(128)}, u32[]{:S(2)}) copy-start(f32[4]{0:T(128)} %param.17) | copy-start | bytes 52
  24.6 26.6 %collective-permute-start = (bf16[256,2048]{1,0:T(8,128)(2,1)S(1)}, bf16[256,2048]{1,0:T(8,128)(2,1)}, u32[]{:S(2)}, u32[]{:S(2)}) collective-permute-start(bf16[256,2048]{1,0:T(8,128)(2,1)S(1)} %constant_dynamic-slice_fusion.1), channel_id=1, source_target_pairs={{0,512},{512,0},{1,513},{513,1},{2,514},{514,2},{3,515},{515,3},{4... | collective-permute-start | bytes 3145736 | tf_op jit(solution)/shard_map/ppermute | solution.py:152
  70.0 5.1 %copy-start.7 = (bf16[2048,896]{1,0:T(8,128)(2,1)S(1)}, bf16[2048,896]{1,0:T(8,128)(2,1)}, u32[]{:S(2)}) copy-start(bf16[2048,896]{1,0:T(8,128)(2,1)} %all-gather.2.cloned.1.call-done) | copy-start | bytes 11010052
  72.6 10.9 %collective-permute-start.1 = (bf16[256,384]{1,0:T(8,128)(2,1)S(1)}, bf16[256,384]{1,0:T(8,128)(2,1)S(1)}, u32[]{:S(2)}, u32[]{:S(2)}) collective-permute-start(bf16[256,384]{1,0:T(8,128)(2,1)S(1)} %fusion.22), channel_id=1, source_target_pairs={{0,512},{512,0},{1,513},{513,1},{2,514},{514,2},{3,515},{515,3},{4... | collective-permute-start | bytes 589832 | tf_op jit(solution)/shard_map/ppermute | solution.py:175
  77.1 10.1 %collective-permute-start.2 = (bf16[256,512]{1,0:T(8,128)(2,1)S(1)}, bf16[256,512]{1,0:T(8,128)(2,1)S(1)}, u32[]{:S(2)}, u32[]{:S(2)}) collective-permute-start(bf16[256,512]{1,0:T(8,128)(2,1)S(1)} %fusion.19), channel_id=1, source_target_pairs={{0,512},{512,0},{1,513},{513,1},{2,514},{514,2},{3,515},{515,3},{4... | collective-permute-start | bytes 786440 | tf_op jit(solution)/shard_map/ppermute | solution.py:176
  82.0 5.2 %copy-start.4 = (f32[4]{0:T(128)S(1)}, f32[4]{0:T(128)}, u32[]{:S(2)}) copy-start(f32[4]{0:T(128)} %param.19) | copy-start | bytes 52
  83.5 0.7 copy-start.2
  87.2 0.7 copy-start.1
  90.8 35.1 %all-to-all-start.1 = ((bf16[8,256,256]{2,1,0:T(8,128)(2,1)}), bf16[8,256,256]{2,1,0:T(8,128)(2,1)S(1)}, u32[]{:S(2)}, u32[]{:S(2)}) async-start(bf16[8,256,256]{2,1,0:T(8,128)(2,1)} %shard_map.110), calls=%async_computation.1 | async-start | bytes 2097152 | tf_op jit(solution)/shard_map/all_to_all | solution.py:199
Sparse Core Ops, SparseCore 0:
  10.3 59.7 all-gather.1

commit v5 on v4

--- a/solution.py
+++ b/solution.py
@@ -11,13 +11,13 @@
 SWAP = [(0, 1), (1, 0)]
 
 
-def repack(weight, gain, n_yh, n_x):
-    rows, columns = weight.shape
+def repack(weight, gain, n_yh, n_x, part):
+    rows = weight.shape[0]
+    columns = weight.shape[1] // 2
     width = columns // (n_yh * n_x)
-
-    step = rows // 8
-
-    def kernel(gain_ref, weight_ref, out_ref):
+    step = rows // 4
+
+    def kernel(part_ref, gain_ref, weight_ref, out_ref):
         gains = gain_ref[...]
         for x in range(n_x):
             for y in range(n_yh):
@@ -27,18 +27,21 @@
 
     return pl.pallas_call(
         kernel,
-        grid=(rows // step,),
-        in_specs=[
-            pl.BlockSpec((step, 1), lambda i: (i, 0)),
-            pl.BlockSpec((step, columns), lambda i: (i, 0)),
-        ],
-        out_specs=pl.BlockSpec((n_x, step, n_yh * width), lambda i: (0, i, 0)),
+        grid_spec=pltpu.PrefetchScalarGridSpec(
+            num_scalar_prefetch=1,
+            grid=(rows // step,),
+            in_specs=[
+                pl.BlockSpec((step, 1), lambda i, part: (i, 0)),
+                pl.BlockSpec((step, columns), lambda i, part: (i, part[0])),
+            ],
+            out_specs=pl.BlockSpec((n_x, step, n_yh * width), lambda i, part: (0, i, 0)),
+        ),
         out_shape=jax.ShapeDtypeStruct((n_x, rows, n_yh * width), jnp.bfloat16),
         cost_estimate=pl.CostEstimate(
             flops=rows * columns, bytes_accessed=4 * rows * columns, transcendentals=0
         ),
         name="repack",
-    )(gain[:, None], weight)
+    )(part[None], gain[:, None], weight)
 
 
 def silu(values):
@@ -151,12 +154,20 @@
     given = lax.dynamic_slice_in_dim(tokens, (1 - k_half) * k_rows, k_rows, 1)
     given = lax.ppermute(given, "yl", SWAP)
 
-    whole = lax.all_gather(mine, ("z", "core"), axis=0, tiled=True)
-
+    n_z, core = lax.axis_size("z"), lax.axis_index("core")
+    copies = jnp.broadcast_to(mine[None], (n_z,) + mine.shape)
+    own = lax.all_to_all(copies, "z", 0, 0).reshape(n_z * rows, -1)
     width = out_weight.shape[1] // (n_yh * n_x)
-    pieces = repack(out_weight, norm_gain, n_yh, n_x)
-    group_weight = lax.all_to_all(pieces, "x", 0, 0)
-    group_weight = group_weight.reshape(n_x * channels, n_yh * width)
+    pieces = repack(out_weight, norm_gain, n_yh // 2, n_x, core)
+    half_own = lax.all_to_all(pieces, "x", 0, 0)
+
+    def by_core(values):
+        split = values.reshape(tok_rows, n_z, 2, rows)
+        first = split[:, :, 0].reshape(tok_rows, n_z * rows)
+        second = split[:, :, 1].reshape(tok_rows, n_z * rows)
+        return jnp.where(core == 0, first, second), jnp.where(core == 0, second, first)
+
+    kept, given = by_core(kept), by_core(given)
 
     def padded(values):
         return jnp.pad(values, (0, 128 - heads_here))[None]
@@ -168,13 +179,24 @@
     skips = jnp.repeat(d_skip, two_p)[None]
     rate, bias = padded(a_log), padded(dt_bias)
 
-    def product(left, columns):
-        return jnp.dot(left, whole[:, columns], preferred_element_type=f32)
-
+    ready = (own, kept, given, conv_group, x_taps, skips, rate, bias)
+    own, kept, given, conv_group, x_taps, skips, rate, bias = lax.optimization_barrier(ready)
+    theirs = lax.ppermute(own, "core", SWAP)
     small, large = slice(zx_cols, None), slice(0, zx_cols)
-    small_away = lax.ppermute(product(given, small).astype(bf16), "yl", SWAP)
-    large_away = lax.ppermute(product(given, large).astype(bf16), "yl", SWAP)
-    small_own, large_own = product(kept, small), product(kept, large)
+
+    def product(left, columns, begun):
+        return begun[:, columns] + jnp.dot(
+            left, theirs[:, columns], preferred_element_type=f32
+        )
+
+    given_begun = jnp.dot(given[0], own, preferred_element_type=f32)
+    kept_begun = jnp.dot(kept[0], own, preferred_element_type=f32)
+    small_away = product(given[1], small, given_begun).astype(bf16)
+    small_away = lax.ppermute(small_away, "yl", SWAP)
+    large_away = product(given[1], large, given_begun).astype(bf16)
+    large_away = lax.ppermute(large_away, "yl", SWAP)
+    small_own = product(kept[1], small, kept_begun)
+    large_own = product(kept[1], large, kept_begun)
     mix = on_chip(
         mixing_kernel,
         jax.ShapeDtypeStruct((heads_here, tok_rows, tok_rows), bf16),
@@ -185,7 +207,8 @@
         rate,
         bias,
     )
-    mix, group_weight = lax.optimization_barrier((mix, group_weight))
+    mix, half_own = lax.optimization_barrier((mix, half_own))
+    half_theirs = lax.ppermute(half_own, "core", SWAP)
     spread = on_chip(
         gated_kernel,
         jax.ShapeDtypeStruct((n_x, tok_rows, channels), bf16),
@@ -199,13 +222,16 @@
     group = lax.all_to_all(spread, "x", 0, 0)
     squares = jnp.sum(jnp.square(group.astype(f32)), axis=(0, 2))
     scale = lax.rsqrt(squares / (n_x * channels) + 1e-05)
-    parts = jnp.einsum(
-        "xtc,xcyw->ytw",
-        group,
-        group_weight.reshape(n_x, channels, n_yh, width),
-        preferred_element_type=f32,
-    )
-    parts = (parts * scale[None, :, None]).astype(bf16)
+
+    def partial_out(half):
+        half = half.reshape(n_x, channels, n_yh // 2, width)
+        out = jnp.einsum("xtc,xcyw->ytw", group, half, preferred_element_type=f32)
+        return (out * scale[None, :, None]).astype(bf16)
+
+    ours, others = partial_out(half_own), partial_out(half_theirs)
+    parts = jnp.concatenate(
+        [jnp.where(core == 0, ours, others), jnp.where(core == 0, others, ours)], axis=0
+    )
     got = lax.all_to_all(parts, "yh", 0, 0)
     return jnp.sum(got.astype(f32), axis=0).astype(bf16)
 

time: 154 us -> 167 us (1.084)
  waiting for transfers between devices: 54.8 us -> 69.6 us
  between operations: 13.5 us -> 0.22 us
  starting transfers between devices: 31.8 us -> 39.2 us
  local copies, waits for them, and re-layouts: 13.1 us -> 15.6 us
  Pallas kernels: 11.9 us -> 9.44 us
  other arithmetic: 1.08 us -> 3.03 us
  matrix products: 9.9 us -> 11.8 us
    all_to_all x1 -> x2, waiting for transfers between devices: 0.01 us -> 21.9 us  [the longest x1 12.1 us: layer(): own = lax.all_to_all(copies, 'z', 0, 0).reshape(n_z * rows, -1)]
    all_gather x1 -> x0, waiting for transfers between devices: 18.8 us -> none  [layer(): whole = lax.all_gather(mine, ('z', 'core'), axis=0, tiled=True)]
    all_to_all x1 -> x2, starting transfers between devices: 6.76 us -> 23.6 us  [the longest x1 16.7 us: layer(): own = lax.all_to_all(copies, 'z', 0, 0).reshape(n_z * rows, -1)]
    ppermute x1, starting transfers between devices: 12.5 us -> 2.23 us  [layer(): given = lax.ppermute(given, 'yl', SWAP)]
    ppermute x1, waiting for transfers between devices: 11.5 us -> 20.5 us  [layer(): given = lax.ppermute(given, 'yl', SWAP)]
    ppermute x2 -> x4, starting transfers between devices: 5.84 us -> 9.84 us  [the longest x1 3.6 us: layer(): large_away = lax.ppermute(large_away, 'yl', SWAP)]
    reshape x1 -> x0, local copies, waits for them, and re-layouts: 3.97 us -> none  [layer(): group_weight.reshape(n_x, channels, n_yh, width)]
    unnamed x20 -> x30, local copies, waits for them, and re-layouts: 3.3 us -> 7.24 us
  transfers between devices with their start and end apart: 6 -> 8, of which waited for: 4 -> 4; matrix products, arithmetic and copies ran while one was open for 10% -> 13% of each run, Pallas kernels for 6% -> 4%
where the time goes in v5:
time: 167 us; the launch traced here: 166 us
  waiting for transfers between devices  69.6 us (42%)
  starting transfers between devices  39.2 us (23%)
  blocking collectives  17.5 us (10%)
  local copies, waits for them, and re-layouts  15.6 us (9%)
  matrix products  11.8 us (7%)
  Pallas kernels  9.44 us (6%)
  other arithmetic  3.03 us (2%)
    all_to_all x1, waiting for transfers between devices, layer(): group = lax.all_to_all(spread, 'x', 0, 0)  27.2 us
    ppermute x1, waiting for transfers between devices, layer(): given = lax.ppermute(given, 'yl', SWAP)  20.5 us
    all_to_all x1, blocking collectives, layer(): got = lax.all_to_all(parts, 'yh', 0, 0)  17.5 us
    all_to_all x1, starting transfers between devices, layer(): own = lax.all_to_all(copies, 'z', 0, 0).reshape(n_z * rows, -1)  16.7 us
    all_to_all x1, waiting for transfers between devices, layer(): own = lax.all_to_all(copies, 'z', 0, 0).reshape(n_z * rows, -1)  12.1 us
    all_to_all x1, waiting for transfers between devices, layer(): half_own = lax.all_to_all(pieces, 'x', 0, 0)  9.75 us
    dot_general x4, matrix products, product(): jnp.dot(left, theirs[:, columns], preferred_element_type=f32)  8.14 us
    unnamed x30, local copies, waits for them, and re-layouts  7.24 us
  transfers between devices with their start and end apart: 8, of which 4 were waited for; matrix products, arithmetic and copies ran while one was open for 13% of the time, Pallas kernels for 4%

profile of v5, /device:TPU:16, one launch (start us, length us, event | category | flops | bytes accessed | tf_op | source)
XLA Modules:
  0.0 166.3 jit_solution(1729537048128318862)
XLA Ops:
  2.0 1.5 broadcast_in_dim.28
  3.5 16.7 %all-to-all-start = ((bf16[8,128,896]{2,1,0:T(8,128)(2,1)}), bf16[8,128,896]{2,1,0:T(8,128)(2,1)S(1)}, u32[]{:S(2)}, u32[]{:S(2)}) async-start(bf16[8,128,896]{2,1,0:T(8,128)(2,1)} %broadcast_in_dim.28), calls=%async_computation | async-start | bytes 3670016 | tf_op jit(solution)/shard_map/all_to_all | solution.py:159
  20.1 2.7 %constant_dynamic-slice_fusion.1 = (bf16[256,2048]{1,0:T(8,128)(2,1)S(1)}, bf16[256,2048]{1,0:T(8,128)(2,1)}) fusion(bf16[256,4096]{1,0:T(8,128)(2,1)} %param.11, s32[]{:T(128)S(6)} %select_n.68, s32[]{:T(128)S(6)} %select_n.63), kind=kLoop, calls=%fused_computation.36 | loop fusion | bytes 4194312 | tf_op jit(solution)/shard_map/dynamic_slice | solution.py:154
  24.2 2.2 %collective-permute-start = (bf16[256,2048]{0,1:T(8,128)(2,1)}, bf16[256,2048]{0,1:T(8,128)(2,1)}, u32[]{:S(2)}, u32[]{:S(2)}) collective-permute-start(bf16[256,2048]{0,1:T(8,128)(2,1)} %copy.35), channel_id=1, source_target_pairs={{0,512},{512,0},{1,513},{513,1},{2,514},{514,2},{3,515},{515,3},{4... | collective-permute-start | bytes 3145736 | tf_op jit(solution)/shard_map/ppermute | solution.py:155
  30.5 20.5 %collective-permute-done = bf16[256,2048]{0,1:T(8,128)(2,1)} collective-permute-done((bf16[256,2048]{0,1:T(8,128)(2,1)}, bf16[256,2048]{0,1:T(8,128)(2,1)}, u32[]{:S(2)}, u32[]{:S(2)}) %collective-permute-start) | collective-permute-done | bytes 1048608 | tf_op jit(solution)/shard_map/ppermute | solution.py:155
  51.0 2.6 %broadcast_select_fusion = (bf16[256,8,1,128]{0,3,2,1:T(8,128)(2,1)}, bf16[256,8,1,128]{0,3,2,1:T(8,128)(2,1)}, bf16[256,8,1,128]{0,3,2,1:T(8,128)(2,1)}, bf16[256,8,1,128]{0,3,2,1:T(8,128)(2,1)}) fusion(pred[]{:T(512)S(6)} %eq.2, bf16[256,8,2,128]{0,3,2,1:T(8,128)(2,1)} %bitcast.4, bf16[256,8,2,128]{0,3,2,1:T(8,128)(2,1)S(1)} %bitcast.77), kind=kLoop, calls=%fused_computation.23 | loop fusion | flops 1048576 | bytes 4194305 | tf_op jit(solution)/shard_map/jit(_where)/select_n | solution.py:168
  53.6 12.1 %all-to-all-done = bf16[8,128,896]{2,1,0:T(8,128)(2,1)S(1)} async-done(((bf16[8,128,896]{2,1,0:T(8,128)(2,1)}), bf16[8,128,896]{2,1,0:T(8,128)(2,1)S(1)}, u32[]{:S(2)}, u32[]{:S(2)}) %all-to-all-start) | async-done | bytes 1835040 | tf_op jit(solution)/shard_map/all_to_all | solution.py:159
  66.3 1.9 %collective-permute-start.1 = (bf16[1024,896]{1,0:T(8,128)(2,1)S(1)}, bf16[1024,896]{1,0:T(8,128)(2,1)}, u32[]{:S(2)}, u32[]{:S(2)}) collective-permute-start(bf16[1024,896]{1,0:T(8,128)(2,1)S(1)} %bitcast.74), channel_id=1, source_target_pairs={{0,32},{32,0},{1,33},{33,1},{2,34},{34,2},{3,35},{35,3},{4,36},{36... | collective-permute-start | bytes 5505032 | tf_op jit(solution)/shard_map/ppermute | solution.py:184
  69.1 3.6 %repack.1 = bf16[8,256,256]{2,1,0:T(8,128)(2,1)} custom-call(s32[1]{0:T(128)} %bitcast.10.part_ref, f32[256,1]{1,0:T(8,128)} %copy.28.gain_ref, bf16[256,4096]{1,0:T(8,128)(2,1)} %weight_ref.1), custom_call_target="tpu_custom_call" | custom-call | flops 524288 | bytes 2097152 | tf_op jit(solution)/shard_map/repack/pallas_call | solution.py:28
  72.7 6.9 %all-to-all-start.1 = ((bf16[8,256,256]{2,1,0:T(8,128)(2,1)}), bf16[8,256,256]{2,1,0:T(8,128)(2,1)}, u32[]{:S(2)}, u32[]{:S(2)}) async-start(bf16[8,256,256]{2,1,0:T(8,128)(2,1)} %repack.1), calls=%async_computation.1 | async-start | bytes 2097152 | tf_op jit(solution)/shard_map/all_to_all | solution.py:162
  81.7 1.6 fusion.1
  83.3 2.4 %collective-permute-start.2 = (bf16[256,384]{1,0:T(8,128)(2,1)S(1)}, bf16[256,384]{1,0:T(8,128)(2,1)S(1)}, u32[]{:S(2)}, u32[]{:S(2)}) collective-permute-start(bf16[256,384]{1,0:T(8,128)(2,1)S(1)} %fusion.1), channel_id=1, source_target_pairs={{0,512},{512,0},{1,513},{513,1},{2,514},{514,2},{3,515},{515,3},{4... | collective-permute-start | bytes 589832 | tf_op jit(solution)/shard_map/ppermute | solution.py:195
  85.7 1.7 %fusion = bf16[256,512]{1,0:T(8,128)(2,1)S(1)} fusion(bf16[256,1024]{0,1:T(8,128)(2,1)S(1)} %bitcast.83, bf16[1024,896]{1,0:T(8,128)(2,1)} %collective-permute-done.1, f32[256,896]{1,0:T(8,128)S(1)} %fusion.21), kind=kOutput, calls=%fused_computation.3 | convolution fusion | flops 268697600 | bytes 2359296 | tf_op jit(solution)/shard_map/dot_general | solution.py:188
  87.4 3.6 %collective-permute-start.3 = (bf16[256,512]{1,0:T(8,128)(2,1)S(1)}, bf16[256,512]{1,0:T(8,128)(2,1)S(1)}, u32[]{:S(2)}, u32[]{:S(2)}) collective-permute-start(bf16[256,512]{1,0:T(8,128)(2,1)S(1)} %fusion), channel_id=1, source_target_pairs={{0,512},{512,0},{1,513},{513,1},{2,514},{514,2},{3,515},{515,3},{4... | collective-permute-start | bytes 786440 | tf_op jit(solution)/shard_map/ppermute | solution.py:197
  91.0 2.5 %convolution_add_fusion.1.own_ref = f32[256,512]{1,0:T(8,128)} fusion(bf16[256,1024]{0,1:T(8,128)(2,1)S(1)} %bitcast.80, bf16[1024,896]{1,0:T(8,128)(2,1)} %collective-permute-done.1, f32[256,896]{1,0:T(8,128)S(1)} %fusion.20), kind=kOutput, calls=%fused_computation.2 | convolution fusion | flops 268566528 | bytes 2621440 | tf_op jit(solution)/shard_map/dot_general | solution.py:188
  93.5 2.4 %convolution_add_fusion.3.own_ref = f32[256,384]{1,0:T(8,128)} fusion(bf16[256,1024]{0,1:T(8,128)(2,1)S(1)} %bitcast.81, bf16[1024,896]{1,0:T(8,128)(2,1)} %collective-permute-done.1, f32[256,896]{1,0:T(8,128)S(1)} %fusion.20), kind=kOutput, calls=%fused_computation.5 | convolution fusion | flops 201424896 | bytes 2097152 | tf_op jit(solution)/shard_map/dot_general | solution.py:188
  96.5 2.9 %shard_map.109.mix_ref = bf16[4,256,256]{2,1,0:T(8,128)(2,1)} custom-call(f32[256,384]{1,0:T(8,128)} %convolution_add_fusion.3.own_ref, bf16[256,384]{1,0:T(8,128)(2,1)} %copy-done.6, f32[4,256]{1,0:T(4,128)} %constant_dynamic-slice_fusion.taps_ref, f32[1,128]{1,0:T(1,128)} %get-tuple-element.23.rate_ref, f32[1,128]{1,0:T(1,128)} %get-tuple-element.24.bias_ref), custom_call_target="tpu_custom_call" | custom-call | flops 2621440 | bytes 1119232 | tf_op jit(solution)/shard_map/pallas_call | solution.py:111
  99.4 9.8 %all-to-all-done.1 = bf16[8,256,256]{2,1,0:T(8,128)(2,1)} async-done(((bf16[8,256,256]{2,1,0:T(8,128)(2,1)}), bf16[8,256,256]{2,1,0:T(8,128)(2,1)}, u32[]{:S(2)}, u32[]{:S(2)}) %all-to-all-start.1) | async-done | bytes 1048608 | tf_op jit(solution)/shard_map/all_to_all | solution.py:162
  109.9 2.9 %shard_map.110 = bf16[8,256,256]{2,1,0:T(8,128)(2,1)} custom-call(f32[256,512]{1,0:T(8,128)} %convolution_add_fusion.1.own_ref, bf16[256,512]{1,0:T(8,128)(2,1)} %copy-done.5, f32[4,512]{1,0:T(4,128)} %bitcast.86, f32[1,512]{1,0:T(1,128)} %bitcast.87, bf16[4,256,256]{2,1,0:T(8,128)(2,1)} %shard_map.109.mix_ref), custom_call_target="tpu_custom_call" | custom-call | flops 67108864 | bytes 2369536 | tf_op jit(solution)/shard_map/pallas_call | solution.py:111
  112.8 3.6 %all-to-all-start.2 = ((bf16[8,256,256]{2,1,0:T(8,128)(2,1)}), bf16[8,256,256]{2,1,0:T(8,128)(2,1)S(1)}, u32[]{:S(2)}, u32[]{:S(2)}) async-start(bf16[8,256,256]{2,1,0:T(8,128)(2,1)} %shard_map.110), calls=%async_computation.2 | async-start | bytes 2097152 | tf_op jit(solution)/shard_map/all_to_all | solution.py:222
  116.3 2.0 %collective-permute-start.4 = (bf16[8,256,256]{2,1,0:T(8,128)(2,1)}, bf16[8,256,256]{2,1,0:T(8,128)(2,1)S(1)}, u32[]{:S(2)}, u32[]{:S(2)}) collective-permute-start(bf16[8,256,256]{2,1,0:T(8,128)(2,1)} %all-to-all-done.1), channel_id=1, source_target_pairs={{0,32},{32,0},{1,33},{33,1},{2,34},{34,2},{3,35},{35,3},{4,36},{36... | collective-permute-start | bytes 3145736 | tf_op jit(solution)/shard_map/ppermute | solution.py:211
  118.3 27.2 %all-to-all-done.2 = bf16[8,256,256]{2,1,0:T(8,128)(2,1)S(1)} async-done(((bf16[8,256,256]{2,1,0:T(8,128)(2,1)}), bf16[8,256,256]{2,1,0:T(8,128)(2,1)S(1)}, u32[]{:S(2)}, u32[]{:S(2)}) %all-to-all-start.2) | async-done | bytes 1048608 | tf_op jit(solution)/shard_map/all_to_all | solution.py:222
  146.3 1.7 %select_bitcast_fusion.1 = (bf16[2,256,128]{1,2,0:T(8,128)(2,1)S(1)}, bf16[2,256,128]{1,2,0:T(8,128)(2,1)S(1)}) fusion(bf16[2,128,256]{2,1,0:T(8,128)(2,1)S(1)} %fusion.5, pred[]{:T(512)S(6)} %eq.2, f32[256]{0:T(256)S(1)} %add_rsqrt_fusion, bf16[8,256,256]{2,1,0:T(8,128)(2,1)S(1)} %all-to-all-done.2, bf16[8,256,256]{2,1,0:T(8,128)(2,1)} %all-to-all-done.1), kind=kOutput, calls=%fused_computation.31 | convolution fusion | flops 268697600 | bytes 2491393 | tf_op jit(solution)/shard_map/xtc,xcyw->ytw/dot_general | solution.py:228
  148.1 17.5 %all_to_all.20 = bf16[4,256,128]{1,2,0:T(8,128)(2,1)S(1)} all-to-all(bf16[4,256,128]{1,2,0:T(8,128)(2,1)S(1)} %pad_maximum_fusion), channel_id=1, replica_groups=mesh['yl'=2,'z'=8,'core'=2,'yh'=4,'x'=8] {'yh'}, dimensions={0} | all-to-all | bytes 524288 | tf_op jit(solution)/shard_map/all_to_all | solution.py:235
  (51 shorter events, 13.7 us)
Async XLA Ops:
  0.0 1.8 %copy-start = (bf16[128,1024]{1,0:T(8,128)(2,1)S(1)}, bf16[128,1024]{1,0:T(8,128)(2,1)}, u32[]{:S(2)}) copy-start(bf16[128,1024]{1,0:T(8,128)(2,1)} %param.14) | copy-start | bytes 786436
  3.5 62.3 %all-to-all-start = ((bf16[8,128,896]{2,1,0:T(8,128)(2,1)}), bf16[8,128,896]{2,1,0:T(8,128)(2,1)S(1)}, u32[]{:S(2)}, u32[]{:S(2)}) async-start(bf16[8,128,896]{2,1,0:T(8,128)(2,1)} %broadcast_in_dim.28), calls=%async_computation | async-start | bytes 3670016 | tf_op jit(solution)/shard_map/all_to_all | solution.py:159
  22.8 5.1 %copy-start.7 = (f32[4,256]{1,0:T(4,128)S(1)}, f32[4,256]{1,0:T(4,128)}, u32[]{:S(2)}) copy-start(f32[4,256]{1,0:T(4,128)} %param.15) | copy-start | bytes 12292
  22.8 5.8 %copy-start.10 = (f32[4]{0:T(128)S(1)}, f32[4]{0:T(128)}, u32[]{:S(2)}) copy-start(f32[4]{0:T(128)} %param.18) | copy-start | bytes 52
  22.8 5.8 %copy-start.11 = (f32[4]{0:T(128)S(1)}, f32[4]{0:T(128)}, u32[]{:S(2)}) copy-start(f32[4]{0:T(128)} %param.17) | copy-start | bytes 52
  24.2 26.8 %collective-permute-start = (bf16[256,2048]{0,1:T(8,128)(2,1)}, bf16[256,2048]{0,1:T(8,128)(2,1)}, u32[]{:S(2)}, u32[]{:S(2)}) collective-permute-start(bf16[256,2048]{0,1:T(8,128)(2,1)} %copy.35), channel_id=1, source_target_pairs={{0,512},{512,0},{1,513},{513,1},{2,514},{514,2},{3,515},{515,3},{4... | collective-permute-start | bytes 3145736 | tf_op jit(solution)/shard_map/ppermute | solution.py:155
  51.0 14.7 %copy-start.9 = (f32[4]{0:T(128)S(1)}, f32[4]{0:T(128)}, u32[]{:S(2)}) copy-start(f32[4]{0:T(128)} %param.19) | copy-start | bytes 52
  51.0 17.3 %copy-start.8 = (f32[256]{0:T(256)S(1)}, f32[256]{0:T(256)}, u32[]{:S(2)}) copy-start(f32[256]{0:T(256)} %param.20) | copy-start | bytes 3076
  66.3 15.0 %collective-permute-start.1 = (bf16[1024,896]{1,0:T(8,128)(2,1)S(1)}, bf16[1024,896]{1,0:T(8,128)(2,1)}, u32[]{:S(2)}, u32[]{:S(2)}) collective-permute-start(bf16[1024,896]{1,0:T(8,128)(2,1)S(1)} %bitcast.74), channel_id=1, source_target_pairs={{0,32},{32,0},{1,33},{33,1},{2,34},{34,2},{3,35},{35,3},{4,36},{36... | collective-permute-start | bytes 5505032 | tf_op jit(solution)/shard_map/ppermute | solution.py:184
  72.7 6.9 %copy-start.2 = (bf16[256,8,1,128]{0,3,2,1:T(8,128)(2,1)S(1)}, bf16[256,8,1,128]{0,3,2,1:T(8,128)(2,1)}, u32[]{:S(2)}) copy-start(bf16[256,8,1,128]{0,3,2,1:T(8,128)(2,1)} %get-tuple-element.32) | copy-start | bytes 1572868
  72.7 36.5 %all-to-all-start.1 = ((bf16[8,256,256]{2,1,0:T(8,128)(2,1)}), bf16[8,256,256]{2,1,0:T(8,128)(2,1)}, u32[]{:S(2)}, u32[]{:S(2)}) async-start(bf16[8,256,256]{2,1,0:T(8,128)(2,1)} %repack.1), calls=%async_computation.1 | async-start | bytes 2097152 | tf_op jit(solution)/shard_map/all_to_all | solution.py:162
  79.6 1.0 copy-start.1
  80.6 1.0 copy-start.4
  83.3 7.7 %copy-start.3 = (bf16[256,8,1,128]{0,3,2,1:T(8,128)(2,1)S(1)}, bf16[256,8,1,128]{0,3,2,1:T(8,128)(2,1)}, u32[]{:S(2)}) copy-start(bf16[256,8,1,128]{0,3,2,1:T(8,128)(2,1)} %get-tuple-element.38) | copy-start | bytes 1572868
  83.3 12.6 %collective-permute-start.2 = (bf16[256,384]{1,0:T(8,128)(2,1)S(1)}, bf16[256,384]{1,0:T(8,128)(2,1)S(1)}, u32[]{:S(2)}, u32[]{:S(2)}) collective-permute-start(bf16[256,384]{1,0:T(8,128)(2,1)S(1)} %fusion.1), channel_id=1, source_target_pairs={{0,512},{512,0},{1,513},{513,1},{2,514},{514,2},{3,515},{515,3},{4... | collective-permute-start | bytes 589832 | tf_op jit(solution)/shard_map/ppermute | solution.py:195
  87.4 21.8 %collective-permute-start.3 = (bf16[256,512]{1,0:T(8,128)(2,1)S(1)}, bf16[256,512]{1,0:T(8,128)(2,1)S(1)}, u32[]{:S(2)}, u32[]{:S(2)}) collective-permute-start(bf16[256,512]{1,0:T(8,128)(2,1)S(1)} %fusion), channel_id=1, source_target_pairs={{0,512},{512,0},{1,513},{513,1},{2,514},{514,2},{3,515},{515,3},{4... | collective-permute-start | bytes 786440 | tf_op jit(solution)/shard_map/ppermute | solution.py:197
  95.8 0.7 copy-start.6
  109.2 0.7 copy-start.5
  112.8 32.7 %all-to-all-start.2 = ((bf16[8,256,256]{2,1,0:T(8,128)(2,1)}), bf16[8,256,256]{2,1,0:T(8,128)(2,1)S(1)}, u32[]{:S(2)}, u32[]{:S(2)}) async-start(bf16[8,256,256]{2,1,0:T(8,128)(2,1)} %shard_map.110), calls=%async_computation.2 | async-start | bytes 2097152 | tf_op jit(solution)/shard_map/all_to_all | solution.py:222
  116.3 29.5 %collective-permute-start.4 = (bf16[8,256,256]{2,1,0:T(8,128)(2,1)}, bf16[8,256,256]{2,1,0:T(8,128)(2,1)S(1)}, u32[]{:S(2)}, u32[]{:S(2)}) collective-permute-start(bf16[8,256,256]{2,1,0:T(8,128)(2,1)} %all-to-all-done.1), channel_id=1, source_target_pairs={{0,32},{32,0},{1,33},{33,1},{2,34},{34,2},{3,35},{35,3},{4,36},{36... | collective-permute-start | bytes 3145736 | tf_op jit(solution)/shard_map/ppermute | solution.py:211

commit v6 on v5

--- a/solution.py
+++ b/solution.py
@@ -104,6 +104,28 @@
             pair = jnp.where(first, kept, out).astype(jnp.bfloat16)
             for copy in range(out_ref.shape[0]):
                 out_ref[copy, :, (h // 2) * wide : (h // 2 + 1) * wide] = pair
+
+
+def finish_kernel(core_ref, group_ref, own_ref, theirs_ref, out_ref):
+    f32 = jnp.float32
+    n_x, rows, channels = group_ref.shape
+    width = out_ref.shape[2]
+    many = own_ref.shape[2] // width
+    squares = jnp.zeros((rows, 1), f32)
+    totals = [jnp.zeros((rows, many * width), f32) for _ in range(2)]
+    for x in range(n_x):
+        values = group_ref[x]
+        squares += jnp.sum(jnp.square(values.astype(f32)), axis=1, keepdims=True)
+        totals = [
+            total + jnp.dot(values, ref[x], preferred_element_type=f32)
+            for total, ref in zip(totals, (own_ref, theirs_ref))
+        ]
+    scale = lax.rsqrt(squares / (n_x * channels) + 1e-05)
+    start = core_ref[0] * many
+    for total, first in zip(totals, (start, many - start)):
+        done = (total * scale).astype(jnp.bfloat16)
+        for y in range(many):
+            out_ref[first + y] = done[:, y * width : (y + 1) * width]
 
 
 def on_chip(kernel, out_shape, flops, *args):
@@ -159,7 +181,16 @@
     own = lax.all_to_all(copies, "z", 0, 0).reshape(n_z * rows, -1)
     width = out_weight.shape[1] // (n_yh * n_x)
     pieces = repack(out_weight, norm_gain, n_yh // 2, n_x, core)
-    half_own = lax.all_to_all(pieces, "x", 0, 0)
+    x_pos = lax.axis_index("x")
+
+    def piece(k):
+        return lax.dynamic_slice_in_dim(pieces, (x_pos + k) % n_x, 1, 0)
+
+    half_own = jnp.zeros_like(pieces)
+    half_own = lax.dynamic_update_slice_in_dim(half_own, piece(0), x_pos, 0)
+    for k in range(1, n_x):
+        came = lax.ppermute(piece(k), "x", [(i, (i + k) % n_x) for i in range(n_x)])
+        half_own = lax.dynamic_update_slice_in_dim(half_own, came, (x_pos - k) % n_x, 0)
 
     def by_core(values):
         split = values.reshape(tok_rows, n_z, 2, rows)
@@ -179,8 +210,9 @@
     skips = jnp.repeat(d_skip, two_p)[None]
     rate, bias = padded(a_log), padded(dt_bias)
 
-    ready = (own, kept, given, conv_group, x_taps, skips, rate, bias)
-    own, kept, given, conv_group, x_taps, skips, rate, bias = lax.optimization_barrier(ready)
+    ready = (own, kept, given, conv_group, x_taps, skips, rate, bias, half_own)
+    ready = lax.optimization_barrier(ready)
+    own, kept, given, conv_group, x_taps, skips, rate, bias, half_own = ready
     theirs = lax.ppermute(own, "core", SWAP)
     small, large = slice(zx_cols, None), slice(0, zx_cols)
 
@@ -207,7 +239,6 @@
         rate,
         bias,
     )
-    mix, half_own = lax.optimization_barrier((mix, half_own))
     half_theirs = lax.ppermute(half_own, "core", SWAP)
     spread = on_chip(
         gated_kernel,
@@ -220,18 +251,18 @@
         mix,
     )
     group = lax.all_to_all(spread, "x", 0, 0)
-    squares = jnp.sum(jnp.square(group.astype(f32)), axis=(0, 2))
-    scale = lax.rsqrt(squares / (n_x * channels) + 1e-05)
-
-    def partial_out(half):
-        half = half.reshape(n_x, channels, n_yh // 2, width)
-        out = jnp.einsum("xtc,xcyw->ytw", group, half, preferred_element_type=f32)
-        return (out * scale[None, :, None]).astype(bf16)
-
-    ours, others = partial_out(half_own), partial_out(half_theirs)
-    parts = jnp.concatenate(
-        [jnp.where(core == 0, ours, others), jnp.where(core == 0, others, ours)], axis=0
-    )
+    parts = pl.pallas_call(
+        finish_kernel,
+        in_specs=[pl.BlockSpec(memory_space=pltpu.SMEM)]
+        + [pl.BlockSpec(memory_space=pltpu.VMEM)] * 3,
+        out_shape=jax.ShapeDtypeStruct((n_yh, tok_rows, width), bf16),
+        cost_estimate=pl.CostEstimate(
+            flops=2 * tok_rows * n_x * channels * n_yh * width,
+            bytes_accessed=6 * n_x * tok_rows * channels,
+            transcendentals=0,
+        ),
+        name="finish",
+    )(core[None], group, half_own, half_theirs)
     got = lax.all_to_all(parts, "yh", 0, 0)
     return jnp.sum(got.astype(f32), axis=0).astype(bf16)
 

time: 167 us -> 164 us (0.982)
  waiting for transfers between devices: 69.6 us -> 29.7 us
  starting transfers between devices: 39.2 us -> 64 us
  local copies, waits for them, and re-layouts: 15.6 us -> 28.2 us
  matrix products: 11.8 us -> 5.92 us
  Pallas kernels: 9.44 us -> 12.7 us
    ppermute x0 -> x7, starting transfers between devices: none -> 30 us  [layer(): came = lax.ppermute(piece(k), 'x', [(i, (i + k) % n_x) for i in range(n_x)])]
    ppermute x1, waiting for transfers between devices: 20.5 us -> 0.01 us  [layer(): given = lax.ppermute(given, 'yl', SWAP)]
    all_to_all x1, waiting for transfers between devices: 12.1 us -> 0.01 us  [layer(): own = lax.all_to_all(copies, 'z', 0, 0).reshape(n_z * rows, -1)]
    all_to_all x1 -> x0, waiting for transfers between devices: 9.75 us -> none  [layer(): half_own = lax.all_to_all(pieces, 'x', 0, 0)]
    dynamic_update_slice x0 -> x7, local copies, waits for them, and re-layouts: none -> 8.24 us  [layer(): lax.dynamic_update_slice_in_dim(half_own, came, (x_pos - k) % n_x, 0)]
    all_to_all x1 -> x0, starting transfers between devices: 6.89 us -> none  [layer(): half_own = lax.all_to_all(pieces, 'x', 0, 0)]
    dot_general x4, matrix products: 8.14 us -> 3.42 us  [product(): jnp.dot(left, theirs[:, columns], preferred_element_type=f32)]
    all_to_all x1, waiting for transfers between devices: 27.2 us -> 23.6 us  [layer(): group = lax.all_to_all(spread, 'x', 0, 0)]
  transfers between devices with their start and end apart: 8 -> 14, of which waited for: 4 -> 5; matrix products, arithmetic and copies ran while one was open for 13% -> 18% of each run, Pallas kernels for 4% -> 4%
where the time goes in v6:
time: 164 us; the launch traced here: 163 us
  starting transfers between devices  64 us (39%)
  waiting for transfers between devices  29.7 us (18%)
  local copies, waits for them, and re-layouts  28.2 us (17%)
  blocking collectives  18.4 us (11%)
  Pallas kernels  12.7 us (8%)
  matrix products  5.92 us (4%)
  other arithmetic  3.38 us (2%)
    ppermute x7, starting transfers between devices, layer(): came = lax.ppermute(piece(k), 'x', [(i, (i + k) % n_x) for i in range(n_x)])  30 us
    all_to_all x1, waiting for transfers between devices, layer(): group = lax.all_to_all(spread, 'x', 0, 0)  23.6 us
    all_to_all x1, blocking collectives, layer(): got = lax.all_to_all(parts, 'yh', 0, 0)  18.4 us
    all_to_all x1, starting transfers between devices, layer(): own = lax.all_to_all(copies, 'z', 0, 0).reshape(n_z * rows, -1)  16.8 us
    unnamed x30, local copies, waits for them, and re-layouts  8.41 us
    dynamic_update_slice x7, local copies, waits for them, and re-layouts, layer(): lax.dynamic_update_slice_in_dim(half_own, came, (x_pos - k) % n_x, 0)  8.24 us
    pallas_call x2, Pallas kernels, on_chip(): pl.pallas_call(kernel, out_shape=out_shape, cost_estimate=pl.CostEstimate...  5.81 us
    all_to_all x1, starting transfers between devices, layer(): group = lax.all_to_all(spread, 'x', 0, 0)  5.19 us
  transfers between devices with their start and end apart: 14, of which 5 were waited for; matrix products, arithmetic and copies ran while one was open for 18% of the time, Pallas kernels for 4%

profile of v6, /device:TPU:16, one launch (start us, length us, event | category | flops | bytes accessed | tf_op | source)
XLA Modules:
  0.0 162.6 jit_solution(789696468623996780)
XLA Ops:
  3.4 16.8 %all-to-all-start = ((bf16[8,128,896]{2,1,0:T(8,128)(2,1)}), bf16[8,128,896]{2,1,0:T(8,128)(2,1)S(1)}, u32[]{:S(2)}, u32[]{:S(2)}) async-start(bf16[8,128,896]{2,1,0:T(8,128)(2,1)} %broadcast_in_dim.31), calls=%async_computation | async-start | bytes 3670016 | tf_op jit(solution)/shard_map/all_to_all | solution.py:181
  21.1 3.6 %repack.1 = bf16[8,256,256]{2,1,0:T(8,128)(2,1)} custom-call(s32[1]{0:T(128)} %bitcast.part_ref.core_ref, f32[256,1]{1,0:T(8,128)} %copy.18.gain_ref, bf16[256,4096]{1,0:T(8,128)(2,1)} %weight_ref.1), custom_call_target="tpu_custom_call" | custom-call | flops 524288 | bytes 2097152 | tf_op jit(solution)/shard_map/repack/pallas_call | solution.py:28
  25.7 2.1 %constant_dynamic-slice_fusion = (bf16[1,256,256]{2,1,0:T(8,128)(2,1)S(1)}, bf16[1,256,256]{2,1,0:T(8,128)(2,1)S(1)}, bf16[1,256,256]{2,1,0:T(8,128)(2,1)S(1)}, ...) fusion(bf16[8,256,256]{2,1,0:T(8,128)(2,1)} %repack.1, ...), kind=kLoop, calls=%fused_computation.19 | loop fusion | bytes 2097188 | tf_op jit(solution)/shard_map/dynamic_slice | solution.py:187
  27.9 3.4 %collective-permute-start.1 = (bf16[1,256,256]{2,1,0:T(8,128)(2,1)}, bf16[1,256,256]{2,1,0:T(8,128)(2,1)}, u32[]{:S(2)}, u32[]{:S(2)}) collective-permute-start(bf16[1,256,256]{2,1,0:T(8,128)(2,1)} %get-tuple-element.35), channel_id=1, source_target_pairs={{0,1},{1,2},{2,3},{3,4},{4,5},{5,6},{6,7},{7,0},{8,9},{9,10},{10,1... | collective-permute-start | bytes 393224 | tf_op jit(solution)/shard_map/ppermute | solution.py:192
  31.3 4.3 %collective-permute-start.2 = (bf16[1,256,256]{2,1,0:T(8,128)(2,1)}, bf16[1,256,256]{2,1,0:T(8,128)(2,1)}, u32[]{:S(2)}, u32[]{:S(2)}) collective-permute-start(bf16[1,256,256]{2,1,0:T(8,128)(2,1)} %get-tuple-element.34), channel_id=1, source_target_pairs={{0,2},{1,3},{2,4},{3,5},{4,6},{5,7},{6,0},{7,1},{8,10},{9,11},{10,... | collective-permute-start | bytes 393224 | tf_op jit(solution)/shard_map/ppermute | solution.py:192
  35.6 4.7 %collective-permute-start.3 = (bf16[1,256,256]{2,1,0:T(8,128)(2,1)}, bf16[1,256,256]{2,1,0:T(8,128)(2,1)}, u32[]{:S(2)}, u32[]{:S(2)}) collective-permute-start(bf16[1,256,256]{2,1,0:T(8,128)(2,1)} %get-tuple-element.33), channel_id=1, source_target_pairs={{0,3},{1,4},{2,5},{3,6},{4,7},{5,0},{6,1},{7,2},{8,11},{9,12},{10,... | collective-permute-start | bytes 393224 | tf_op jit(solution)/shard_map/ppermute | solution.py:192
  40.3 4.2 %collective-permute-start.4 = (bf16[1,256,256]{2,1,0:T(8,128)(2,1)}, bf16[1,256,256]{2,1,0:T(8,128)(2,1)}, u32[]{:S(2)}, u32[]{:S(2)}) collective-permute-start(bf16[1,256,256]{2,1,0:T(8,128)(2,1)} %get-tuple-element.32), channel_id=1, source_target_pairs={{0,4},{1,5},{2,6},{3,7},{4,0},{5,1},{6,2},{7,3},{8,12},{9,13},{10,... | collective-permute-start | bytes 393224 | tf_op jit(solution)/shard_map/ppermute | solution.py:192
  44.4 2.7 %constant_dynamic-slice_fusion.8 = (bf16[256,2048]{1,0:T(8,128)(2,1)}, bf16[256,2048]{1,0:T(8,128)(2,1)S(1)}) fusion(bf16[256,4096]{1,0:T(8,128)(2,1)} %param.11, s32[]{:T(128)S(6)} %select_n.160, s32[]{:T(128)S(6)} %select_n.155), kind=kLoop, calls=%fused_computation.34 | loop fusion | bytes 4194312 | tf_op jit(solution)/shard_map/dynamic_slice | solution.py:176
  47.2 2.3 %copy.20 = bf16[256,2048]{0,1:T(8,128)(2,1)} copy(bf16[256,2048]{1,0:T(8,128)(2,1)} %get-tuple-element.27) | data formatting | bytes 2097152
  49.4 2.2 %collective-permute-start = (bf16[256,2048]{0,1:T(8,128)(2,1)}, bf16[256,2048]{0,1:T(8,128)(2,1)}, u32[]{:S(2)}, u32[]{:S(2)}) collective-permute-start(bf16[256,2048]{0,1:T(8,128)(2,1)} %copy.20), channel_id=1, source_target_pairs={{0,512},{512,0},{1,513},{513,1},{2,514},{514,2},{3,515},{515,3},{4... | collective-permute-start | bytes 3145736 | tf_op jit(solution)/shard_map/ppermute | solution.py:177
  56.3 4.7 %collective-permute-start.5 = (bf16[1,256,256]{2,1,0:T(8,128)(2,1)S(1)}, bf16[1,256,256]{2,1,0:T(8,128)(2,1)S(1)}, u32[]{:S(2)}, u32[]{:S(2)}) collective-permute-start(bf16[1,256,256]{2,1,0:T(8,128)(2,1)S(1)} %get-tuple-element.31), channel_id=1, source_target_pairs={{0,5},{1,6},{2,7},{3,0},{4,1},{5,2},{6,3},{7,4},{8,13},{9,14},{10,... | collective-permute-start | bytes 393224 | tf_op jit(solution)/shard_map/ppermute | solution.py:192
  62.6 5.4 %collective-permute-start.6 = (bf16[1,256,256]{2,1,0:T(8,128)(2,1)S(1)}, bf16[1,256,256]{2,1,0:T(8,128)(2,1)S(1)}, u32[]{:S(2)}, u32[]{:S(2)}) collective-permute-start(bf16[1,256,256]{2,1,0:T(8,128)(2,1)S(1)} %get-tuple-element.30), channel_id=1, source_target_pairs={{0,6},{1,7},{2,0},{3,1},{4,2},{5,3},{6,4},{7,5},{8,14},{9,15},{10,... | collective-permute-start | bytes 393224 | tf_op jit(solution)/shard_map/ppermute | solution.py:192
  69.6 3.3 %collective-permute-start.7 = (bf16[1,256,256]{2,1,0:T(8,128)(2,1)S(1)}, bf16[1,256,256]{2,1,0:T(8,128)(2,1)S(1)}, u32[]{:S(2)}, u32[]{:S(2)}) collective-permute-start(bf16[1,256,256]{2,1,0:T(8,128)(2,1)S(1)} %get-tuple-element.29), channel_id=1, source_target_pairs={{0,7},{1,0},{2,1},{3,2},{4,3},{5,4},{6,5},{7,6},{8,15},{9,8},{10,9... | collective-permute-start | bytes 393224 | tf_op jit(solution)/shard_map/ppermute | solution.py:192
  78.0 2.7 %broadcast_select_fusion = (bf16[256,8,1,128]{0,3,2,1:T(8,128)(2,1)}, bf16[256,8,1,128]{0,3,2,1:T(8,128)(2,1)}, bf16[256,8,1,128]{0,3,2,1:T(8,128)(2,1)}, bf16[256,8,1,128]{0,3,2,1:T(8,128)(2,1)}) fusion(pred[]{:T(512)S(6)} %eq.22, bf16[256,8,2,128]{0,3,2,1:T(8,128)(2,1)} %bitcast.5, bf16[256,8,2,128]{0,3,2,1:T(8,128)(2,1)S(1)} %bitcast.34), kind=kLoop, calls=%fused_computation.10 | loop fusion | flops 1048576 | bytes 4194305 | tf_op jit(solution)/shard_map/jit(_where)/select_n | solution.py:199
  81.4 1.9 %collective-permute-start.8 = (bf16[1024,896]{1,0:T(8,128)(2,1)S(1)}, bf16[1024,896]{1,0:T(8,128)(2,1)S(1)}, u32[]{:S(2)}, u32[]{:S(2)}) collective-permute-start(bf16[1024,896]{1,0:T(8,128)(2,1)S(1)} %bitcast.31), channel_id=1, source_target_pairs={{0,32},{32,0},{1,33},{33,1},{2,34},{34,2},{3,35},{35,3},{4,36},{36... | collective-permute-start | bytes 5505032 | tf_op jit(solution)/shard_map/ppermute | solution.py:216
  87.5 3.7 %collective-permute-start.10 = (bf16[256,384]{1,0:T(8,128)(2,1)S(1)}, bf16[256,384]{1,0:T(8,128)(2,1)S(1)}, u32[]{:S(2)}, u32[]{:S(2)}) collective-permute-start(bf16[256,384]{1,0:T(8,128)(2,1)S(1)} %fusion.1), channel_id=1, source_target_pairs={{0,512},{512,0},{1,513},{513,1},{2,514},{514,2},{3,515},{515,3},{4... | collective-permute-start | bytes 589832 | tf_op jit(solution)/shard_map/ppermute | solution.py:227
  91.7 2.2 %collective-permute-start.9 = (bf16[256,512]{1,0:T(8,128)(2,1)S(1)}, bf16[256,512]{1,0:T(8,128)(2,1)S(1)}, u32[]{:S(2)}, u32[]{:S(2)}) collective-permute-start(bf16[256,512]{1,0:T(8,128)(2,1)S(1)} %fusion), channel_id=1, source_target_pairs={{0,512},{512,0},{1,513},{513,1},{2,514},{514,2},{3,515},{515,3},{4... | collective-permute-start | bytes 786440 | tf_op jit(solution)/shard_map/ppermute | solution.py:229
  97.6 2.9 %shard_map.109.mix_ref = bf16[4,256,256]{2,1,0:T(8,128)(2,1)} custom-call(f32[256,384]{1,0:T(8,128)} %convolution_add_fusion.3.own_ref, bf16[256,384]{1,0:T(8,128)(2,1)} %copy-done.8, f32[4,256]{1,0:T(4,128)} %constant_dynamic-slice_fusion.7.taps_ref, f32[1,128]{1,0:T(1,128)} %get-tuple-element.24.rate_ref, f32[1,128]{1,0:T(1,128)} %get-tuple-element.25.bias_ref), custom_call_target="tpu_custom_call" | custom-call | flops 2621440 | bytes 1119232 | tf_op jit(solution)/shard_map/pallas_call | solution.py:133
  102.8 2.9 %shard_map.110 = bf16[8,256,256]{2,1,0:T(8,128)(2,1)} custom-call(f32[256,512]{1,0:T(8,128)} %convolution_add_fusion.1.own_ref, bf16[256,512]{1,0:T(8,128)(2,1)} %copy-done.7, f32[4,512]{1,0:T(4,128)} %bitcast.43, f32[1,512]{1,0:T(1,128)} %bitcast.44, bf16[4,256,256]{2,1,0:T(8,128)(2,1)} %shard_map.109.mix_ref), custom_call_target="tpu_custom_call" | custom-call | flops 67108864 | bytes 2369536 | tf_op jit(solution)/shard_map/pallas_call | solution.py:133
  105.7 5.2 %all-to-all-start.1 = ((bf16[8,256,256]{2,1,0:T(8,128)(2,1)}), bf16[8,256,256]{2,1,0:T(8,128)(2,1)S(1)}, u32[]{:S(2)}, u32[]{:S(2)}) async-start(bf16[8,256,256]{2,1,0:T(8,128)(2,1)} %shard_map.110), calls=%async_computation.1 | async-start | bytes 2097152 | tf_op jit(solution)/shard_map/all_to_all | solution.py:253
  112.8 2.8 %collective-permute-done.11.theirs_ref = bf16[8,256,256]{2,1,0:T(8,128)(2,1)S(1)} collective-permute-done((bf16[8,256,256]{2,1,0:T(8,128)(2,1)}, bf16[8,256,256]{2,1,0:T(8,128)(2,1)S(1)}, u32[]{:S(2)}, u32[]{:S(2)}) %collective-permute-start.11) | collective-permute-done | bytes 1048608 | tf_op jit(solution)/shard_map/ppermute | solution.py:242
  115.7 23.6 %all-to-all-done.1.group_ref = bf16[8,256,256]{2,1,0:T(8,128)(2,1)S(1)} async-done(((bf16[8,256,256]{2,1,0:T(8,128)(2,1)}), bf16[8,256,256]{2,1,0:T(8,128)(2,1)S(1)}, u32[]{:S(2)}, u32[]{:S(2)}) %all-to-all-start.1) | async-done | bytes 1048608 | tf_op jit(solution)/shard_map/all_to_all | solution.py:253
  140.2 3.3 %finish.1 = bf16[4,256,128]{2,1,0:T(8,128)(2,1)} custom-call(s32[1]{0:T(128)} %bitcast.part_ref.core_ref, bf16[8,256,256]{2,1,0:T(8,128)(2,1)} %copy-done.2, bf16[8,256,256]{2,1,0:T(8,128)(2,1)} %constant_dynamic-update-slice_fusion.6.own_ref, bf16[8,256,256]{2,1,0:T(8,128)(2,1)} %copy-done.4), custom_call_target="tpu_custom_call" | custom-call | flops 536870912 | bytes 3145728 | tf_op jit(solution)/shard_map/finish/pallas_call | solution.py:254
  143.5 18.4 %all_to_all.15 = bf16[4,256,128]{2,1,0:T(8,128)(2,1)S(1)} all-to-all(bf16[4,256,128]{2,1,0:T(8,128)(2,1)} %finish.1), channel_id=1, replica_groups=mesh['yl'=2,'z'=8,'core'=2,'yh'=4,'x'=8] {'yh'}, dimensions={0} | all-to-all | bytes 524288 | tf_op jit(solution)/shard_map/all_to_all | solution.py:266
  (67 shorter events, 32.9 us)
Async XLA Ops:
  0.0 1.8 %copy-start = (bf16[128,1024]{1,0:T(8,128)(2,1)S(1)}, bf16[128,1024]{1,0:T(8,128)(2,1)}, u32[]{:S(2)}) copy-start(bf16[128,1024]{1,0:T(8,128)(2,1)} %param.14) | copy-start | bytes 786436
  3.4 16.8 %copy-start.10 = (f32[256]{0:T(256)S(1)}, f32[256]{0:T(256)}, u32[]{:S(2)}) copy-start(f32[256]{0:T(256)} %param.20) | copy-start | bytes 3076
  3.4 77.3 %all-to-all-start = ((bf16[8,128,896]{2,1,0:T(8,128)(2,1)}), bf16[8,128,896]{2,1,0:T(8,128)(2,1)S(1)}, u32[]{:S(2)}, u32[]{:S(2)}) async-start(bf16[8,128,896]{2,1,0:T(8,128)(2,1)} %broadcast_in_dim.31), calls=%async_computation | async-start | bytes 3670016 | tf_op jit(solution)/shard_map/all_to_all | solution.py:181
  27.9 28.4 %collective-permute-start.1 = (bf16[1,256,256]{2,1,0:T(8,128)(2,1)}, bf16[1,256,256]{2,1,0:T(8,128)(2,1)}, u32[]{:S(2)}, u32[]{:S(2)}) collective-permute-start(bf16[1,256,256]{2,1,0:T(8,128)(2,1)} %get-tuple-element.35), channel_id=1, source_target_pairs={{0,1},{1,2},{2,3},{3,4},{4,5},{5,6},{6,7},{7,0},{8,9},{9,10},{10,1... | collective-permute-start | bytes 393224 | tf_op jit(solution)/shard_map/ppermute | solution.py:192
  31.3 31.3 %collective-permute-start.2 = (bf16[1,256,256]{2,1,0:T(8,128)(2,1)}, bf16[1,256,256]{2,1,0:T(8,128)(2,1)}, u32[]{:S(2)}, u32[]{:S(2)}) collective-permute-start(bf16[1,256,256]{2,1,0:T(8,128)(2,1)} %get-tuple-element.34), channel_id=1, source_target_pairs={{0,2},{1,3},{2,4},{3,5},{4,6},{5,7},{6,0},{7,1},{8,10},{9,11},{10,... | collective-permute-start | bytes 393224 | tf_op jit(solution)/shard_map/ppermute | solution.py:192
  35.6 34.0 %collective-permute-start.3 = (bf16[1,256,256]{2,1,0:T(8,128)(2,1)}, bf16[1,256,256]{2,1,0:T(8,128)(2,1)}, u32[]{:S(2)}, u32[]{:S(2)}) collective-permute-start(bf16[1,256,256]{2,1,0:T(8,128)(2,1)} %get-tuple-element.33), channel_id=1, source_target_pairs={{0,3},{1,4},{2,5},{3,6},{4,7},{5,0},{6,1},{7,2},{8,11},{9,12},{10,... | collective-permute-start | bytes 393224 | tf_op jit(solution)/shard_map/ppermute | solution.py:192
  40.3 34.2 %collective-permute-start.4 = (bf16[1,256,256]{2,1,0:T(8,128)(2,1)}, bf16[1,256,256]{2,1,0:T(8,128)(2,1)}, u32[]{:S(2)}, u32[]{:S(2)}) collective-permute-start(bf16[1,256,256]{2,1,0:T(8,128)(2,1)} %get-tuple-element.32), channel_id=1, source_target_pairs={{0,4},{1,5},{2,6},{3,7},{4,0},{5,1},{6,2},{7,3},{8,12},{9,13},{10,... | collective-permute-start | bytes 393224 | tf_op jit(solution)/shard_map/ppermute | solution.py:192
  47.1 4.5 %copy-start.9 = (f32[4,256]{1,0:T(4,128)S(1)}, f32[4,256]{1,0:T(4,128)}, u32[]{:S(2)}) copy-start(f32[4,256]{1,0:T(4,128)} %param.15) | copy-start | bytes 12292
  49.4 28.6 %collective-permute-start = (bf16[256,2048]{0,1:T(8,128)(2,1)}, bf16[256,2048]{0,1:T(8,128)(2,1)}, u32[]{:S(2)}, u32[]{:S(2)}) collective-permute-start(bf16[256,2048]{0,1:T(8,128)(2,1)} %copy.20), channel_id=1, source_target_pairs={{0,512},{512,0},{1,513},{513,1},{2,514},{514,2},{3,515},{515,3},{4... | collective-permute-start | bytes 3145736 | tf_op jit(solution)/shard_map/ppermute | solution.py:177
  55.7 22.4 %copy-start.1 = (bf16[256,2048]{0,1:T(8,128)(2,1)S(1)}, bf16[256,2048]{0,1:T(8,128)(2,1)}, u32[]{:S(2)}) copy-start(bf16[256,2048]{0,1:T(8,128)(2,1)} %copy.19) | copy-start | bytes 3145732
  56.3 19.8 %collective-permute-start.5 = (bf16[1,256,256]{2,1,0:T(8,128)(2,1)S(1)}, bf16[1,256,256]{2,1,0:T(8,128)(2,1)S(1)}, u32[]{:S(2)}, u32[]{:S(2)}) collective-permute-start(bf16[1,256,256]{2,1,0:T(8,128)(2,1)S(1)} %get-tuple-element.31), channel_id=1, source_target_pairs={{0,5},{1,6},{2,7},{3,0},{4,1},{5,2},{6,3},{7,4},{8,13},{9,14},{10,... | collective-permute-start | bytes 393224 | tf_op jit(solution)/shard_map/ppermute | solution.py:192
  62.6 14.1 %collective-permute-start.6 = (bf16[1,256,256]{2,1,0:T(8,128)(2,1)S(1)}, bf16[1,256,256]{2,1,0:T(8,128)(2,1)S(1)}, u32[]{:S(2)}, u32[]{:S(2)}) collective-permute-start(bf16[1,256,256]{2,1,0:T(8,128)(2,1)S(1)} %get-tuple-element.30), channel_id=1, source_target_pairs={{0,6},{1,7},{2,0},{3,1},{4,2},{5,3},{6,4},{7,5},{8,14},{9,15},{10,... | collective-permute-start | bytes 393224 | tf_op jit(solution)/shard_map/ppermute | solution.py:192
  69.6 7.8 %collective-permute-start.7 = (bf16[1,256,256]{2,1,0:T(8,128)(2,1)S(1)}, bf16[1,256,256]{2,1,0:T(8,128)(2,1)S(1)}, u32[]{:S(2)}, u32[]{:S(2)}) collective-permute-start(bf16[1,256,256]{2,1,0:T(8,128)(2,1)S(1)} %get-tuple-element.29), channel_id=1, source_target_pairs={{0,7},{1,0},{2,1},{3,2},{4,3},{5,4},{6,5},{7,6},{8,15},{9,8},{10,9... | collective-permute-start | bytes 393224 | tf_op jit(solution)/shard_map/ppermute | solution.py:192
  78.0 2.7 %copy-start.11 = (f32[4]{0:T(128)S(1)}, f32[4]{0:T(128)}, u32[]{:S(2)}) copy-start(f32[4]{0:T(128)} %param.19) | copy-start | bytes 52
  80.7 4.4 %copy-start.3 = (bf16[256,8,1,128]{0,3,2,1:T(8,128)(2,1)S(1)}, bf16[256,8,1,128]{0,3,2,1:T(8,128)(2,1)}, u32[]{:S(2)}) copy-start(bf16[256,8,1,128]{0,3,2,1:T(8,128)(2,1)} %get-tuple-element.41) | copy-start | bytes 1572868
  81.4 5.7 %collective-permute-start.8 = (bf16[1024,896]{1,0:T(8,128)(2,1)S(1)}, bf16[1024,896]{1,0:T(8,128)(2,1)S(1)}, u32[]{:S(2)}, u32[]{:S(2)}) collective-permute-start(bf16[1024,896]{1,0:T(8,128)(2,1)S(1)} %bitcast.31), channel_id=1, source_target_pairs={{0,32},{32,0},{1,33},{33,1},{2,34},{34,2},{3,35},{35,3},{4,36},{36... | collective-permute-start | bytes 5505032 | tf_op jit(solution)/shard_map/ppermute | solution.py:216
  85.1 2.0 %copy-start.6 = (bf16[256,8,1,128]{0,3,2,1:T(8,128)(2,1)S(1)}, bf16[256,8,1,128]{0,3,2,1:T(8,128)(2,1)}, u32[]{:S(2)}) copy-start(bf16[256,8,1,128]{0,3,2,1:T(8,128)(2,1)} %get-tuple-element.37) | copy-start | bytes 1572868
  87.5 6.5 %copy-start.5 = (bf16[256,8,1,128]{0,3,2,1:T(8,128)(2,1)S(1)}, bf16[256,8,1,128]{0,3,2,1:T(8,128)(2,1)}, u32[]{:S(2)}) copy-start(bf16[256,8,1,128]{0,3,2,1:T(8,128)(2,1)} %get-tuple-element.42) | copy-start | bytes 1572868
  87.5 9.4 %collective-permute-start.10 = (bf16[256,384]{1,0:T(8,128)(2,1)S(1)}, bf16[256,384]{1,0:T(8,128)(2,1)S(1)}, u32[]{:S(2)}, u32[]{:S(2)}) collective-permute-start(bf16[256,384]{1,0:T(8,128)(2,1)S(1)} %fusion.1), channel_id=1, source_target_pairs={{0,512},{512,0},{1,513},{513,1},{2,514},{514,2},{3,515},{515,3},{4... | collective-permute-start | bytes 589832 | tf_op jit(solution)/shard_map/ppermute | solution.py:227
  91.7 10.4 %collective-permute-start.9 = (bf16[256,512]{1,0:T(8,128)(2,1)S(1)}, bf16[256,512]{1,0:T(8,128)(2,1)S(1)}, u32[]{:S(2)}, u32[]{:S(2)}) collective-permute-start(bf16[256,512]{1,0:T(8,128)(2,1)S(1)} %fusion), channel_id=1, source_target_pairs={{0,512},{512,0},{1,513},{513,1},{2,514},{514,2},{3,515},{515,3},{4... | collective-permute-start | bytes 786440 | tf_op jit(solution)/shard_map/ppermute | solution.py:229
  105.7 33.5 %all-to-all-start.1 = ((bf16[8,256,256]{2,1,0:T(8,128)(2,1)}), bf16[8,256,256]{2,1,0:T(8,128)(2,1)S(1)}, u32[]{:S(2)}, u32[]{:S(2)}) async-start(bf16[8,256,256]{2,1,0:T(8,128)(2,1)} %shard_map.110), calls=%async_computation.1 | async-start | bytes 2097152 | tf_op jit(solution)/shard_map/all_to_all | solution.py:253
  110.9 4.8 %collective-permute-start.11 = (bf16[8,256,256]{2,1,0:T(8,128)(2,1)}, bf16[8,256,256]{2,1,0:T(8,128)(2,1)S(1)}, u32[]{:S(2)}, u32[]{:S(2)}) collective-permute-start(bf16[8,256,256]{2,1,0:T(8,128)(2,1)} %constant_dynamic-update-slice_fusion.6.own_ref), channel_id=1, source_target_pairs={{0,32},{32,0},{1,33},{33,1},{2,34},{34,2},{3,35},{35,3},{4,36},{36... | collective-permute-start | bytes 3145736 | tf_op jit(solution)/shard_map/ppermute | solution.py:242
  115.7 23.6 %copy-start.4 = (bf16[8,256,256]{2,1,0:T(8,128)(2,1)}, bf16[8,256,256]{2,1,0:T(8,128)(2,1)S(1)}, u32[]{:S(2)}) copy-start(bf16[8,256,256]{2,1,0:T(8,128)(2,1)S(1)} %collective-permute-done.11.theirs_ref) | copy-start | bytes 3145732
  139.2 1.0 copy-start.2
  (2 other events, 1.4 us)

commit v7 on v6

--- a/solution.py
+++ b/solution.py
@@ -42,6 +42,42 @@
         ),
         name="repack",
     )(part[None], gain[:, None], weight)
+
+
+def sort_tokens(tokens, k_half, core, width):
+    length, columns = tokens.shape
+    step, half = length // 4, columns // 2
+    blocks = half // (2 * width)
+
+    def kernel(where_ref, near_ref, far_ref, *out_refs):
+        swapped = where_ref[1] == 1
+        for in_ref, out_ref in zip((near_ref, far_ref), out_refs):
+            for block in range(blocks):
+                first = in_ref[:, 2 * block * width : (2 * block + 1) * width]
+                second = in_ref[:, (2 * block + 1) * width : (2 * block + 2) * width]
+                to = slice(block * width, (block + 1) * width)
+                out_ref[0, :, to] = jnp.where(swapped, second, first)
+                out_ref[1, :, to] = jnp.where(swapped, first, second)
+
+    shape = jax.ShapeDtypeStruct((2, length, half // 2), tokens.dtype)
+    out_spec = pl.BlockSpec((2, step, half // 2), lambda i, where: (0, i, 0))
+    return pl.pallas_call(
+        kernel,
+        grid_spec=pltpu.PrefetchScalarGridSpec(
+            num_scalar_prefetch=1,
+            grid=(length // step,),
+            in_specs=[
+                pl.BlockSpec((step, half), lambda i, where: (i, where[0])),
+                pl.BlockSpec((step, half), lambda i, where: (i, 1 - where[0])),
+            ],
+            out_specs=[out_spec, out_spec],
+        ),
+        out_shape=[shape, shape],
+        cost_estimate=pl.CostEstimate(
+            flops=length * columns, bytes_accessed=4 * length * columns, transcendentals=0
+        ),
+        name="sort_tokens",
+    )(jnp.stack([k_half, core]), tokens, tokens)
 
 
 def silu(values):
@@ -170,35 +206,31 @@
         ],
         axis=1,
     )
-    k_half = lax.axis_index("yl")
-    k_rows = tokens.shape[1] // 2
-    kept = lax.dynamic_slice_in_dim(tokens, k_half * k_rows, k_rows, 1)
-    given = lax.dynamic_slice_in_dim(tokens, (1 - k_half) * k_rows, k_rows, 1)
+    core, z_pos, n_z = lax.axis_index("core"), lax.axis_index("z"), lax.axis_size("z")
+    kept, given = sort_tokens(tokens, lax.axis_index("yl"), core, rows)
     given = lax.ppermute(given, "yl", SWAP)
 
-    n_z, core = lax.axis_size("z"), lax.axis_index("core")
-    copies = jnp.broadcast_to(mine[None], (n_z,) + mine.shape)
-    own = lax.all_to_all(copies, "z", 0, 0).reshape(n_z * rows, -1)
+    up = [(i, (i + 1) % n_z) for i in range(n_z)]
+    down = [(i, (i - 1) % n_z) for i in range(n_z)]
+    own = jnp.zeros((n_z,) + mine.shape, bf16)
+
+    def place(total, block, offset, row=0):
+        return lax.dynamic_update_slice(total, block[None], ((z_pos + offset) % n_z, row, 0))
+
+    own = place(own, mine, 0)
+    above = below = mine
+    for i in range(1, n_z // 2):
+        below = lax.ppermute(below, "z", up)
+        above = lax.ppermute(above, "z", down)
+        own = place(place(own, below, -i), above, i)
+    below = lax.ppermute(below[: rows // 2], "z", up)
+    above = lax.ppermute(above[rows // 2 :], "z", down)
+    own = place(place(own, below, n_z // 2), above, n_z // 2, rows // 2)
+    own = own.reshape(n_z * rows, -1)
+
     width = out_weight.shape[1] // (n_yh * n_x)
     pieces = repack(out_weight, norm_gain, n_yh // 2, n_x, core)
-    x_pos = lax.axis_index("x")
-
-    def piece(k):
-        return lax.dynamic_slice_in_dim(pieces, (x_pos + k) % n_x, 1, 0)
-
-    half_own = jnp.zeros_like(pieces)
-    half_own = lax.dynamic_update_slice_in_dim(half_own, piece(0), x_pos, 0)
-    for k in range(1, n_x):
-        came = lax.ppermute(piece(k), "x", [(i, (i + k) % n_x) for i in range(n_x)])
-        half_own = lax.dynamic_update_slice_in_dim(half_own, came, (x_pos - k) % n_x, 0)
-
-    def by_core(values):
-        split = values.reshape(tok_rows, n_z, 2, rows)
-        first = split[:, :, 0].reshape(tok_rows, n_z * rows)
-        second = split[:, :, 1].reshape(tok_rows, n_z * rows)
-        return jnp.where(core == 0, first, second), jnp.where(core == 0, second, first)
-
-    kept, given = by_core(kept), by_core(given)
+    half_own = lax.all_to_all(pieces, "x", 0, 0)
 
     def padded(values):
         return jnp.pad(values, (0, 128 - heads_here))[None]
@@ -210,9 +242,6 @@
     skips = jnp.repeat(d_skip, two_p)[None]
     rate, bias = padded(a_log), padded(dt_bias)
 
-    ready = (own, kept, given, conv_group, x_taps, skips, rate, bias, half_own)
-    ready = lax.optimization_barrier(ready)
-    own, kept, given, conv_group, x_taps, skips, rate, bias, half_own = ready
     theirs = lax.ppermute(own, "core", SWAP)
     small, large = slice(zx_cols, None), slice(0, zx_cols)
 
@@ -239,6 +268,7 @@
         rate,
         bias,
     )
+    mix, half_own = lax.optimization_barrier((mix, half_own))
     half_theirs = lax.ppermute(half_own, "core", SWAP)
     spread = on_chip(
         gated_kernel,

time: 164 us -> 172 us (1.049)
  local copies, waits for them, and re-layouts: 28.2 us -> 8.2 us
  waiting for transfers between devices: 29.7 us -> 47.5 us
  matrix products: 5.92 us -> 12 us
  Pallas kernels: 12.7 us -> 17.5 us
  other arithmetic: 3.38 us -> 1.29 us
  starting transfers between devices: 64 us -> 66 us
    ppermute x7 -> x8, waiting for transfers between devices: 0.02 us -> 10.5 us  [the longest x3 8.23 us: layer(): below = lax.ppermute(below, 'z', up)]
    ppermute x7 -> x8, starting transfers between devices: 30 us -> 40.4 us  [the longest x3 24.3 us: layer(): above = lax.ppermute(above, 'z', down)]
    ppermute x1, waiting for transfers between devices: 0.01 us -> 9.77 us  [layer(): given = lax.ppermute(given, 'yl', SWAP)]
    all_to_all x1, starting transfers between devices: 16.8 us -> 7.23 us  [layer(): half_own = lax.all_to_all(pieces, 'x', 0, 0)]
    dynamic_update_slice x7 -> x8, local copies, waits for them, and re-layouts: 8.24 us -> 0.23 us  [place(): lax.dynamic_update_slice(total, block[None], ((z_pos + offset) % n_z, row...]
    dot_general x4, matrix products: 3.42 us -> 8.46 us  [product(): jnp.dot(left, theirs[:, columns], preferred_element_type=f32)]
    dynamic_slice x2 -> x0, local copies, waits for them, and re-layouts: 4.85 us -> none  [the longest x1 2.71 us: layer(): given = lax.dynamic_slice_in_dim(tokens, (1 - k_half) * k_rows, k_rows, 1)]
    pallas_call x0 -> x1, Pallas kernels: none -> 4.79 us  [sort_tokens(): pl.pallas_call(kernel, grid_spec=pltpu.PrefetchScalarGridSpec(num_scalar_...]
  transfers between devices with their start and end apart: 14 -> 15, of which waited for: 5 -> 9; matrix products, arithmetic and copies ran while one was open for 18% -> 9% of each run, Pallas kernels for 4% -> 7%
where the time goes in v7:
time: 172 us; the launch traced here: 171 us
  starting transfers between devices  66 us (38%)
  waiting for transfers between devices  47.5 us (28%)
  blocking collectives  18.1 us (11%)
  Pallas kernels  17.5 us (10%)
  matrix products  12 us (7%)
  local copies, waits for them, and re-layouts  8.2 us (5%)
    ppermute x3, starting transfers between devices, layer(): above = lax.ppermute(above, 'z', down)  24.3 us
    all_to_all x1, waiting for transfers between devices, layer(): group = lax.all_to_all(spread, 'x', 0, 0)  23 us
    all_to_all x1, blocking collectives, layer(): got = lax.all_to_all(parts, 'yh', 0, 0)  18.1 us
    ppermute x1, waiting for transfers between devices, layer(): given = lax.ppermute(given, 'yl', SWAP)  9.77 us
    ppermute x3, starting transfers between devices, layer(): below = lax.ppermute(below, 'z', up)  9.01 us
    dot_general x4, matrix products, product(): jnp.dot(left, theirs[:, columns], preferred_element_type=f32)  8.46 us
    ppermute x3, waiting for transfers between devices, layer(): below = lax.ppermute(below, 'z', up)  8.23 us
    all_to_all x1, starting transfers between devices, layer(): half_own = lax.all_to_all(pieces, 'x', 0, 0)  7.23 us
  transfers between devices with their start and end apart: 15, of which 9 were waited for; matrix products, arithmetic and copies ran while one was open for 9% of the time, Pallas kernels for 7%

profile of v7, /device:TPU:16, one launch (start us, length us, event | category | flops | bytes accessed | tf_op | source)
XLA Modules:
  0.0 171.0 jit_solution(8348209124232999985)
XLA Ops:
  2.2 5.2 %collective-permute-start = (bf16[128,896]{1,0:T(8,128)(2,1)S(1)}, bf16[128,896]{1,0:T(8,128)(2,1)S(1)}, u32[]{:S(2)}, u32[]{:S(2)}) collective-permute-start(bf16[128,896]{1,0:T(8,128)(2,1)S(1)} %get-tuple-element.14), channel_id=1, source_target_pairs={{0,64},{64,128},{128,192},{192,256},{256,320},{320,384},{384,448},... | collective-permute-start | bytes 688136 | tf_op jit(solution)/shard_map/ppermute | solution.py:223
  7.4 14.0 %collective-permute-start.1 = (bf16[128,896]{1,0:T(8,128)(2,1)S(1)}, bf16[128,896]{1,0:T(8,128)(2,1)S(1)}, u32[]{:S(2)}, u32[]{:S(2)}) collective-permute-start(bf16[128,896]{1,0:T(8,128)(2,1)S(1)} %get-tuple-element.14), channel_id=1, source_target_pairs={{0,448},{64,0},{128,64},{192,128},{256,192},{320,256},{384,320},{4... | collective-permute-start | bytes 688136 | tf_op jit(solution)/shard_map/ppermute | solution.py:224
  21.6 3.5 %collective-permute-done = bf16[128,896]{1,0:T(8,128)(2,1)S(1)} collective-permute-done((bf16[128,896]{1,0:T(8,128)(2,1)S(1)}, bf16[128,896]{1,0:T(8,128)(2,1)S(1)}, u32[]{:S(2)}, u32[]{:S(2)}) %collective-permute-start) | collective-permute-done | bytes 229408 | tf_op jit(solution)/shard_map/ppermute | solution.py:223
  27.0 5.1 %collective-permute-start.3 = (bf16[128,896]{1,0:T(8,128)(2,1)S(1)}, bf16[128,896]{1,0:T(8,128)(2,1)S(1)}, u32[]{:S(2)}, u32[]{:S(2)}) collective-permute-start(bf16[128,896]{1,0:T(8,128)(2,1)S(1)} %collective-permute-done.1), channel_id=1, source_target_pairs={{0,448},{64,0},{128,64},{192,128},{256,192},{320,256},{384,320},{4... | collective-permute-start | bytes 688136 | tf_op jit(solution)/shard_map/ppermute | solution.py:224
  32.2 2.7 %collective-permute-done.2 = bf16[128,896]{1,0:T(8,128)(2,1)S(1)} collective-permute-done((bf16[128,896]{1,0:T(8,128)(2,1)S(1)}, bf16[128,896]{1,0:T(8,128)(2,1)S(1)}, u32[]{:S(2)}, u32[]{:S(2)}) %collective-permute-start.2) | collective-permute-done | bytes 229408 | tf_op jit(solution)/shard_map/ppermute | solution.py:223
  36.9 5.1 %collective-permute-start.5 = (bf16[128,896]{1,0:T(8,128)(2,1)S(1)}, bf16[128,896]{1,0:T(8,128)(2,1)S(1)}, u32[]{:S(2)}, u32[]{:S(2)}) collective-permute-start(bf16[128,896]{1,0:T(8,128)(2,1)S(1)} %collective-permute-done.3), channel_id=1, source_target_pairs={{0,448},{64,0},{128,64},{192,128},{256,192},{320,256},{384,320},{4... | collective-permute-start | bytes 688136 | tf_op jit(solution)/shard_map/ppermute | solution.py:224
  42.1 2.0 %collective-permute-done.4 = bf16[128,896]{1,0:T(8,128)(2,1)S(1)} collective-permute-done((bf16[128,896]{1,0:T(8,128)(2,1)S(1)}, bf16[128,896]{1,0:T(8,128)(2,1)S(1)}, u32[]{:S(2)}, u32[]{:S(2)}) %collective-permute-start.4) | collective-permute-done | bytes 229408 | tf_op jit(solution)/shard_map/ppermute | solution.py:223
  46.0 5.1 %collective-permute-start.7 = (bf16[64,896]{1,0:T(8,128)(2,1)S(1)}, bf16[64,896]{1,0:T(8,128)(2,1)S(1)}, u32[]{:S(2)}, u32[]{:S(2)}) collective-permute-start(bf16[64,896]{1,0:T(8,128)(2,1)S(1)} %slice.53), channel_id=1, source_target_pairs={{0,448},{64,0},{128,64},{192,128},{256,192},{320,256},{384,320},{4... | collective-permute-start | bytes 344072 | tf_op jit(solution)/shard_map/ppermute | solution.py:227
  56.0 4.8 %sort_tokens.1 = (bf16[2,256,1024]{2,1,0:T(8,128)(2,1)}, bf16[2,256,1024]{2,1,0:T(8,128)(2,1)}) custom-call(s32[2]{0:T(128)} %pad_add_fusion.where_ref, bf16[256,4096]{1,0:T(8,128)(2,1)} %far_ref.1, bf16[256,4096]{1,0:T(8,128)(2,1)} %far_ref.1), custom_call_target="tpu_custom_call" | custom-call | flops 1048576 | bytes 4194304 | tf_op jit(solution)/shard_map/sort_tokens/pallas_call | solution.py:64
  63.6 3.6 %repack.1 = bf16[8,256,256]{2,1,0:T(8,128)(2,1)} custom-call(s32[1]{0:T(128)} %bitcast.part_ref.core_ref, f32[256,1]{1,0:T(8,128)} %copy.14.gain_ref, bf16[256,4096]{1,0:T(8,128)(2,1)} %weight_ref.1), custom_call_target="tpu_custom_call" | custom-call | flops 524288 | bytes 2097152 | tf_op jit(solution)/shard_map/repack/pallas_call | solution.py:28
  67.2 7.2 %all-to-all-start = ((bf16[8,256,256]{2,1,0:T(8,128)(2,1)}), bf16[8,256,256]{2,1,0:T(8,128)(2,1)S(1)}, u32[]{:S(2)}, u32[]{:S(2)}) async-start(bf16[8,256,256]{2,1,0:T(8,128)(2,1)} %repack.1), calls=%async_computation | async-start | bytes 2097152 | tf_op jit(solution)/shard_map/all_to_all | solution.py:233
  78.8 9.8 %collective-permute-done.9 = bf16[2,256,1024]{2,1,0:T(8,128)(2,1)} collective-permute-done((bf16[2,256,1024]{2,1,0:T(8,128)(2,1)}, bf16[2,256,1024]{2,1,0:T(8,128)(2,1)}, u32[]{:S(2)}, u32[]{:S(2)}) %collective-permute-start.9) | collective-permute-done | bytes 1048608 | tf_op jit(solution)/shard_map/ppermute | solution.py:211
  92.3 2.2 %collective-permute-start.10 = (bf16[256,512]{1,0:T(8,128)(2,1)S(1)}, bf16[256,512]{1,0:T(8,128)(2,1)S(1)}, u32[]{:S(2)}, u32[]{:S(2)}) collective-permute-start(bf16[256,512]{1,0:T(8,128)(2,1)S(1)} %fusion.8), channel_id=1, source_target_pairs={{0,512},{512,0},{1,513},{513,1},{2,514},{514,2},{3,515},{515,3},{4... | collective-permute-start | bytes 786440 | tf_op jit(solution)/shard_map/ppermute | solution.py:258
  96.2 3.6 %collective-permute-start.11 = (bf16[256,384]{1,0:T(8,128)(2,1)S(1)}, bf16[256,384]{1,0:T(8,128)(2,1)S(1)}, u32[]{:S(2)}, u32[]{:S(2)}) collective-permute-start(bf16[256,384]{1,0:T(8,128)(2,1)S(1)} %fusion.23), channel_id=1, source_target_pairs={{0,512},{512,0},{1,513},{513,1},{2,514},{514,2},{3,515},{515,3},{4... | collective-permute-start | bytes 589832 | tf_op jit(solution)/shard_map/ppermute | solution.py:256
  99.9 2.5 %slice_add_fusion.1.own_ref = f32[256,512]{1,0:T(8,128)} fusion(f32[256,896]{1,0:T(8,128)S(1)} %fusion.16, bf16[1024,896]{1,0:T(8,128)(2,1)} %collective-permute-done.8, bf16[2,256,1024]{2,1,0:T(8,128)(2,1)S(1)} %copy-done.3), kind=kOutput, calls=%fused_computation.13 | convolution fusion | flops 268566528 | bytes 2621440 | tf_op jit(solution)/shard_map/dot_general | solution.py:249
  102.4 2.4 %slice_add_fusion.3.own_ref = f32[256,384]{1,0:T(8,128)} fusion(f32[256,896]{1,0:T(8,128)S(1)} %fusion.16, bf16[1024,896]{1,0:T(8,128)(2,1)} %collective-permute-done.8, bf16[2,256,1024]{2,1,0:T(8,128)(2,1)S(1)} %copy-done.3), kind=kOutput, calls=%fused_computation.23 | convolution fusion | flops 201424896 | bytes 2097152 | tf_op jit(solution)/shard_map/dot_general | solution.py:249
  106.9 2.9 %shard_map.109.mix_ref = bf16[4,256,256]{2,1,0:T(8,128)(2,1)} custom-call(f32[256,384]{1,0:T(8,128)} %slice_add_fusion.3.own_ref, bf16[256,384]{1,0:T(8,128)(2,1)} %copy-done.5, f32[4,256]{1,0:T(4,128)} %constant_dynamic-slice_fusion.taps_ref, f32[1,128]{1,0:T(1,128)} %get-tuple-element.16.rate_ref, f32[1,128]{1,0:T(1,128)} %get-tuple-element.15.bias_ref), custom_call_target="tpu_custom_call" | custom-call | flops 2621440 | bytes 1119232 | tf_op jit(solution)/shard_map/pallas_call | solution.py:169
  110.6 2.9 %shard_map.110 = bf16[8,256,256]{2,1,0:T(8,128)(2,1)} custom-call(f32[256,512]{1,0:T(8,128)} %slice_add_fusion.1.own_ref, bf16[256,512]{1,0:T(8,128)(2,1)} %copy-done.4, f32[4,512]{1,0:T(4,128)} %bitcast.66, f32[1,512]{1,0:T(1,128)} %bitcast.67, bf16[4,256,256]{2,1,0:T(8,128)(2,1)} %shard_map.109.mix_ref), custom_call_target="tpu_custom_call" | custom-call | flops 67108864 | bytes 2369536 | tf_op jit(solution)/shard_map/pallas_call | solution.py:169
  113.5 6.8 %all-to-all-start.1 = ((bf16[8,256,256]{2,1,0:T(8,128)(2,1)}), bf16[8,256,256]{2,1,0:T(8,128)(2,1)S(1)}, u32[]{:S(2)}, u32[]{:S(2)}) async-start(bf16[8,256,256]{2,1,0:T(8,128)(2,1)} %shard_map.110), calls=%async_computation.1 | async-start | bytes 2097152 | tf_op jit(solution)/shard_map/all_to_all | solution.py:283
  120.2 1.9 %collective-permute-start.12 = (bf16[8,256,256]{2,1,0:T(8,128)(2,1)S(1)}, bf16[8,256,256]{2,1,0:T(8,128)(2,1)}, u32[]{:S(2)}, u32[]{:S(2)}) collective-permute-start(bf16[8,256,256]{2,1,0:T(8,128)(2,1)S(1)} %all-to-all-done.own_ref), channel_id=1, source_target_pairs={{0,32},{32,0},{1,33},{33,1},{2,34},{34,2},{3,35},{35,3},{4,36},{36... | collective-permute-start | bytes 3145736 | tf_op jit(solution)/shard_map/ppermute | solution.py:272
  122.2 2.8 %collective-permute-done.12.theirs_ref = bf16[8,256,256]{2,1,0:T(8,128)(2,1)} collective-permute-done((bf16[8,256,256]{2,1,0:T(8,128)(2,1)S(1)}, bf16[8,256,256]{2,1,0:T(8,128)(2,1)}, u32[]{:S(2)}, u32[]{:S(2)}) %collective-permute-start.12) | collective-permute-done | bytes 1048608 | tf_op jit(solution)/shard_map/ppermute | solution.py:272
  124.9 23.0 %all-to-all-done.1.group_ref = bf16[8,256,256]{2,1,0:T(8,128)(2,1)S(1)} async-done(((bf16[8,256,256]{2,1,0:T(8,128)(2,1)}), bf16[8,256,256]{2,1,0:T(8,128)(2,1)S(1)}, u32[]{:S(2)}, u32[]{:S(2)}) %all-to-all-start.1) | async-done | bytes 1048608 | tf_op jit(solution)/shard_map/all_to_all | solution.py:283
  148.9 3.3 %finish.1 = bf16[4,256,128]{2,1,0:T(8,128)(2,1)} custom-call(s32[1]{0:T(128)} %bitcast.part_ref.core_ref, bf16[8,256,256]{2,1,0:T(8,128)(2,1)} %copy-done.2, bf16[8,256,256]{2,1,0:T(8,128)(2,1)} %copy-done.1, bf16[8,256,256]{2,1,0:T(8,128)(2,1)} %collective-permute-done.12.theirs_ref), custom_call_target="tpu_custom_call" | custom-call | flops 536870912 | bytes 3145728 | tf_op jit(solution)/shard_map/finish/pallas_call | solution.py:284
  152.2 18.1 %all_to_all.15 = bf16[4,256,128]{2,1,0:T(8,128)(2,1)S(1)} all-to-all(bf16[4,256,128]{2,1,0:T(8,128)(2,1)} %finish.1), channel_id=1, replica_groups=mesh['yl'=2,'z'=8,'core'=2,'yh'=4,'x'=8] {'yh'}, dimensions={0} | all-to-all | bytes 524288 | tf_op jit(solution)/shard_map/all_to_all | solution.py:296
  (66 shorter events, 30.0 us)
Async XLA Ops:
  0.0 1.9 %copy-start = (bf16[128,1024]{1,0:T(8,128)(2,1)S(1)}, bf16[128,1024]{1,0:T(8,128)(2,1)}, u32[]{:S(2)}) copy-start(bf16[128,1024]{1,0:T(8,128)(2,1)} %param.14) | copy-start | bytes 786436
  2.2 22.9 %collective-permute-start = (bf16[128,896]{1,0:T(8,128)(2,1)S(1)}, bf16[128,896]{1,0:T(8,128)(2,1)S(1)}, u32[]{:S(2)}, u32[]{:S(2)}) collective-permute-start(bf16[128,896]{1,0:T(8,128)(2,1)S(1)} %get-tuple-element.14), channel_id=1, source_target_pairs={{0,64},{64,128},{128,192},{192,256},{256,320},{320,384},{384,448},... | collective-permute-start | bytes 688136 | tf_op jit(solution)/shard_map/ppermute | solution.py:223
  7.4 19.6 %collective-permute-start.1 = (bf16[128,896]{1,0:T(8,128)(2,1)S(1)}, bf16[128,896]{1,0:T(8,128)(2,1)S(1)}, u32[]{:S(2)}, u32[]{:S(2)}) collective-permute-start(bf16[128,896]{1,0:T(8,128)(2,1)S(1)} %get-tuple-element.14), channel_id=1, source_target_pairs={{0,448},{64,0},{128,64},{192,128},{256,192},{320,256},{384,320},{4... | collective-permute-start | bytes 688136 | tf_op jit(solution)/shard_map/ppermute | solution.py:224
  25.1 9.9 %collective-permute-start.2 = (bf16[128,896]{1,0:T(8,128)(2,1)S(1)}, bf16[128,896]{1,0:T(8,128)(2,1)S(1)}, u32[]{:S(2)}, u32[]{:S(2)}) collective-permute-start(bf16[128,896]{1,0:T(8,128)(2,1)S(1)} %collective-permute-done), channel_id=1, source_target_pairs={{0,64},{64,128},{128,192},{192,256},{256,320},{320,384},{384,448},... | collective-permute-start | bytes 688136 | tf_op jit(solution)/shard_map/ppermute | solution.py:223
  27.0 9.9 %collective-permute-start.3 = (bf16[128,896]{1,0:T(8,128)(2,1)S(1)}, bf16[128,896]{1,0:T(8,128)(2,1)S(1)}, u32[]{:S(2)}, u32[]{:S(2)}) collective-permute-start(bf16[128,896]{1,0:T(8,128)(2,1)S(1)} %collective-permute-done.1), channel_id=1, source_target_pairs={{0,448},{64,0},{128,64},{192,128},{256,192},{320,256},{384,320},{4... | collective-permute-start | bytes 688136 | tf_op jit(solution)/shard_map/ppermute | solution.py:224
  35.0 9.1 %collective-permute-start.4 = (bf16[128,896]{1,0:T(8,128)(2,1)S(1)}, bf16[128,896]{1,0:T(8,128)(2,1)S(1)}, u32[]{:S(2)}, u32[]{:S(2)}) collective-permute-start(bf16[128,896]{1,0:T(8,128)(2,1)S(1)} %collective-permute-done.2), channel_id=1, source_target_pairs={{0,64},{64,128},{128,192},{192,256},{256,320},{320,384},{384,448},... | collective-permute-start | bytes 688136 | tf_op jit(solution)/shard_map/ppermute | solution.py:223
  36.9 9.1 %collective-permute-start.5 = (bf16[128,896]{1,0:T(8,128)(2,1)S(1)}, bf16[128,896]{1,0:T(8,128)(2,1)S(1)}, u32[]{:S(2)}, u32[]{:S(2)}) collective-permute-start(bf16[128,896]{1,0:T(8,128)(2,1)S(1)} %collective-permute-done.3), channel_id=1, source_target_pairs={{0,448},{64,0},{128,64},{192,128},{256,192},{320,256},{384,320},{4... | collective-permute-start | bytes 688136 | tf_op jit(solution)/shard_map/ppermute | solution.py:224
  44.1 7.9 %collective-permute-start.6 = (bf16[64,896]{1,0:T(8,128)(2,1)S(1)}, bf16[64,896]{1,0:T(8,128)(2,1)S(1)}, u32[]{:S(2)}, u32[]{:S(2)}) collective-permute-start(bf16[64,896]{1,0:T(8,128)(2,1)S(1)} %slice.52), channel_id=1, source_target_pairs={{0,64},{64,128},{128,192},{192,256},{256,320},{320,384},{384,448},... | collective-permute-start | bytes 344072 | tf_op jit(solution)/shard_map/ppermute | solution.py:226
  46.0 7.5 %collective-permute-start.7 = (bf16[64,896]{1,0:T(8,128)(2,1)S(1)}, bf16[64,896]{1,0:T(8,128)(2,1)S(1)}, u32[]{:S(2)}, u32[]{:S(2)}) collective-permute-start(bf16[64,896]{1,0:T(8,128)(2,1)S(1)} %slice.53), channel_id=1, source_target_pairs={{0,448},{64,0},{128,64},{192,128},{256,192},{320,256},{384,320},{4... | collective-permute-start | bytes 344072 | tf_op jit(solution)/shard_map/ppermute | solution.py:227
  53.6 36.8 %collective-permute-start.8 = (bf16[1024,896]{1,0:T(8,128)(2,1)S(1)}, bf16[1024,896]{1,0:T(8,128)(2,1)}, u32[]{:S(2)}, u32[]{:S(2)}) collective-permute-start(bf16[1024,896]{1,0:T(8,128)(2,1)S(1)} %bitcast.61), channel_id=1, source_target_pairs={{0,32},{32,0},{1,33},{33,1},{2,34},{34,2},{3,35},{35,3},{4,36},{36... | collective-permute-start | bytes 5505032 | tf_op jit(solution)/shard_map/ppermute | solution.py:245
  56.0 6.7 %copy-start.7 = (f32[256]{0:T(256)S(1)}, f32[256]{0:T(256)}, u32[]{:S(2)}) copy-start(f32[256]{0:T(256)} %param.20) | copy-start | bytes 3076
  60.8 27.8 %collective-permute-start.9 = (bf16[2,256,1024]{2,1,0:T(8,128)(2,1)}, bf16[2,256,1024]{2,1,0:T(8,128)(2,1)}, u32[]{:S(2)}, u32[]{:S(2)}) collective-permute-start(bf16[2,256,1024]{2,1,0:T(8,128)(2,1)} %get-tuple-element.10), channel_id=1, source_target_pairs={{0,512},{512,0},{1,513},{513,1},{2,514},{514,2},{3,515},{515,3},{4... | collective-permute-start | bytes 3145736 | tf_op jit(solution)/shard_map/ppermute | solution.py:211
  67.2 7.2 %copy-start.6 = (f32[4,256]{1,0:T(4,128)S(1)}, f32[4,256]{1,0:T(4,128)}, u32[]{:S(2)}) copy-start(f32[4,256]{1,0:T(4,128)} %param.15) | copy-start | bytes 12292
  67.2 9.3 %copy-start.9 = (f32[4]{0:T(128)S(1)}, f32[4]{0:T(128)}, u32[]{:S(2)}) copy-start(f32[4]{0:T(128)} %param.18) | copy-start | bytes 52
  67.2 9.3 %copy-start.10 = (f32[4]{0:T(128)S(1)}, f32[4]{0:T(128)}, u32[]{:S(2)}) copy-start(f32[4]{0:T(128)} %param.17) | copy-start | bytes 52
  67.2 42.6 %all-to-all-start = ((bf16[8,256,256]{2,1,0:T(8,128)(2,1)}), bf16[8,256,256]{2,1,0:T(8,128)(2,1)S(1)}, u32[]{:S(2)}, u32[]{:S(2)}) async-start(bf16[8,256,256]{2,1,0:T(8,128)(2,1)} %repack.1), calls=%async_computation | async-start | bytes 2097152 | tf_op jit(solution)/shard_map/all_to_all | solution.py:233
  90.3 9.5 %copy-start.3 = (bf16[2,256,1024]{2,1,0:T(8,128)(2,1)S(1)}, bf16[2,256,1024]{2,1,0:T(8,128)(2,1)}, u32[]{:S(2)}) copy-start(bf16[2,256,1024]{2,1,0:T(8,128)(2,1)} %get-tuple-element.9) | copy-start | bytes 3145732
  92.3 17.5 %collective-permute-start.10 = (bf16[256,512]{1,0:T(8,128)(2,1)S(1)}, bf16[256,512]{1,0:T(8,128)(2,1)S(1)}, u32[]{:S(2)}, u32[]{:S(2)}) collective-permute-start(bf16[256,512]{1,0:T(8,128)(2,1)S(1)} %fusion.8), channel_id=1, source_target_pairs={{0,512},{512,0},{1,513},{513,1},{2,514},{514,2},{3,515},{515,3},{4... | collective-permute-start | bytes 786440 | tf_op jit(solution)/shard_map/ppermute | solution.py:258
  96.2 10.0 %collective-permute-start.11 = (bf16[256,384]{1,0:T(8,128)(2,1)S(1)}, bf16[256,384]{1,0:T(8,128)(2,1)S(1)}, u32[]{:S(2)}, u32[]{:S(2)}) collective-permute-start(bf16[256,384]{1,0:T(8,128)(2,1)S(1)} %fusion.23), channel_id=1, source_target_pairs={{0,512},{512,0},{1,513},{513,1},{2,514},{514,2},{3,515},{515,3},{4... | collective-permute-start | bytes 589832 | tf_op jit(solution)/shard_map/ppermute | solution.py:256
  102.4 7.5 %copy-start.8 = (f32[4]{0:T(128)S(1)}, f32[4]{0:T(128)}, u32[]{:S(2)}) copy-start(f32[4]{0:T(128)} %param.19) | copy-start | bytes 52
  109.8 10.4 %copy-start.1 = (bf16[8,256,256]{2,1,0:T(8,128)(2,1)}, bf16[8,256,256]{2,1,0:T(8,128)(2,1)S(1)}, u32[]{:S(2)}) copy-start(bf16[8,256,256]{2,1,0:T(8,128)(2,1)S(1)} %all-to-all-done.own_ref) | copy-start | bytes 3145732
  113.5 34.4 %all-to-all-start.1 = ((bf16[8,256,256]{2,1,0:T(8,128)(2,1)}), bf16[8,256,256]{2,1,0:T(8,128)(2,1)S(1)}, u32[]{:S(2)}, u32[]{:S(2)}) async-start(bf16[8,256,256]{2,1,0:T(8,128)(2,1)} %shard_map.110), calls=%async_computation.1 | async-start | bytes 2097152 | tf_op jit(solution)/shard_map/all_to_all | solution.py:283
  120.2 4.7 %collective-permute-start.12 = (bf16[8,256,256]{2,1,0:T(8,128)(2,1)S(1)}, bf16[8,256,256]{2,1,0:T(8,128)(2,1)}, u32[]{:S(2)}, u32[]{:S(2)}) collective-permute-start(bf16[8,256,256]{2,1,0:T(8,128)(2,1)S(1)} %all-to-all-done.own_ref), channel_id=1, source_target_pairs={{0,32},{32,0},{1,33},{33,1},{2,34},{34,2},{3,35},{35,3},{4,36},{36... | collective-permute-start | bytes 3145736 | tf_op jit(solution)/shard_map/ppermute | solution.py:272
  147.9 1.0 copy-start.2
  (2 other events, 1.5 us)

commit v8 on v4

--- a/solution.py
+++ b/solution.py
@@ -93,7 +93,7 @@
         both = own_ref[:, columns] + away_ref[:, columns].astype(f32)
         conv = causal(both, taps_ref, columns)
         out = jnp.dot(mix_ref[h], conv, preferred_element_type=f32)
-        out = out + skip_ref[:, columns] * conv.astype(f32)
+        out = out + skip_ref[:, h : h + 1] * conv.astype(f32)
         out = out * pltpu.roll(silu(both), half, 1)
         if h % 2 == 0:
             kept = pltpu.roll(out, half, 1)
@@ -101,6 +101,75 @@
             pair = jnp.where(first, kept, out).astype(jnp.bfloat16)
             for copy in range(out_ref.shape[0]):
                 out_ref[copy, :, (h // 2) * wide : (h // 2 + 1) * wide] = pair
+
+
+def pack(zx_weight, dt_weight, bc_weight, group_id, group_cols, columns):
+    rows, heads, wide = zx_weight.shape
+    start = heads * wide
+
+    def kernel(group_ref, zx_ref, dt_ref, bc_ref, out_ref):
+        for h in range(heads):
+            out_ref[:, h * wide : (h + 1) * wide] = zx_ref[:, h, :]
+        out_ref[:, start : start + group_cols] = bc_ref[...]
+        last = start + group_cols
+        out_ref[:, last:] = jnp.zeros((rows, columns - last), out_ref.dtype)
+        out_ref[:, last : last + heads] = dt_ref[...]
+
+    return pl.pallas_call(
+        kernel,
+        grid_spec=pltpu.PrefetchScalarGridSpec(
+            num_scalar_prefetch=1,
+            grid=(1,),
+            in_specs=[
+                pl.BlockSpec((rows, heads, wide), lambda i, group: (0, 0, 0)),
+                pl.BlockSpec((rows, heads), lambda i, group: (0, 0)),
+                pl.BlockSpec((rows, group_cols), lambda i, group: (0, group[0])),
+            ],
+            out_specs=pl.BlockSpec((rows, columns), lambda i, group: (0, 0)),
+        ),
+        out_shape=jax.ShapeDtypeStruct((rows, columns), zx_weight.dtype),
+        name="pack",
+    )(group_id[None], zx_weight, dt_weight, bc_weight)
+
+
+def split_product(left, right, cut):
+    rows, depth = left.shape
+    columns = right.shape[1]
+    step = depth // 4
+
+    def kernel(left_ref, right_ref, first_ref, rest_ref, total_ref):
+        @pl.when(pl.program_id(0) == 0)
+        def _():
+            total_ref[...] = jnp.zeros_like(total_ref)
+
+        total_ref[...] += jnp.dot(left_ref[...], right_ref[...], preferred_element_type=jnp.float32)
+
+        @pl.when(pl.program_id(0) == pl.num_programs(0) - 1)
+        def _():
+            first_ref[...] = total_ref[:, :cut].astype(first_ref.dtype)
+            rest_ref[...] = total_ref[:, cut:].astype(rest_ref.dtype)
+
+    return pl.pallas_call(
+        kernel,
+        grid=(depth // step,),
+        in_specs=[
+            pl.BlockSpec((rows, step), lambda k: (0, k)),
+            pl.BlockSpec((step, columns), lambda k: (k, 0)),
+        ],
+        out_specs=[
+            pl.BlockSpec((rows, cut), lambda k: (0, 0)),
+            pl.BlockSpec((rows, columns - cut), lambda k: (0, 0)),
+        ],
+        out_shape=[
+            jax.ShapeDtypeStruct((rows, cut), jnp.bfloat16),
+            jax.ShapeDtypeStruct((rows, columns - cut), jnp.bfloat16),
+        ],
+        scratch_shapes=[pltpu.VMEM((rows, columns), jnp.float32)],
+        cost_estimate=pl.CostEstimate(
+            flops=2 * rows * depth * columns, bytes_accessed=2 * depth * columns, transcendentals=0
+        ),
+        name="split_product",
+    )(left, right)
 
 
 def on_chip(kernel, out_shape, flops, *args):
@@ -127,30 +196,31 @@
 ):
     f32, bf16 = jnp.float32, jnp.bfloat16
     tok_rows = tokens.shape[0]
-    rows, heads_here, two_p = zx_weight.shape
+    _, heads_here, two_p = zx_weight.shape
     head_size = two_p // 2
     channels = heads_here * head_size
     n_yh, n_x = lax.axis_size("yh"), lax.axis_size("x")
     group_id = lax.axis_index("yh")
     group_cols = bc_weight.shape[1] // n_yh
-    bc_part = lax.dynamic_slice_in_dim(bc_weight, group_id * group_cols, group_cols, 1)
     zx_cols = heads_here * two_p
     pad = -(zx_cols + group_cols + heads_here) % 128
-    mine = jnp.concatenate(
-        [
-            zx_weight.reshape(rows, zx_cols),
-            bc_part,
-            dt_weight,
-            jnp.zeros((rows, pad), bf16),
-        ],
-        axis=1,
-    )
+    columns = zx_cols + group_cols + heads_here + pad
+    mine = pack(zx_weight, dt_weight, bc_weight, group_id, group_cols, columns)
     k_half = lax.axis_index("yl")
     k_rows = tokens.shape[1] // 2
     kept = lax.dynamic_slice_in_dim(tokens, k_half * k_rows, k_rows, 1)
     given = lax.dynamic_slice_in_dim(tokens, (1 - k_half) * k_rows, k_rows, 1)
     given = lax.ppermute(given, "yl", SWAP)
 
+    def padded(values):
+        return jnp.pad(values, (0, 128 - heads_here))[None]
+
+    conv_group = lax.dynamic_slice_in_dim(conv_bc, group_id * group_cols, group_cols, 1)
+    taps = conv_x.shape[0]
+    x_taps = conv_x.reshape(taps, heads_here, head_size)
+    x_taps = jnp.concatenate([jnp.zeros_like(x_taps), x_taps], axis=2).reshape(taps, zx_cols)
+    skips, rate, bias = padded(d_skip), padded(a_log), padded(dt_bias)
+
     whole = lax.all_gather(mine, ("z", "core"), axis=0, tiled=True)
 
     width = out_weight.shape[1] // (n_yh * n_x)
@@ -158,22 +228,16 @@
     group_weight = lax.all_to_all(pieces, "x", 0, 0)
     group_weight = group_weight.reshape(n_x * channels, n_yh * width)
 
-    def padded(values):
-        return jnp.pad(values, (0, 128 - heads_here))[None]
-
-    conv_group = lax.dynamic_slice_in_dim(conv_bc, group_id * group_cols, group_cols, 1)
-    taps = conv_x.shape[0]
-    x_taps = conv_x.reshape(taps, heads_here, head_size)
-    x_taps = jnp.concatenate([jnp.zeros_like(x_taps), x_taps], axis=2).reshape(taps, zx_cols)
-    skips = jnp.repeat(d_skip, two_p)[None]
-    rate, bias = padded(a_log), padded(dt_bias)
+    ready = (whole, conv_group, x_taps, skips, rate, bias)
+    whole, conv_group, x_taps, skips, rate, bias = lax.optimization_barrier(ready)
 
     def product(left, columns):
         return jnp.dot(left, whole[:, columns], preferred_element_type=f32)
 
     small, large = slice(zx_cols, None), slice(0, zx_cols)
-    small_away = lax.ppermute(product(given, small).astype(bf16), "yl", SWAP)
-    large_away = lax.ppermute(product(given, large).astype(bf16), "yl", SWAP)
+    large_away, small_away = split_product(given, whole, zx_cols)
+    small_away = lax.ppermute(small_away, "yl", SWAP)
+    large_away = lax.ppermute(large_away, "yl", SWAP)
     small_own, large_own = product(kept, small), product(kept, large)
     mix = on_chip(
         mixing_kernel,

time: 154 us -> 157 us (1.019)
  the two profiles are of different devices: /device:TPU:16 before, /device:TPU:1 now
where the time goes in v8:
time: 157 us; the launch traced here: 156 us
  waiting for transfers between devices  65.2 us (42%)
  starting transfers between devices  22.3 us (14%)
  Pallas kernels  18.8 us (12%)
  blocking collectives  15.5 us (10%)
  between operations  13.5 us (9%)
  local copies, waits for them, and re-layouts  12.3 us (8%)
  matrix products  8.36 us (5%)
    all_gather x1, waiting for transfers between devices, layer(): whole = lax.all_gather(mine, ('z', 'core'), axis=0, tiled=True)  39.9 us
    all_to_all x1, waiting for transfers between devices, layer(): group = lax.all_to_all(spread, 'x', 0, 0)  25.2 us
    all_to_all x1, blocking collectives, layer(): got = lax.all_to_all(parts, 'yh', 0, 0)  15.5 us
    all_to_all x1, starting transfers between devices, layer(): group_weight = lax.all_to_all(pieces, 'x', 0, 0)  7.3 us
    all_to_all x1, starting transfers between devices, layer(): group = lax.all_to_all(spread, 'x', 0, 0)  6.37 us
    pallas_call x1, Pallas kernels, repack(): pl.pallas_call(kernel, grid=(rows // step,), in_specs=[pl.BlockSpec((step...  6.12 us
    dot_general x2, matrix products, product(): return jnp.dot(left, whole[:, columns], preferred_element_type=f32)  6.01 us
    pallas_call x2, Pallas kernels, on_chip(): pl.pallas_call(kernel, out_shape=out_shape, cost_estimate=pl.CostEstimate...  5.85 us
  transfers between devices with their start and end apart: 6, of which 2 were waited for; matrix products, arithmetic and copies ran while one was open for 9% of the time, Pallas kernels for 9%

profile of v8, /device:TPU:1, one launch (start us, length us, event | category | flops | bytes accessed | tf_op | source)
XLA Modules:
  0.0 156.2 jit_solution(122229372802568852)
XLA Ops:
  6.5 1.6 copy.17.dt_ref
  8.1 1.9 %pack.1 = bf16[128,896]{1,0:T(8,128)(2,1)} custom-call(s32[1]{0:T(128)} %bitcast.group_ref, bf16[128,4,128]{2,1,0:T(4,128)(2,1)} %zx_ref.1, bf16[128,4]{1,0:T(8,128)(2,1)} %copy.17.dt_ref, bf16[128,1024]{1,0:T(8,128)(2,1)} %bc_ref.1), custom_call_target="tpu_custom_call" | custom-call | tf_op jit(solution)/shard_map/pack/pallas_call | solution.py:118
  10.1 1.5 copy.18.gain_ref
  11.5 6.1 %repack.1 = bf16[8,256,512]{2,1,0:T(8,128)(2,1)} custom-call(f32[256,1]{1,0:T(8,128)} %copy.18.gain_ref, bf16[256,4096]{1,0:T(8,128)(2,1)} %weight_ref.1), custom_call_target="tpu_custom_call" | custom-call | flops 1048576 | bytes 4194304 | tf_op jit(solution)/shard_map/repack/pallas_call | solution.py:28
  17.6 7.3 %all-to-all-start = ((bf16[8,256,512]{2,1,0:T(8,128)(2,1)}), bf16[8,256,512]{2,1,0:T(8,128)(2,1)}, u32[]{:S(2)}, u32[]{:S(2)}) async-start(bf16[8,256,512]{2,1,0:T(8,128)(2,1)} %repack.1), calls=%async_computation | async-start | bytes 4194304 | tf_op jit(solution)/shard_map/all_to_all | solution.py:228
  25.1 3.3 %collective-permute-start = (bf16[256,2048]{1,0:T(8,128)(2,1)S(1)}, bf16[256,2048]{1,0:T(8,128)(2,1)}, u32[]{:S(2)}, u32[]{:S(2)}) collective-permute-start(bf16[256,2048]{1,0:T(8,128)(2,1)S(1)} %constant_dynamic-slice_fusion), channel_id=1, source_target_pairs={{0,512},{512,0},{1,513},{513,1},{2,514},{514,2},{3,515},{515,3},{4... | collective-permute-start | bytes 3145736 | tf_op jit(solution)/shard_map/ppermute | solution.py:213
  28.6 0.6 copy.37
  30.3 1.3 constant_dynamic-slice_fusion.1.taps_ref
  31.6 39.9 %all-gather.2.cloned.1.call-done.right_ref = bf16[2048,896]{1,0:T(8,128)(2,1)} async-done(((bf16[128,896]{1,0:T(8,128)(2,1)}), bf16[2048,896]{1,0:T(8,128)(2,1)}) %all-gather.2.cloned.1.call-update) | async-done | bytes 3670032 | tf_op jit(solution)/shard_map/all_gather | solution.py:224
  71.5 4.9 %split_product.1 = (bf16[256,512]{1,0:T(8,128)(2,1)}, bf16[256,384]{1,0:T(8,128)(2,1)}) custom-call(bf16[256,2048]{1,0:T(8,128)(2,1)} %collective-permute-done.left_ref, bf16[2048,896]{1,0:T(8,128)(2,1)} %all-gather.2.cloned.1.call-done.right_ref), custom_call_target="tpu_custom_call" | custom-call | flops 939524096 | bytes 3670016 | tf_op jit(solution)/shard_map/split_product/pallas_call | solution.py:152
  76.4 3.0 %collective-permute-start.1 = (bf16[256,384]{1,0:T(8,128)(2,1)}, bf16[256,384]{1,0:T(8,128)(2,1)S(1)}, u32[]{:S(2)}, u32[]{:S(2)}) collective-permute-start(bf16[256,384]{1,0:T(8,128)(2,1)} %get-tuple-element.16), channel_id=1, source_target_pairs={{0,512},{512,0},{1,513},{513,1},{2,514},{514,2},{3,515},{515,3},{4... | collective-permute-start | bytes 589832 | tf_op jit(solution)/shard_map/ppermute | solution.py:239
  79.4 2.3 %collective-permute-start.2 = (bf16[256,512]{1,0:T(8,128)(2,1)}, bf16[256,512]{1,0:T(8,128)(2,1)S(1)}, u32[]{:S(2)}, u32[]{:S(2)}) collective-permute-start(bf16[256,512]{1,0:T(8,128)(2,1)} %get-tuple-element.21), channel_id=1, source_target_pairs={{0,512},{512,0},{1,513},{513,1},{2,514},{514,2},{3,515},{515,3},{4... | collective-permute-start | bytes 786440 | tf_op jit(solution)/shard_map/ppermute | solution.py:240
  81.6 3.1 %fusion.2.own_ref = f32[256,512]{1,0:T(8,128)} fusion(bf16[2048,896]{1,0:T(8,128)(2,1)} %all-gather.2.cloned.1.call-done.right_ref, bf16[256,4096]{1,0:T(8,128)(2,1)S(1)} %copy-done, s32[]{:T(128)S(6)} %select_n.9), kind=kOutput, calls=%fused_computation.3 | convolution fusion | flops 536870912 | bytes 3670020 | tf_op jit(solution)/shard_map/dot_general | solution.py:235
  84.8 2.9 %fusion.4.own_ref = f32[256,384]{1,0:T(8,128)} fusion(bf16[2048,896]{1,0:T(8,128)(2,1)} %all-gather.2.cloned.1.call-done.right_ref, bf16[256,4096]{1,0:T(8,128)(2,1)S(1)} %copy-done, s32[]{:T(128)S(6)} %select_n.9), kind=kOutput, calls=%fused_computation.5 | convolution fusion | flops 402653184 | bytes 3014660 | tf_op jit(solution)/shard_map/dot_general | solution.py:235
  87.7 0.7 copy-done.2
  88.3 2.9 %shard_map.109.mix_ref = bf16[4,256,256]{2,1,0:T(8,128)(2,1)} custom-call(f32[256,384]{1,0:T(8,128)} %fusion.4.own_ref, bf16[256,384]{1,0:T(8,128)(2,1)} %copy-done.2, f32[4,256]{1,0:T(4,128)} %constant_dynamic-slice_fusion.1.taps_ref, f32[1,128]{1,0:T(1,128)} %get-tuple-element.18.rate_ref, f32[1,128]{1,0:T(1,128)} %get-tuple-element.19.bias_ref), custom_call_target="tpu_custom_call" | custom-call | flops 2621440 | bytes 1119232 | tf_op jit(solution)/shard_map/pallas_call | solution.py:177
  91.3 0.7 copy-done.1
  92.0 2.9 %shard_map.110 = bf16[8,256,256]{2,1,0:T(8,128)(2,1)} custom-call(f32[256,512]{1,0:T(8,128)} %fusion.2.own_ref, bf16[256,512]{1,0:T(8,128)(2,1)} %copy-done.1, f32[4,512]{1,0:T(4,128)} %bitcast.28, f32[1,128]{1,0:T(1,128)} %pad_bitcast_fusion.3.skip_ref, bf16[4,256,256]{2,1,0:T(8,128)(2,1)} %shard_map.109.mix_ref), custom_call_target="tpu_custom_call" | custom-call | flops 67108864 | bytes 2368000 | tf_op jit(solution)/shard_map/pallas_call | solution.py:177
  94.9 6.4 %all-to-all-start.1 = ((bf16[8,256,256]{2,1,0:T(8,128)(2,1)}), bf16[8,256,256]{2,1,0:T(8,128)(2,1)S(1)}, u32[]{:S(2)}, u32[]{:S(2)}) async-start(bf16[8,256,256]{2,1,0:T(8,128)(2,1)} %shard_map.110), calls=%async_computation.1 | async-start | bytes 2097152 | tf_op jit(solution)/shard_map/all_to_all | solution.py:263
  101.3 4.0 %reshape.23 = bf16[8,256,4,128]{3,2,1,0:T(4,128)(2,1)} reshape(bf16[2048,512]{1,0:T(8,128)(2,1)} %bitcast.5) | data formatting | bytes 4194304 | tf_op jit(solution)/shard_map/reshape | solution.py:269
  105.2 25.2 %all-to-all-done.1 = bf16[8,256,256]{2,1,0:T(8,128)(2,1)S(1)} async-done(((bf16[8,256,256]{2,1,0:T(8,128)(2,1)}), bf16[8,256,256]{2,1,0:T(8,128)(2,1)S(1)}, u32[]{:S(2)}, u32[]{:S(2)}) %all-to-all-start.1) | async-done | bytes 1048608 | tf_op jit(solution)/shard_map/all_to_all | solution.py:263
  130.8 2.4 %fusion.15 = bf16[4,256,128]{1,2,0:T(8,128)(2,1)S(1)} fusion(bf16[8,256,4,128]{3,2,1,0:T(4,128)(2,1)} %reshape.23, bf16[8,256,256]{2,1,0:T(8,128)(2,1)S(1)} %all-to-all-done.1, f32[256]{0:T(256)S(1)} %add_rsqrt_fusion), kind=kOutput, calls=%fused_computation.10 | convolution fusion | flops 537133056 | bytes 3408896 | tf_op jit(solution)/shard_map/xtc,xcyw->ytw/dot_general | solution.py:266
  133.1 15.5 %all_to_all.15 = bf16[4,256,128]{1,2,0:T(8,128)(2,1)S(1)} all-to-all(bf16[4,256,128]{1,2,0:T(8,128)(2,1)S(1)} %fusion.15), channel_id=1, replica_groups=mesh['yl'=2,'z'=8,'core'=2,'yh'=4,'x'=8] {'yh'}, dimensions={0} | all-to-all | bytes 524288 | tf_op jit(solution)/shard_map/all_to_all | solution.py:273
  148.7 0.7 copy.21
  (26 shorter events, 1.7 us)
Async XLA Ops:
  6.5 18.5 %copy-start = (bf16[256,4096]{1,0:T(8,128)(2,1)S(1)}, bf16[256,4096]{1,0:T(8,128)(2,1)}, u32[]{:S(2)}) copy-start(bf16[256,4096]{1,0:T(8,128)(2,1)} %param.11) | copy-start | bytes 6291460
  6.5 64.9 %all-gather.2.cloned.1.call-start = ((), (), s32[]{:S(2)}) async-start(), calls=%async_computation.3 | async-start | bytes 3899392 | tf_op jit(solution)/shard_map/all_gather | solution.py:224
  17.6 73.6 %all-to-all-start = ((bf16[8,256,512]{2,1,0:T(8,128)(2,1)}), bf16[8,256,512]{2,1,0:T(8,128)(2,1)}, u32[]{:S(2)}, u32[]{:S(2)}) async-start(bf16[8,256,512]{2,1,0:T(8,128)(2,1)} %repack.1), calls=%async_computation | async-start | bytes 4194304 | tf_op jit(solution)/shard_map/all_to_all | solution.py:228
  24.9 3.5 %copy-start.3 = (f32[4,256]{1,0:T(4,128)S(1)}, f32[4,256]{1,0:T(4,128)}, u32[]{:S(2)}) copy-start(f32[4,256]{1,0:T(4,128)} %param.15) | copy-start | bytes 12292
  25.0 4.2 %copy-start.6 = (f32[4]{0:T(128)S(1)}, f32[4]{0:T(128)}, u32[]{:S(2)}) copy-start(f32[4]{0:T(128)} %param.19) | copy-start | bytes 52
  25.0 4.7 %copy-start.4 = (f32[4]{0:T(128)S(1)}, f32[4]{0:T(128)}, u32[]{:S(2)}) copy-start(f32[4]{0:T(128)} %param.18) | copy-start | bytes 52
  25.0 4.7 %copy-start.5 = (f32[4]{0:T(128)S(1)}, f32[4]{0:T(128)}, u32[]{:S(2)}) copy-start(f32[4]{0:T(128)} %param.17) | copy-start | bytes 52
  25.1 46.4 %collective-permute-start = (bf16[256,2048]{1,0:T(8,128)(2,1)S(1)}, bf16[256,2048]{1,0:T(8,128)(2,1)}, u32[]{:S(2)}, u32[]{:S(2)}) collective-permute-start(bf16[256,2048]{1,0:T(8,128)(2,1)S(1)} %constant_dynamic-slice_fusion), channel_id=1, source_target_pairs={{0,512},{512,0},{1,513},{513,1},{2,514},{514,2},{3,515},{515,3},{4... | collective-permute-start | bytes 3145736 | tf_op jit(solution)/shard_map/ppermute | solution.py:213
  76.4 11.3 %collective-permute-start.1 = (bf16[256,384]{1,0:T(8,128)(2,1)}, bf16[256,384]{1,0:T(8,128)(2,1)S(1)}, u32[]{:S(2)}, u32[]{:S(2)}) collective-permute-start(bf16[256,384]{1,0:T(8,128)(2,1)} %get-tuple-element.16), channel_id=1, source_target_pairs={{0,512},{512,0},{1,513},{513,1},{2,514},{514,2},{3,515},{515,3},{4... | collective-permute-start | bytes 589832 | tf_op jit(solution)/shard_map/ppermute | solution.py:239
  79.4 11.9 %collective-permute-start.2 = (bf16[256,512]{1,0:T(8,128)(2,1)}, bf16[256,512]{1,0:T(8,128)(2,1)S(1)}, u32[]{:S(2)}, u32[]{:S(2)}) collective-permute-start(bf16[256,512]{1,0:T(8,128)(2,1)} %get-tuple-element.21), channel_id=1, source_target_pairs={{0,512},{512,0},{1,513},{513,1},{2,514},{514,2},{3,515},{515,3},{4... | collective-permute-start | bytes 786440 | tf_op jit(solution)/shard_map/ppermute | solution.py:240
  87.7 0.7 copy-start.2
  91.3 0.7 copy-start.1
  94.9 35.6 %all-to-all-start.1 = ((bf16[8,256,256]{2,1,0:T(8,128)(2,1)}), bf16[8,256,256]{2,1,0:T(8,128)(2,1)S(1)}, u32[]{:S(2)}, u32[]{:S(2)}) async-start(bf16[8,256,256]{2,1,0:T(8,128)(2,1)} %shard_map.110), calls=%async_computation.1 | async-start | bytes 2097152 | tf_op jit(solution)/shard_map/all_to_all | solution.py:263
Sparse Core Ops, SparseCore 0:
  10.2 61.2 all-gather.1

commit v9 on v4

--- a/solution.py
+++ b/solution.py
@@ -74,10 +74,14 @@
         preferred_element_type=f32,
     )
     cum_t, steps_t = cum.T, steps.T
+    half = length // 2
     for h in range(heads):
-        seg = cum[:, h : h + 1] - cum_t[h : h + 1, :]
-        decay = jnp.exp(jnp.where(lower, seg, -1e30))
-        out_ref[h] = (inner * decay * steps_t[h : h + 1, :]).astype(jnp.bfloat16)
+        for rows, seen in ((slice(0, half), half), (slice(half, length), length)):
+            seg = cum[rows, h : h + 1] - cum_t[h : h + 1, :seen]
+            decay = jnp.exp(jnp.where(lower[rows, :seen], seg, -1e30))
+            mixed = inner[rows, :seen] * decay * steps_t[h : h + 1, :seen]
+            out_ref[h, rows, :seen] = mixed.astype(jnp.bfloat16)
+        out_ref[h, :half, half:] = jnp.zeros((half, length - half), jnp.bfloat16)
 
 
 def gated_kernel(own_ref, away_ref, taps_ref, skip_ref, mix_ref, out_ref):
@@ -93,7 +97,7 @@
         both = own_ref[:, columns] + away_ref[:, columns].astype(f32)
         conv = causal(both, taps_ref, columns)
         out = jnp.dot(mix_ref[h], conv, preferred_element_type=f32)
-        out = out + skip_ref[:, columns] * conv.astype(f32)
+        out = out + skip_ref[:, h : h + 1] * conv.astype(f32)
         out = out * pltpu.roll(silu(both), half, 1)
         if h % 2 == 0:
             kept = pltpu.roll(out, half, 1)
@@ -151,6 +155,15 @@
     given = lax.dynamic_slice_in_dim(tokens, (1 - k_half) * k_rows, k_rows, 1)
     given = lax.ppermute(given, "yl", SWAP)
 
+    def padded(values):
+        return jnp.pad(values, (0, 128 - heads_here))[None]
+
+    conv_group = lax.dynamic_slice_in_dim(conv_bc, group_id * group_cols, group_cols, 1)
+    taps = conv_x.shape[0]
+    x_taps = conv_x.reshape(taps, heads_here, head_size)
+    x_taps = jnp.concatenate([jnp.zeros_like(x_taps), x_taps], axis=2).reshape(taps, zx_cols)
+    skips, rate, bias = padded(d_skip), padded(a_log), padded(dt_bias)
+
     whole = lax.all_gather(mine, ("z", "core"), axis=0, tiled=True)
 
     width = out_weight.shape[1] // (n_yh * n_x)
@@ -158,15 +171,8 @@
     group_weight = lax.all_to_all(pieces, "x", 0, 0)
     group_weight = group_weight.reshape(n_x * channels, n_yh * width)
 
-    def padded(values):
-        return jnp.pad(values, (0, 128 - heads_here))[None]
-
-    conv_group = lax.dynamic_slice_in_dim(conv_bc, group_id * group_cols, group_cols, 1)
-    taps = conv_x.shape[0]
-    x_taps = conv_x.reshape(taps, heads_here, head_size)
-    x_taps = jnp.concatenate([jnp.zeros_like(x_taps), x_taps], axis=2).reshape(taps, zx_cols)
-    skips = jnp.repeat(d_skip, two_p)[None]
-    rate, bias = padded(a_log), padded(dt_bias)
+    ready = (whole, conv_group, x_taps, skips, rate, bias)
+    whole, conv_group, x_taps, skips, rate, bias = lax.optimization_barrier(ready)
 
     def product(left, columns):
         return jnp.dot(left, whole[:, columns], preferred_element_type=f32)

time: 154 us -> 154 us (level)
    ppermute x1, waiting for transfers between devices: 11.5 us -> 0.01 us  [layer(): given = lax.ppermute(given, 'yl', SWAP)]
    all_gather x1, waiting for transfers between devices: 18.8 us -> 29.7 us  [layer(): whole = lax.all_gather(mine, ('z', 'core'), axis=0, tiled=True)]
  transfers between devices with their start and end apart: 6 -> 6, of which waited for: 4 -> 3; matrix products, arithmetic and copies ran while one was open for 10% -> 11% of each run, Pallas kernels for 6% -> 6%
where the time goes in v9:
time: 154 us
  waiting for transfers between devices  54.3 us (35%)
  starting transfers between devices  31.7 us (21%)
  blocking collectives  17.3 us (11%)
  local copies, waits for them, and re-layouts  13.7 us (9%)
  between operations  13.5 us (9%)
  Pallas kernels  11.9 us (8%)
  matrix products  9.91 us (6%)
    all_gather x1, waiting for transfers between devices, layer(): whole = lax.all_gather(mine, ('z', 'core'), axis=0, tiled=True)  29.7 us
    all_to_all x1, waiting for transfers between devices, layer(): group = lax.all_to_all(spread, 'x', 0, 0)  24.5 us
    all_to_all x1, blocking collectives, layer(): got = lax.all_to_all(parts, 'yh', 0, 0)  17.3 us
    ppermute x1, starting transfers between devices, layer(): given = lax.ppermute(given, 'yl', SWAP)  12.5 us
    dot_general x4, matrix products, product(): return jnp.dot(left, whole[:, columns], preferred_element_type=f32)  7.56 us
    all_to_all x1, starting transfers between devices, layer(): group_weight = lax.all_to_all(pieces, 'x', 0, 0)  6.76 us
    all_to_all x1, starting transfers between devices, layer(): group = lax.all_to_all(spread, 'x', 0, 0)  6.65 us
    pallas_call x1, Pallas kernels, repack(): pl.pallas_call(kernel, grid=(rows // step,), in_specs=[pl.BlockSpec((step...  6.12 us
  transfers between devices with their start and end apart: 6, of which 3 were waited for; matrix products, arithmetic and copies ran while one was open for 11% of the time, Pallas kernels for 6%

profile of v9, /device:TPU:16, one launch (start us, length us, event | category | flops | bytes accessed | tf_op | source)
XLA Modules:
  0.0 153.6 jit_solution(11562972218210781826)
XLA Ops:
  6.5 1.0 copy.17
  7.5 0.9 copy.39
  8.5 0.8 constant_dynamic-slice_fusion.2
  9.4 0.7 maximum_maximum_fusion
  10.1 1.5 copy.18.gain_ref
  11.6 6.1 %repack.1 = bf16[8,256,512]{2,1,0:T(8,128)(2,1)} custom-call(f32[256,1]{1,0:T(8,128)} %copy.18.gain_ref, bf16[256,4096]{1,0:T(8,128)(2,1)} %weight_ref.1), custom_call_target="tpu_custom_call" | custom-call | flops 1048576 | bytes 4194304 | tf_op jit(solution)/shard_map/repack/pallas_call | solution.py:28
  17.7 6.8 %all-to-all-start = ((bf16[8,256,512]{2,1,0:T(8,128)(2,1)}), bf16[8,256,512]{2,1,0:T(8,128)(2,1)}, u32[]{:S(2)}, u32[]{:S(2)}) async-start(bf16[8,256,512]{2,1,0:T(8,128)(2,1)} %repack.1), calls=%async_computation | async-start | bytes 4194304 | tf_op jit(solution)/shard_map/all_to_all | solution.py:171
  24.6 12.5 %collective-permute-start = (bf16[256,2048]{1,0:T(8,128)(2,1)S(1)}, bf16[256,2048]{1,0:T(8,128)(2,1)}, u32[]{:S(2)}, u32[]{:S(2)}) collective-permute-start(bf16[256,2048]{1,0:T(8,128)(2,1)S(1)} %constant_dynamic-slice_fusion), channel_id=1, source_target_pairs={{0,512},{512,0},{1,513},{513,1},{2,514},{514,2},{3,515},{515,3},{4... | collective-permute-start | bytes 3145736 | tf_op jit(solution)/shard_map/ppermute | solution.py:156
  39.1 1.3 constant_dynamic-slice_fusion.1.taps_ref
  40.3 29.7 %all-gather.2.cloned.1.call-done = bf16[2048,896]{1,0:T(8,128)(2,1)} async-done(((bf16[128,896]{1,0:T(8,128)(2,1)}), bf16[2048,896]{1,0:T(8,128)(2,1)}) %all-gather.2.cloned.1.call-update) | async-done | bytes 3670032 | tf_op jit(solution)/shard_map/all_gather | solution.py:167
  70.0 2.6 %fusion.22 = bf16[256,384]{1,0:T(8,128)(2,1)S(1)} fusion(bf16[256,2048]{1,0:T(8,128)(2,1)} %collective-permute-done, bf16[2048,896]{1,0:T(8,128)(2,1)} %all-gather.2.cloned.1.call-done), kind=kOutput, calls=%fused_computation.15 | convolution fusion | flops 402751488 | bytes 2818048 | tf_op jit(solution)/shard_map/dot_general | solution.py:178
  72.6 2.5 %collective-permute-start.1 = (bf16[256,384]{1,0:T(8,128)(2,1)S(1)}, bf16[256,384]{1,0:T(8,128)(2,1)S(1)}, u32[]{:S(2)}, u32[]{:S(2)}) collective-permute-start(bf16[256,384]{1,0:T(8,128)(2,1)S(1)} %fusion.22), channel_id=1, source_target_pairs={{0,512},{512,0},{1,513},{513,1},{2,514},{514,2},{3,515},{515,3},{4... | collective-permute-start | bytes 589832 | tf_op jit(solution)/shard_map/ppermute | solution.py:181
  75.2 2.0 %fusion.19 = bf16[256,512]{1,0:T(8,128)(2,1)S(1)} fusion(bf16[256,2048]{1,0:T(8,128)(2,1)} %collective-permute-done, bf16[2048,896]{1,0:T(8,128)(2,1)S(1)} %copy-done.6), kind=kOutput, calls=%fused_computation.14 | convolution fusion | flops 537001984 | bytes 3407872 | tf_op jit(solution)/shard_map/dot_general | solution.py:178
  77.2 3.3 %collective-permute-start.2 = (bf16[256,512]{1,0:T(8,128)(2,1)S(1)}, bf16[256,512]{1,0:T(8,128)(2,1)S(1)}, u32[]{:S(2)}, u32[]{:S(2)}) collective-permute-start(bf16[256,512]{1,0:T(8,128)(2,1)S(1)} %fusion.19), channel_id=1, source_target_pairs={{0,512},{512,0},{1,513},{513,1},{2,514},{514,2},{3,515},{515,3},{4... | collective-permute-start | bytes 786440 | tf_op jit(solution)/shard_map/ppermute | solution.py:182
  80.5 1.6 %fusion.4.own_ref = f32[256,512]{1,0:T(8,128)} fusion(bf16[2048,896]{1,0:T(8,128)(2,1)S(1)} %copy-done.6, bf16[256,4096]{1,0:T(8,128)(2,1)S(1)} %copy-done, s32[]{:T(128)S(6)} %select_n.10), kind=kOutput, calls=%fused_computation.5 | convolution fusion | flops 536870912 | bytes 3670020 | tf_op jit(solution)/shard_map/dot_general | solution.py:178
  82.0 1.5 fusion.8.own_ref
  84.2 2.9 %shard_map.109.mix_ref = bf16[4,256,256]{2,1,0:T(8,128)(2,1)} custom-call(f32[256,384]{1,0:T(8,128)} %fusion.8.own_ref, bf16[256,384]{1,0:T(8,128)(2,1)} %copy-done.2, f32[4,256]{1,0:T(4,128)} %constant_dynamic-slice_fusion.1.taps_ref, f32[1,128]{1,0:T(1,128)} %get-tuple-element.15.rate_ref, f32[1,128]{1,0:T(1,128)} %get-tuple-element.16.bias_ref), custom_call_target="tpu_custom_call" | custom-call | flops 2621440 | bytes 1119232 | tf_op jit(solution)/shard_map/pallas_call | solution.py:112
  87.9 2.9 %shard_map.110 = bf16[8,256,256]{2,1,0:T(8,128)(2,1)} custom-call(f32[256,512]{1,0:T(8,128)} %fusion.4.own_ref, bf16[256,512]{1,0:T(8,128)(2,1)} %copy-done.1, f32[4,512]{1,0:T(4,128)} %bitcast.35, f32[1,128]{1,0:T(1,128)} %pad_bitcast_fusion.3.skip_ref, bf16[4,256,256]{2,1,0:T(8,128)(2,1)} %shard_map.109.mix_ref), custom_call_target="tpu_custom_call" | custom-call | flops 67108864 | bytes 2368000 | tf_op jit(solution)/shard_map/pallas_call | solution.py:112
  90.9 6.6 %all-to-all-start.1 = ((bf16[8,256,256]{2,1,0:T(8,128)(2,1)}), bf16[8,256,256]{2,1,0:T(8,128)(2,1)S(1)}, u32[]{:S(2)}, u32[]{:S(2)}) async-start(bf16[8,256,256]{2,1,0:T(8,128)(2,1)} %shard_map.110), calls=%async_computation.1 | async-start | bytes 2097152 | tf_op jit(solution)/shard_map/all_to_all | solution.py:205
  97.5 4.0 %reshape.27 = bf16[8,256,4,128]{3,2,1,0:T(4,128)(2,1)} reshape(bf16[2048,512]{1,0:T(8,128)(2,1)} %bitcast.4) | data formatting | bytes 4194304 | tf_op jit(solution)/shard_map/reshape | solution.py:211
  101.5 24.5 %all-to-all-done.1 = bf16[8,256,256]{2,1,0:T(8,128)(2,1)S(1)} async-done(((bf16[8,256,256]{2,1,0:T(8,128)(2,1)}), bf16[8,256,256]{2,1,0:T(8,128)(2,1)S(1)}, u32[]{:S(2)}, u32[]{:S(2)}) %all-to-all-start.1) | async-done | bytes 1048608 | tf_op jit(solution)/shard_map/all_to_all | solution.py:205
  126.2 2.4 %fusion.25 = bf16[4,256,128]{1,2,0:T(8,128)(2,1)S(1)} fusion(bf16[8,256,4,128]{3,2,1,0:T(4,128)(2,1)} %reshape.27, bf16[8,256,256]{2,1,0:T(8,128)(2,1)S(1)} %all-to-all-done.1, f32[256]{0:T(256)S(1)} %add_rsqrt_fusion), kind=kOutput, calls=%fused_computation.16 | convolution fusion | flops 537133056 | bytes 3408896 | tf_op jit(solution)/shard_map/xtc,xcyw->ytw/dot_general | solution.py:208
  128.6 17.3 %all_to_all.15 = bf16[4,256,128]{1,2,0:T(8,128)(2,1)S(1)} all-to-all(bf16[4,256,128]{1,2,0:T(8,128)(2,1)S(1)} %fusion.25), channel_id=1, replica_groups=mesh['yl'=2,'z'=8,'core'=2,'yh'=4,'x'=8] {'yh'}, dimensions={0} | all-to-all | bytes 524288 | tf_op jit(solution)/shard_map/all_to_all | solution.py:215
  146.0 0.7 copy.21
  (33 shorter events, 4.0 us)
Async XLA Ops:
  6.5 18.0 %copy-start = (bf16[256,4096]{1,0:T(8,128)(2,1)S(1)}, bf16[256,4096]{1,0:T(8,128)(2,1)}, u32[]{:S(2)}) copy-start(bf16[256,4096]{1,0:T(8,128)(2,1)} %param.11) | copy-start | bytes 6291460
  6.5 63.5 %all-gather.2.cloned.1.call-start = ((), (), s32[]{:S(2)}) async-start(), calls=%async_computation.3 | async-start | bytes 3899392 | tf_op jit(solution)/shard_map/all_gather | solution.py:167
  17.7 69.4 %all-to-all-start = ((bf16[8,256,512]{2,1,0:T(8,128)(2,1)}), bf16[8,256,512]{2,1,0:T(8,128)(2,1)}, u32[]{:S(2)}, u32[]{:S(2)}) async-start(bf16[8,256,512]{2,1,0:T(8,128)(2,1)} %repack.1), calls=%async_computation | async-start | bytes 4194304 | tf_op jit(solution)/shard_map/all_to_all | solution.py:171
  24.5 12.6 %copy-start.3 = (f32[4,256]{1,0:T(4,128)S(1)}, f32[4,256]{1,0:T(4,128)}, u32[]{:S(2)}) copy-start(f32[4,256]{1,0:T(4,128)} %param.15) | copy-start | bytes 12292
  24.5 13.4 %copy-start.7 = (f32[4]{0:T(128)S(1)}, f32[4]{0:T(128)}, u32[]{:S(2)}) copy-start(f32[4]{0:T(128)} %param.19) | copy-start | bytes 52
  24.5 14.0 %copy-start.4 = (f32[4]{0:T(128)S(1)}, f32[4]{0:T(128)}, u32[]{:S(2)}) copy-start(f32[4]{0:T(128)} %param.18) | copy-start | bytes 52
  24.5 14.0 %copy-start.5 = (f32[4]{0:T(128)S(1)}, f32[4]{0:T(128)}, u32[]{:S(2)}) copy-start(f32[4]{0:T(128)} %param.17) | copy-start | bytes 52
  24.6 45.4 %collective-permute-start = (bf16[256,2048]{1,0:T(8,128)(2,1)S(1)}, bf16[256,2048]{1,0:T(8,128)(2,1)}, u32[]{:S(2)}, u32[]{:S(2)}) collective-permute-start(bf16[256,2048]{1,0:T(8,128)(2,1)S(1)} %constant_dynamic-slice_fusion), channel_id=1, source_target_pairs={{0,512},{512,0},{1,513},{513,1},{2,514},{514,2},{3,515},{515,3},{4... | collective-permute-start | bytes 3145736 | tf_op jit(solution)/shard_map/ppermute | solution.py:156
  70.0 5.1 %copy-start.6 = (bf16[2048,896]{1,0:T(8,128)(2,1)S(1)}, bf16[2048,896]{1,0:T(8,128)(2,1)}, u32[]{:S(2)}) copy-start(bf16[2048,896]{1,0:T(8,128)(2,1)} %all-gather.2.cloned.1.call-done) | copy-start | bytes 11010052
  72.6 10.9 %collective-permute-start.1 = (bf16[256,384]{1,0:T(8,128)(2,1)S(1)}, bf16[256,384]{1,0:T(8,128)(2,1)S(1)}, u32[]{:S(2)}, u32[]{:S(2)}) collective-permute-start(bf16[256,384]{1,0:T(8,128)(2,1)S(1)} %fusion.22), channel_id=1, source_target_pairs={{0,512},{512,0},{1,513},{513,1},{2,514},{514,2},{3,515},{515,3},{4... | collective-permute-start | bytes 589832 | tf_op jit(solution)/shard_map/ppermute | solution.py:181
  77.2 10.1 %collective-permute-start.2 = (bf16[256,512]{1,0:T(8,128)(2,1)S(1)}, bf16[256,512]{1,0:T(8,128)(2,1)S(1)}, u32[]{:S(2)}, u32[]{:S(2)}) collective-permute-start(bf16[256,512]{1,0:T(8,128)(2,1)S(1)} %fusion.19), channel_id=1, source_target_pairs={{0,512},{512,0},{1,513},{513,1},{2,514},{514,2},{3,515},{515,3},{4... | collective-permute-start | bytes 786440 | tf_op jit(solution)/shard_map/ppermute | solution.py:182
  83.5 0.7 copy-start.2
  87.2 0.7 copy-start.1
  90.9 35.1 %all-to-all-start.1 = ((bf16[8,256,256]{2,1,0:T(8,128)(2,1)}), bf16[8,256,256]{2,1,0:T(8,128)(2,1)S(1)}, u32[]{:S(2)}, u32[]{:S(2)}) async-start(bf16[8,256,256]{2,1,0:T(8,128)(2,1)} %shard_map.110), calls=%async_computation.1 | async-start | bytes 2097152 | tf_op jit(solution)/shard_map/all_to_all | solution.py:205
Sparse Core Ops, SparseCore 0:
  10.3 59.7 all-gather.1
